TPU v7x, 32 devices: a whole 2x2x4 slice. The times are simulated.
32 devices in a mesh: seq: 8 (over z, x), chan: 4 (over y, core).
Axes of the slice: x: 2, y: 2, z: 4, core: 2. Of those that a mesh axis runs over, the one named last changes fastest.
Arguments:
- inputs: bfloat16 [2048, 2048], P('seq', 'chan'), may hold values from -6 to 6
- weights: bfloat16 [4, 2048, 2048], P(None, None, 'chan'), may hold values from -0.125 to 0.125
- filters: float32 [4, 2048], P(None, 'seq'), may hold values from -0.125 to 0.125
Outputs:
- output: bfloat16 [2048, 2048], P('seq', 'chan')
All inputs are finite; a program needn't handle non-finite values.
Results may differ from a plain program's by a relative error of at most 0.0049.
Values may be sent and summed in bfloat16 or wider, within the bound.
No kernel may reach another device: no remote copies, remote signals or barrier semaphores. Data moves between devices by JAX's collectives and lax.ppermute only.
A program may use at most 64 MiB of HBM per device.

v0:
```python
import functools
import math

import jax
import jax.numpy as jnp
from jax import lax
from jax.experimental import pallas as pl
from jax.experimental.pallas import tpu as pltpu
from jax.sharding import PartitionSpec as P

f32 = jnp.float32
bf16 = jnp.bfloat16
LANES = 128


def swap(value, axis, mask):
    return lax.ppermute(value, axis, [(i, i ^ mask) for i in range(lax.axis_size(axis))])


def params(mib, axes=1):
    return pltpu.CompilerParams(
        dimension_semantics=("arbitrary",) * axes, vmem_limit_bytes=mib * 1024 * 1024
    )


def project_body(meta, *refs, steps, group, has_sum, last):
    x_refs, w_ref = refs[:steps], refs[steps]
    refs = refs[steps + 1 :]
    if has_sum:
        sum_ref, refs = refs[0], refs[1:]
    count = group if last else 1
    out_refs, (held, total) = refs[:count], refs[count:]
    step, k = pl.program_id(0), pl.program_id(1)
    filters = pl.num_programs(1)
    width = w_ref.shape[2]
    sub = width // group
    place = meta[1]

    @pl.when((step == 0) & (k == 0))
    def _():
        for at, x_ref in enumerate(x_refs):
            held[at] = x_ref[...]

    columns = [
        w_ref[0, :, pl.ds(pl.multiple_of((place ^ m) * sub, sub), sub)] for m in range(group)
    ]
    part = jnp.dot(held[step], jnp.concatenate(columns, axis=1), preferred_element_type=f32)
    if has_sum:
        before = jnp.where(step == 0, sum_ref[0], total[k])
        part = part + before
    else:
        part = jnp.where(step == 0, part, part + total[k])
    total[k] = part

    @pl.when((step == steps - 1) & (k == filters - 1))
    def _():
        for j in range(total.shape[0]):
            if last:
                for m in range(group):
                    out_refs[m][:, j * sub : (j + 1) * sub] = total[
                        j, :, m * sub : (m + 1) * sub
                    ].astype(bf16)
            else:
                out_refs[0][j] = total[j]


def project(meta, order, blocks, weights, before, group, last):
    steps = len(blocks)
    tokens, depth = blocks[0].shape
    count, _, width = weights.shape
    whole = pl.BlockSpec((tokens, depth), lambda i, k, meta: (0, 0))
    first, mask = order[0], order[0] ^ order[-1]

    def w_map(i, k, meta):
        return (k, meta[0] ^ (first ^ (i * mask)), 0)

    in_specs = [whole] * steps + [pl.BlockSpec((1, depth, width), w_map)]
    args = [*blocks, weights]
    if before is not None:
        in_specs.append(
            pl.BlockSpec((1, tokens, width), lambda i, k, meta: (jnp.where(i == 0, k, count - 1), 0, 0))
        )
        args.append(before)
    if last:
        shape = (tokens, count * width // group)
        out_shape = [jax.ShapeDtypeStruct(shape, bf16)] * group
        out_specs = [pl.BlockSpec(shape, lambda i, k, meta: (0, 0))] * group
    else:
        shape = (count, tokens, width)
        out_shape = [jax.ShapeDtypeStruct(shape, f32)]
        out_specs = [pl.BlockSpec(shape, lambda i, k, meta: (0, 0, 0))]
    return pl.pallas_call(
        functools.partial(
            project_body, steps=steps, group=group, has_sum=before is not None, last=last
        ),
        grid_spec=pltpu.PrefetchScalarGridSpec(
            num_scalar_prefetch=1,
            grid=(steps, count),
            in_specs=in_specs,
            out_specs=out_specs,
            scratch_shapes=[
                pltpu.VMEM((steps, tokens, depth), bf16),
                pltpu.VMEM((count, tokens, width), f32),
            ],
        ),
        out_shape=out_shape,
        compiler_params=params(24, 2),
        cost_estimate=pl.CostEstimate(
            flops=2 * steps * tokens * depth * width * count,
            bytes_accessed=2 * steps * depth * width * count,
            transcendentals=0,
        ),
        name="project_last" if last else "project_first",
    )(meta, *args)


def toeplitz_body(meta, pieces_ref, out_ref, row, *, order, group):
    count, width = pieces_ref.shape[1:]
    length = len(order) * width
    step = pl.program_id(0)

    @pl.when(step == 0)
    def _():
        row[:, pl.ds(length, width)] = jnp.zeros((row.shape[0], width), f32)
        for at, m in enumerate(order):
            start = length - width * ((meta[3] ^ m) + 1)
            row[0:count, pl.ds(pl.multiple_of(start, width), width)] = pieces_ref[at]

    span = group * width
    start = pl.multiple_of(length - span * (step + 1), width)
    for k in range(count):
        line = jnp.broadcast_to(row[k : k + 1, pl.ds(start, span + width)], (LANES, span + width))
        turned = pltpu.roll(line, 1, 1, stride=1, stride_axis=0).astype(bf16)
        for e in range(group):
            for h in range(width // LANES):
                at = span - width * e - LANES * h
                out_ref[
                    e * width + h * LANES : e * width + (h + 1) * LANES, k * width : (k + 1) * width
                ] = turned[:, at : at + width]


def toeplitz(meta, pieces, order, group):
    blocks, count, width = pieces.shape
    rows, columns = group * width, count * width
    return pl.pallas_call(
        functools.partial(toeplitz_body, order=order, group=group),
        grid_spec=pltpu.PrefetchScalarGridSpec(
            num_scalar_prefetch=1,
            grid=(blocks // group,),
            in_specs=[pl.BlockSpec(pieces.shape, lambda i, meta: (0, 0, 0))],
            out_specs=pl.BlockSpec((rows, columns), lambda i, meta: (i, 0)),
            scratch_shapes=[pltpu.VMEM((8, (blocks + 1) * width), f32)],
        ),
        out_shape=jax.ShapeDtypeStruct((blocks * width, columns), bf16),
        compiler_params=params(16),
        cost_estimate=pl.CostEstimate(
            flops=blocks * width * columns * 8,
            bytes_accessed=2 * blocks * width * columns,
            transcendentals=0,
        ),
        name="toeplitz",
    )(meta, pieces)


def convolve_body(meta, *refs, group, sub, own):
    if own:
        low_ref, high_ref, refs = None, refs[0], refs[1:]
    else:
        low_ref, high_ref, refs = refs[0], refs[1], refs[2:]
    p_refs, out_refs, (held, placed) = refs[:group], refs[group : 2 * group], refs[2 * group :]
    width = p_refs[0].shape[0]
    count = p_refs[0].shape[1] // sub
    place = meta[1]

    @pl.when(pl.program_id(0) == 0)
    def _():
        for m, p_ref in enumerate(p_refs):
            at = pl.multiple_of((place ^ m) * sub, sub)
            for k in range(count):
                held[k * width : (k + 1) * width, pl.ds(at, sub)] = p_ref[
                    :, k * sub : (k + 1) * sub
                ]

    sums = [None] * group
    for pair in range(0, group, 2):
        side = held[:, pair * sub : (pair + 2) * sub]
        top = group - pair
        high = jnp.dot(high_ref[0 : top * width, :], side, preferred_element_type=f32)
        if not own:
            least = group - pair - 1
            low = jnp.dot(low_ref[least * width :, :], side, preferred_element_type=f32)
        for b in (pair, pair + 1):
            lanes = slice((b - pair) * sub, (b - pair + 1) * sub)
            for r in range(group):
                e = r - b
                if e >= 0:
                    term = high[e * width : (e + 1) * width, lanes]
                elif own:
                    continue
                else:
                    e += group - least
                    term = low[e * width : (e + 1) * width, lanes]
                sums[r] = term if sums[r] is None else sums[r] + term
    for r in range(group):
        placed[place ^ r] = sums[r].astype(bf16)
    for m in range(group):
        out_refs[m][...] = placed[m]


def convolve(meta, table, parts, group, own):
    width = parts[0].shape[0]
    blocks = table.shape[0] // width
    count = table.shape[1] // width
    sub = parts[0].shape[1] // count
    rows, columns = group * width, table.shape[1]
    steps = 1 if own else blocks // group - 1
    high = pl.BlockSpec((rows, columns), lambda i, meta: (i if own else i + 1, 0))
    low = pl.BlockSpec((rows, columns), lambda i, meta: (i, 0))
    part = pl.BlockSpec(parts[0].shape, lambda i, meta: (0, 0))
    tables = [high] if own else [low, high]
    return pl.pallas_call(
        functools.partial(convolve_body, group=group, sub=sub, own=own),
        grid_spec=pltpu.PrefetchScalarGridSpec(
            num_scalar_prefetch=1,
            grid=(steps,),
            in_specs=tables + [part] * group,
            out_specs=[pl.BlockSpec((width, sub), lambda i, meta: (i, 0))] * group,
            scratch_shapes=[
                pltpu.VMEM((columns, group * sub), bf16),
                pltpu.VMEM((group, width, sub), bf16),
            ],
        ),
        out_shape=[jax.ShapeDtypeStruct((steps * width, sub), bf16)] * group,
        compiler_params=params(32),
        cost_estimate=pl.CostEstimate(
            flops=2 * steps * rows * columns * group * sub,
            bytes_accessed=2 * (steps + 1) * rows * columns,
            transcendentals=0,
        ),
        name="convolve_own" if own else "convolve_after",
    )(meta, *[table] * len(tables), *parts)


def finish_body(meta, *refs, group):
    parts, out_ref = refs[:-1], refs[-1]
    sub = out_ref.shape[1] // group
    place, own = meta[1], meta[2]
    for m in range(group):
        value = parts[m][...].astype(f32)
        for far in range(1, len(parts) // group):
            other = parts[far * group + m][...].astype(f32)
            value = value + jnp.where((own ^ far) < own, other, 0.0)
        at = pl.multiple_of((place ^ m) * sub, sub)
        out_ref[:, pl.ds(at, sub)] = value.astype(bf16)


def finish(meta, parts, group):
    width, sub = parts[0].shape
    shape = (width, sub * group)
    return pl.pallas_call(
        functools.partial(finish_body, group=group),
        grid_spec=pltpu.PrefetchScalarGridSpec(
            num_scalar_prefetch=1,
            grid=(1,),
            in_specs=[pl.BlockSpec((width, sub), lambda i, meta: (0, 0))] * len(parts),
            out_specs=pl.BlockSpec(shape, lambda i, meta: (0, 0)),
        ),
        out_shape=jax.ShapeDtypeStruct(shape, bf16),
        compiler_params=params(24),
        name="finish",
    )(meta, *parts)


def local(inputs, weights, filters):
    seq, chan = lax.axis_size("seq"), lax.axis_size("chan")
    group = min(4, seq)
    groups = seq // group
    width = inputs.shape[0]
    at_seq, at_chan = lax.axis_index("seq"), lax.axis_index("chan")
    lane = jnp.arange(4)
    meta = jnp.where(
        lane == 0,
        at_chan,
        jnp.where(lane == 1, at_seq % group, jnp.where(lane == 2, at_seq // group, at_seq)),
    ).astype(jnp.int32)

    held = {0: inputs}
    for m in range(1, chan):
        low = m & -m
        held[m] = swap(held[m - low], "chan", low)

    pieces = jnp.flip(filters, axis=1)[None]
    order = [0]
    bit = seq // 2
    while bit:
        pieces = jnp.concatenate([pieces, swap(pieces, "seq", bit)])
        order += [m ^ bit for m in order]
        bit //= 2
    table = toeplitz(meta, pieces, order, group)

    near = [m for m in range(chan) if m < 2]
    far = [m for m in range(chan) if m >= 2]
    (before,) = project(meta, near, [held[m] for m in near], weights, None, group, False)
    mine = project(meta, far, [held[m] for m in far], weights, before, group, True)
    parts = [mine[0]] + [swap(mine[m], "seq", m) for m in range(1, group)]

    pieces = []
    if groups > 1:
        after = convolve(meta, table, parts, group, False)
        for far in range(1, groups):
            ahead = jnp.maximum(((at_seq // group) ^ far) - at_seq // group - 1, 0)
            for m in range(group):
                piece = after[m]
                if groups > 2:
                    piece = lax.dynamic_slice_in_dim(piece, ahead * width, width, 0)
                pieces.append(swap(piece, "seq", far * group + m))
    own = convolve(meta, table, parts, group, True)
    pieces = [own[0]] + [swap(own[m], "seq", m) for m in range(1, group)] + pieces
    return finish(meta, pieces, group)


def solution(mesh):
    in_specs = (P("seq", "chan"), P(None, None, "chan"), P(None, "seq"))
    out_specs = P("seq", "chan")
    return jax.shard_map(local, mesh=mesh, in_specs=in_specs, out_specs=out_specs, check_vma=False)
```

profile of v0, /device:TPU:0, one launch (start us, length us, event | category | flops | bytes accessed | tf_op | source)
XLA Modules:
  0.0 64.6 jit_solution(1329761023637224582)
XLA Ops:
  0.0 3.0 %collective-permute-start.3 = (bf16[256,512]{1,0:T(8,128)(2,1)}, bf16[256,512]{1,0:T(8,128)(2,1)S(1)}, u32[]{:S(2)}, u32[]{:S(2)}) collective-permute-start(bf16[256,512]{1,0:T(8,128)(2,1)} %refs_0_.1), channel_id=1, source_target_pairs={{0,2},{1,3},{2,0},{3,1},{4,6},{5,7},{6,4},{7,5},{8,10},{9,11},{10,... | collective-permute-start | bytes 786440 | tf_op jit(solution)/shard_map/ppermute | solution.py:17
  3.0 0.0 collective-permute-start.5
  3.0 6.5 %collective-permute-done.3.refs_0_ = bf16[256,512]{1,0:T(8,128)(2,1)S(1)} collective-permute-done((bf16[256,512]{1,0:T(8,128)(2,1)}, bf16[256,512]{1,0:T(8,128)(2,1)S(1)}, u32[]{:S(2)}, u32[]{:S(2)}) %collective-permute-start.3) | collective-permute-done | bytes 262176 | tf_op jit(solution)/shard_map/ppermute | solution.py:17
  9.5 0.0 collective-permute-start.4
  9.5 0.9 %rev.4 = f32[4,256]{1,0:T(4,128)S(1)} reverse(f32[4,256]{1,0:T(4,128)} %param.5), dimensions={1} | reverse | bytes 8192 | tf_op jit(solution)/shard_map/jit(_flip)/rev | solution.py:292
  10.4 2.8 %collective-permute-start = (f32[1,4,256]{2,1,0:T(4,128)S(1)}, f32[1,4,256]{2,1,0:T(4,128)S(1)}, u32[]{:S(2)}, u32[]{:S(2)}) collective-permute-start(f32[1,4,256]{2,1,0:T(4,128)S(1)} %bitcast.1), channel_id=1, source_target_pairs={{0,16},{4,20},{8,24},{12,28},{16,0},{20,4},{24,8},{28,12},{1,17},{... | collective-permute-start | bytes 12296 | tf_op jit(solution)/shard_map/ppermute | solution.py:17
  13.2 0.0 collective-permute-done.5.refs_1_
  13.2 0.0 copy-start
  13.2 3.4 %copy-done = bf16[4,2048,512]{2,1,0:T(8,128)(2,1)S(1)} copy-done((bf16[4,2048,512]{2,1,0:T(8,128)(2,1)S(1)}, bf16[4,2048,512]{2,1,0:T(8,128)(2,1)}, u32[]{:S(2)}) %copy-start) | copy-done | bytes 8388632
  16.6 0.0 copy-start.2
  16.6 0.9 %copy-done.2 = bf16[256,512]{1,0:T(8,128)(2,1)S(1)} copy-done((bf16[256,512]{1,0:T(8,128)(2,1)S(1)}, bf16[256,512]{1,0:T(8,128)(2,1)}, u32[]{:S(2)}) %copy-start.2) | copy-done | bytes 262168
  17.5 0.0 copy-start.1
  17.5 3.3 %project_first.1.refs_3_ = f32[4,256,512]{2,1,0:T(8,128)S(1)} custom-call(s32[4]{0:T(128)S(1)} %compare_select_fusion.2.meta, bf16[256,512]{1,0:T(8,128)(2,1)S(1)} %copy-done.2, bf16[256,512]{1,0:T(8,128)(2,1)S(1)} %collective-permute-done.5.refs_1_, bf16[4,2048,512]{2,1,0:T(8,128)(2,1)S(1)} %copy-done), custom_call_target="tpu_custom_call" | custom-call | flops 1073741824 | bytes 4194304 | tf_op jit(solution)/shard_map/project_first/pallas_call | solution.py:92
  20.9 0.0 collective-permute-done.4.refs_1_
  20.9 0.0 copy-done.1
  20.9 3.5 %project_last.1 = (bf16[256,512]{1,0:T(8,128)(2,1)S(1)}, bf16[256,512]{1,0:T(8,128)(2,1)S(1)}, bf16[256,512]{1,0:T(8,128)(2,1)S(1)}, bf16[256,512]{1,0:T(8,128)(2,1)S(1)}) custom-call(s32[4]{0:T(128)S(1)} %compare_select_fusion.2.meta, bf16[256,512]{1,0:T(8,128)(2,1)S(1)} %collective-permute-done.3.refs_0_, ...), custom_call_target="tpu_custom_call" | custom-call | flops 1073741824 | bytes 4194304 | tf_op jit(solution)/shard_map/project_last/pallas_call | solution.py:92
  24.4 1.5 %collective-permute-start.6 = (bf16[256,512]{1,0:T(8,128)(2,1)S(1)}, bf16[256,512]{1,0:T(8,128)(2,1)S(1)}, u32[]{:S(2)}, u32[]{:S(2)}) collective-permute-start(bf16[256,512]{1,0:T(8,128)(2,1)S(1)} %get-tuple-element.18), channel_id=1, source_target_pairs={{0,4},{4,0},{8,12},{12,8},{16,20},{20,16},{24,28},{28,24},{1,5},{5... | collective-permute-start | bytes 786440 | tf_op jit(solution)/shard_map/ppermute | solution.py:17
  25.9 1.6 %collective-permute-start.7 = (bf16[256,512]{1,0:T(8,128)(2,1)S(1)}, bf16[256,512]{1,0:T(8,128)(2,1)S(1)}, u32[]{:S(2)}, u32[]{:S(2)}) collective-permute-start(bf16[256,512]{1,0:T(8,128)(2,1)S(1)} %get-tuple-element.19), channel_id=1, source_target_pairs={{0,8},{4,12},{8,0},{12,4},{16,24},{20,28},{24,16},{28,20},{1,9},{5... | collective-permute-start | bytes 786440 | tf_op jit(solution)/shard_map/ppermute | solution.py:17
  27.5 0.4 collective-permute-start.8
  27.9 0.0 collective-permute-done
  27.9 1.6 %collective-permute-start.1 = (f32[2,4,256]{2,1,0:T(4,128)S(1)}, f32[2,4,256]{2,1,0:T(4,128)S(1)}, u32[]{:S(2)}, u32[]{:S(2)}) collective-permute-start(f32[2,4,256]{2,1,0:T(4,128)S(1)} %pad_maximum_fusion.2), channel_id=1, source_target_pairs={{0,8},{4,12},{8,0},{12,4},{16,24},{20,28},{24,16},{28,20},{1,9},{5... | collective-permute-start | bytes 24584 | tf_op jit(solution)/shard_map/ppermute | solution.py:17
  29.6 10.3 %collective-permute-done.1 = f32[2,4,256]{2,1,0:T(4,128)S(1)} collective-permute-done((f32[2,4,256]{2,1,0:T(4,128)S(1)}, f32[2,4,256]{2,1,0:T(4,128)S(1)}, u32[]{:S(2)}, u32[]{:S(2)}) %collective-permute-start.1) | collective-permute-done | bytes 8224 | tf_op jit(solution)/shard_map/ppermute | solution.py:17
  39.9 0.6 collective-permute-start.2
  40.4 3.2 %collective-permute-done.2 = f32[4,4,256]{2,1,0:T(4,128)S(1)} collective-permute-done((f32[4,4,256]{2,1,0:T(4,128)S(1)}, f32[4,4,256]{2,1,0:T(4,128)S(1)}, u32[]{:S(2)}, u32[]{:S(2)}) %collective-permute-start.2) | collective-permute-done | bytes 16416 | tf_op jit(solution)/shard_map/ppermute | solution.py:17
  43.6 1.4 %toeplitz.1.refs_0_.refs_1_ = bf16[2048,1024]{1,0:T(8,128)(2,1)S(1)} custom-call(s32[4]{0:T(128)S(1)} %compare_select_fusion.2.meta, f32[8,4,256]{2,1,0:T(4,128)S(1)} %pad_maximum_fusion.pieces_ref), custom_call_target="tpu_custom_call" | custom-call | flops 16777216 | bytes 4194304 | tf_op jit(solution)/shard_map/toeplitz/pallas_call | solution.py:145
  45.0 0.0 collective-permute-done.6.refs_2_.refs_3_
  45.0 0.0 collective-permute-done.7.refs_3_.refs_4_
  45.1 0.0 collective-permute-done.8.refs_4_.refs_5_
  45.1 2.3 %convolve_after.1 = (bf16[256,128]{1,0:T(8,128)(2,1)S(1)}, bf16[256,128]{1,0:T(8,128)(2,1)S(1)}, bf16[256,128]{1,0:T(8,128)(2,1)S(1)}, bf16[256,128]{1,0:T(8,128)(2,1)S(1)}) custom-call(s32[4]{0:T(128)S(1)} %compare_select_fusion.2.meta, bf16[2048,1024]{1,0:T(8,128)(2,1)S(1)} %toeplitz.1.refs_0_.refs_1_, bf16[2048,1024]{1,0:T(8,128)(2,1)S(1)} %toeplitz.1.refs_0_.refs_1_, ...), custom_call_target="tpu_custom_call" | custom-call | flops 1073741824 | bytes 4194304 | tf_op jit(solution)/shard_map/convolve_after/pallas_call | solution.py:221
  47.4 0.4 collective-permute-start.12
  47.8 2.6 %collective-permute-start.13 = (bf16[256,128]{1,0:T(8,128)(2,1)S(1)}, bf16[256,128]{1,0:T(8,128)(2,1)S(1)}, u32[]{:S(2)}, u32[]{:S(2)}) collective-permute-start(bf16[256,128]{1,0:T(8,128)(2,1)S(1)} %get-tuple-element.26), channel_id=1, source_target_pairs={{0,20},{4,16},{8,28},{12,24},{16,4},{20,0},{24,12},{28,8},{1,21},{... | collective-permute-start | bytes 196616 | tf_op jit(solution)/shard_map/ppermute | solution.py:17
  50.4 1.3 %collective-permute-start.14 = (bf16[256,128]{1,0:T(8,128)(2,1)S(1)}, bf16[256,128]{1,0:T(8,128)(2,1)S(1)}, u32[]{:S(2)}, u32[]{:S(2)}) collective-permute-start(bf16[256,128]{1,0:T(8,128)(2,1)S(1)} %get-tuple-element.27), channel_id=1, source_target_pairs={{0,24},{4,28},{8,16},{12,20},{16,8},{20,12},{24,0},{28,4},{1,25},{... | collective-permute-start | bytes 196616 | tf_op jit(solution)/shard_map/ppermute | solution.py:17
  51.8 3.4 %collective-permute-start.15 = (bf16[256,128]{1,0:T(8,128)(2,1)S(1)}, bf16[256,128]{1,0:T(8,128)(2,1)S(1)}, u32[]{:S(2)}, u32[]{:S(2)}) collective-permute-start(bf16[256,128]{1,0:T(8,128)(2,1)S(1)} %get-tuple-element.28), channel_id=1, source_target_pairs={{0,28},{4,24},{8,20},{12,16},{16,12},{20,8},{24,4},{28,0},{1,29},{... | collective-permute-start | bytes 196616 | tf_op jit(solution)/shard_map/ppermute | solution.py:17
  55.1 1.7 %convolve_own.1 = (bf16[256,128]{1,0:T(8,128)(2,1)S(1)}, bf16[256,128]{1,0:T(8,128)(2,1)S(1)}, bf16[256,128]{1,0:T(8,128)(2,1)S(1)}, bf16[256,128]{1,0:T(8,128)(2,1)S(1)}) custom-call(s32[4]{0:T(128)S(1)} %compare_select_fusion.2.meta, bf16[2048,1024]{1,0:T(8,128)(2,1)S(1)} %toeplitz.1.refs_0_.refs_1_, ...), custom_call_target="tpu_custom_call" | custom-call | flops 1073741824 | bytes 4194304 | tf_op jit(solution)/shard_map/convolve_own/pallas_call | solution.py:221
  56.9 0.1 collective-permute-start.10
  56.9 0.0 collective-permute-done.12.refs_4_
  56.9 2.0 %collective-permute-start.11 = (bf16[256,128]{1,0:T(8,128)(2,1)S(1)}, bf16[256,128]{1,0:T(8,128)(2,1)S(1)}, u32[]{:S(2)}, u32[]{:S(2)}) collective-permute-start(bf16[256,128]{1,0:T(8,128)(2,1)S(1)} %get-tuple-element.24), channel_id=1, source_target_pairs={{0,12},{4,8},{8,4},{12,0},{16,28},{20,24},{24,20},{28,16},{1,13},{... | collective-permute-start | bytes 196616 | tf_op jit(solution)/shard_map/ppermute | solution.py:17
  59.0 0.0 collective-permute-done.13.refs_5_
  59.0 1.4 %collective-permute-start.9 = (bf16[256,128]{1,0:T(8,128)(2,1)S(1)}, bf16[256,128]{1,0:T(8,128)(2,1)S(1)}, u32[]{:S(2)}, u32[]{:S(2)}) collective-permute-start(bf16[256,128]{1,0:T(8,128)(2,1)S(1)} %get-tuple-element.22), channel_id=1, source_target_pairs={{0,4},{4,0},{8,12},{12,8},{16,20},{20,16},{24,28},{28,24},{1,5},{5... | collective-permute-start | bytes 196616 | tf_op jit(solution)/shard_map/ppermute | solution.py:17
  60.4 0.0 collective-permute-done.14.refs_6_
  60.4 0.0 collective-permute-done.15.refs_7_
  60.4 0.8 %collective-permute-done.10.refs_2_ = bf16[256,128]{1,0:T(8,128)(2,1)S(1)} collective-permute-done((bf16[256,128]{1,0:T(8,128)(2,1)S(1)}, bf16[256,128]{1,0:T(8,128)(2,1)S(1)}, u32[]{:S(2)}, u32[]{:S(2)}) %collective-permute-start.10) | collective-permute-done | bytes 65568 | tf_op jit(solution)/shard_map/ppermute | solution.py:17
  61.2 1.0 %collective-permute-done.11.refs_3_ = bf16[256,128]{1,0:T(8,128)(2,1)S(1)} collective-permute-done((bf16[256,128]{1,0:T(8,128)(2,1)S(1)}, bf16[256,128]{1,0:T(8,128)(2,1)S(1)}, u32[]{:S(2)}, u32[]{:S(2)}) %collective-permute-start.11) | collective-permute-done | bytes 65568 | tf_op jit(solution)/shard_map/ppermute | solution.py:17
  62.2 1.1 %collective-permute-done.9.refs_1_ = bf16[256,128]{1,0:T(8,128)(2,1)S(1)} collective-permute-done((bf16[256,128]{1,0:T(8,128)(2,1)S(1)}, bf16[256,128]{1,0:T(8,128)(2,1)S(1)}, u32[]{:S(2)}, u32[]{:S(2)}) %collective-permute-start.9) | collective-permute-done | bytes 65568 | tf_op jit(solution)/shard_map/ppermute | solution.py:17
  63.2 1.3 %finish.1 = bf16[256,512]{1,0:T(8,128)(2,1)} custom-call(s32[4]{0:T(128)S(1)} %compare_select_fusion.2.meta, bf16[256,128]{1,0:T(8,128)(2,1)S(1)} %get-tuple-element.21.refs_0_, bf16[256,128]{1,0:T(8,128)(2,1)S(1)} %collective-permute-done.9.refs_1_, bf16[256,128]{1,0:T(8,128)(2,1)S(1)} %collective-permute-done.10.refs_2_, ...), custom_call_target="tpu_custom_call" | custom-call | tf_op jit(solution)/shard_map/finish/pallas_call | solution.py:260
  (4 shorter events, 0.0 us)
Async XLA Ops:
  0.0 9.5 %collective-permute-start.3 = (bf16[256,512]{1,0:T(8,128)(2,1)}, bf16[256,512]{1,0:T(8,128)(2,1)S(1)}, u32[]{:S(2)}, u32[]{:S(2)}) collective-permute-start(bf16[256,512]{1,0:T(8,128)(2,1)} %refs_0_.1), channel_id=1, source_target_pairs={{0,2},{1,3},{2,0},{3,1},{4,6},{5,7},{6,4},{7,5},{8,10},{9,11},{10,... | collective-permute-start | bytes 786440 | tf_op jit(solution)/shard_map/ppermute | solution.py:17
  3.0 10.2 %collective-permute-start.5 = (bf16[256,512]{1,0:T(8,128)(2,1)}, bf16[256,512]{1,0:T(8,128)(2,1)S(1)}, u32[]{:S(2)}, u32[]{:S(2)}) collective-permute-start(bf16[256,512]{1,0:T(8,128)(2,1)} %refs_0_.1), channel_id=1, source_target_pairs={{0,1},{1,0},{2,3},{3,2},{4,5},{5,4},{6,7},{7,6},{8,9},{9,8},{10,11... | collective-permute-start | bytes 786440 | tf_op jit(solution)/shard_map/ppermute | solution.py:17
  9.5 11.4 %collective-permute-start.4 = (bf16[256,512]{1,0:T(8,128)(2,1)S(1)}, bf16[256,512]{1,0:T(8,128)(2,1)S(1)}, u32[]{:S(2)}, u32[]{:S(2)}) collective-permute-start(bf16[256,512]{1,0:T(8,128)(2,1)S(1)} %collective-permute-done.3.refs_0_), channel_id=1, source_target_pairs={{0,1},{1,0},{2,3},{3,2},{4,5},{5,4},{6,7},{7,6},{8,9},{9,8},{10,11... | collective-permute-start | bytes 786440 | tf_op jit(solution)/shard_map/ppermute | solution.py:17
  10.4 17.6 %collective-permute-start = (f32[1,4,256]{2,1,0:T(4,128)S(1)}, f32[1,4,256]{2,1,0:T(4,128)S(1)}, u32[]{:S(2)}, u32[]{:S(2)}) collective-permute-start(f32[1,4,256]{2,1,0:T(4,128)S(1)} %bitcast.1), channel_id=1, source_target_pairs={{0,16},{4,20},{8,24},{12,28},{16,0},{20,4},{24,8},{28,12},{1,17},{... | collective-permute-start | bytes 12296 | tf_op jit(solution)/shard_map/ppermute | solution.py:17
  13.2 3.4 %copy-start = (bf16[4,2048,512]{2,1,0:T(8,128)(2,1)S(1)}, bf16[4,2048,512]{2,1,0:T(8,128)(2,1)}, u32[]{:S(2)}) copy-start(bf16[4,2048,512]{2,1,0:T(8,128)(2,1)} %refs_2_.3) | copy-start | bytes 25165828
  16.6 0.9 %copy-start.2 = (bf16[256,512]{1,0:T(8,128)(2,1)S(1)}, bf16[256,512]{1,0:T(8,128)(2,1)}, u32[]{:S(2)}) copy-start(bf16[256,512]{1,0:T(8,128)(2,1)} %refs_0_.1) | copy-start | bytes 786436
  17.5 3.4 %copy-start.1 = (bf16[4,2048,512]{2,1,0:T(8,128)(2,1)S(1)}, bf16[4,2048,512]{2,1,0:T(8,128)(2,1)}, u32[]{:S(2)}) copy-start(bf16[4,2048,512]{2,1,0:T(8,128)(2,1)} %refs_2_.3) | copy-start | bytes 25165828
  24.4 20.7 %collective-permute-start.6 = (bf16[256,512]{1,0:T(8,128)(2,1)S(1)}, bf16[256,512]{1,0:T(8,128)(2,1)S(1)}, u32[]{:S(2)}, u32[]{:S(2)}) collective-permute-start(bf16[256,512]{1,0:T(8,128)(2,1)S(1)} %get-tuple-element.18), channel_id=1, source_target_pairs={{0,4},{4,0},{8,12},{12,8},{16,20},{20,16},{24,28},{28,24},{1,5},{5... | collective-permute-start | bytes 786440 | tf_op jit(solution)/shard_map/ppermute | solution.py:17
  25.9 19.2 %collective-permute-start.7 = (bf16[256,512]{1,0:T(8,128)(2,1)S(1)}, bf16[256,512]{1,0:T(8,128)(2,1)S(1)}, u32[]{:S(2)}, u32[]{:S(2)}) collective-permute-start(bf16[256,512]{1,0:T(8,128)(2,1)S(1)} %get-tuple-element.19), channel_id=1, source_target_pairs={{0,8},{4,12},{8,0},{12,4},{16,24},{20,28},{24,16},{28,20},{1,9},{5... | collective-permute-start | bytes 786440 | tf_op jit(solution)/shard_map/ppermute | solution.py:17
  27.5 17.5 %collective-permute-start.8 = (bf16[256,512]{1,0:T(8,128)(2,1)S(1)}, bf16[256,512]{1,0:T(8,128)(2,1)S(1)}, u32[]{:S(2)}, u32[]{:S(2)}) collective-permute-start(bf16[256,512]{1,0:T(8,128)(2,1)S(1)} %get-tuple-element.20), channel_id=1, source_target_pairs={{0,12},{4,8},{8,4},{12,0},{16,28},{20,24},{24,20},{28,16},{1,13},{... | collective-permute-start | bytes 786440 | tf_op jit(solution)/shard_map/ppermute | solution.py:17
  27.9 11.9 %collective-permute-start.1 = (f32[2,4,256]{2,1,0:T(4,128)S(1)}, f32[2,4,256]{2,1,0:T(4,128)S(1)}, u32[]{:S(2)}, u32[]{:S(2)}) collective-permute-start(f32[2,4,256]{2,1,0:T(4,128)S(1)} %pad_maximum_fusion.2), channel_id=1, source_target_pairs={{0,8},{4,12},{8,0},{12,4},{16,24},{20,28},{24,16},{28,20},{1,9},{5... | collective-permute-start | bytes 24584 | tf_op jit(solution)/shard_map/ppermute | solution.py:17
  39.9 3.7 %collective-permute-start.2 = (f32[4,4,256]{2,1,0:T(4,128)S(1)}, f32[4,4,256]{2,1,0:T(4,128)S(1)}, u32[]{:S(2)}, u32[]{:S(2)}) collective-permute-start(f32[4,4,256]{2,1,0:T(4,128)S(1)} %pad_maximum_fusion.1), channel_id=1, source_target_pairs={{0,4},{4,0},{8,12},{12,8},{16,20},{20,16},{24,28},{28,24},{1,5},{5... | collective-permute-start | bytes 49160 | tf_op jit(solution)/shard_map/ppermute | solution.py:17
  47.4 9.5 %collective-permute-start.12 = (bf16[256,128]{1,0:T(8,128)(2,1)S(1)}, bf16[256,128]{1,0:T(8,128)(2,1)S(1)}, u32[]{:S(2)}, u32[]{:S(2)}) collective-permute-start(bf16[256,128]{1,0:T(8,128)(2,1)S(1)} %get-tuple-element.25), channel_id=1, source_target_pairs={{0,16},{4,20},{8,24},{12,28},{16,0},{20,4},{24,8},{28,12},{1,17},{... | collective-permute-start | bytes 196616 | tf_op jit(solution)/shard_map/ppermute | solution.py:17
  47.8 11.2 %collective-permute-start.13 = (bf16[256,128]{1,0:T(8,128)(2,1)S(1)}, bf16[256,128]{1,0:T(8,128)(2,1)S(1)}, u32[]{:S(2)}, u32[]{:S(2)}) collective-permute-start(bf16[256,128]{1,0:T(8,128)(2,1)S(1)} %get-tuple-element.26), channel_id=1, source_target_pairs={{0,20},{4,16},{8,28},{12,24},{16,4},{20,0},{24,12},{28,8},{1,21},{... | collective-permute-start | bytes 196616 | tf_op jit(solution)/shard_map/ppermute | solution.py:17
  50.4 10.0 %collective-permute-start.14 = (bf16[256,128]{1,0:T(8,128)(2,1)S(1)}, bf16[256,128]{1,0:T(8,128)(2,1)S(1)}, u32[]{:S(2)}, u32[]{:S(2)}) collective-permute-start(bf16[256,128]{1,0:T(8,128)(2,1)S(1)} %get-tuple-element.27), channel_id=1, source_target_pairs={{0,24},{4,28},{8,16},{12,20},{16,8},{20,12},{24,0},{28,4},{1,25},{... | collective-permute-start | bytes 196616 | tf_op jit(solution)/shard_map/ppermute | solution.py:17
  51.8 8.7 %collective-permute-start.15 = (bf16[256,128]{1,0:T(8,128)(2,1)S(1)}, bf16[256,128]{1,0:T(8,128)(2,1)S(1)}, u32[]{:S(2)}, u32[]{:S(2)}) collective-permute-start(bf16[256,128]{1,0:T(8,128)(2,1)S(1)} %get-tuple-element.28), channel_id=1, source_target_pairs={{0,28},{4,24},{8,20},{12,16},{16,12},{20,8},{24,4},{28,0},{1,29},{... | collective-permute-start | bytes 196616 | tf_op jit(solution)/shard_map/ppermute | solution.py:17
  56.9 4.3 %collective-permute-start.10 = (bf16[256,128]{1,0:T(8,128)(2,1)S(1)}, bf16[256,128]{1,0:T(8,128)(2,1)S(1)}, u32[]{:S(2)}, u32[]{:S(2)}) collective-permute-start(bf16[256,128]{1,0:T(8,128)(2,1)S(1)} %get-tuple-element.23), channel_id=1, source_target_pairs={{0,8},{4,12},{8,0},{12,4},{16,24},{20,28},{24,16},{28,20},{1,9},{5... | collective-permute-start | bytes 196616 | tf_op jit(solution)/shard_map/ppermute | solution.py:17
  56.9 5.2 %collective-permute-start.11 = (bf16[256,128]{1,0:T(8,128)(2,1)S(1)}, bf16[256,128]{1,0:T(8,128)(2,1)S(1)}, u32[]{:S(2)}, u32[]{:S(2)}) collective-permute-start(bf16[256,128]{1,0:T(8,128)(2,1)S(1)} %get-tuple-element.24), channel_id=1, source_target_pairs={{0,12},{4,8},{8,4},{12,0},{16,28},{20,24},{24,20},{28,16},{1,13},{... | collective-permute-start | bytes 196616 | tf_op jit(solution)/shard_map/ppermute | solution.py:17
  59.0 4.3 %collective-permute-start.9 = (bf16[256,128]{1,0:T(8,128)(2,1)S(1)}, bf16[256,128]{1,0:T(8,128)(2,1)S(1)}, u32[]{:S(2)}, u32[]{:S(2)}) collective-permute-start(bf16[256,128]{1,0:T(8,128)(2,1)S(1)} %get-tuple-element.22), channel_id=1, source_target_pairs={{0,4},{4,0},{8,12},{12,8},{16,20},{20,16},{24,28},{28,24},{1,5},{5... | collective-permute-start | bytes 196616 | tf_op jit(solution)/shard_map/ppermute | solution.py:17
where the time goes:
time: 64.8 us; the launch traced here: 64.6 us
  starting transfers between devices  22.8 us (35%)
  waiting for transfers between devices  22.8 us (35%)
  Pallas kernels  13.6 us (21%)
  local copies, waits for them, and re-layouts  5.22 us (8%)
    ppermute x16, starting transfers between devices, swap(): lax.ppermute(value, axis, [(i, i ^ mask) for i in range(lax.axis_size(axi...  22.8 us
    ppermute x16, waiting for transfers between devices, swap(): lax.ppermute(value, axis, [(i, i ^ mask) for i in range(lax.axis_size(axi...  22.8 us
    pallas_call x2, Pallas kernels, project(): pl.pallas_call(functools.partial(project_body, steps=steps, group=group,...  6.8 us
    unnamed x6, local copies, waits for them, and re-layouts  4.36 us
    pallas_call x2, Pallas kernels, convolve(): pl.pallas_call(functools.partial(convolve_body, group=group, sub=sub, own...  4.05 us
    pallas_call x1, Pallas kernels, toeplitz(): pl.pallas_call(functools.partial(toeplitz_body, order=order, group=group)...  1.43 us
    pallas_call x1, Pallas kernels, finish(): pl.pallas_call(functools.partial(finish_body, group=group), grid_spec=plt...  1.33 us
  transfers between devices with their start and end apart: 16, of which 6 were waited for; matrix products, arithmetic and copies ran while one was open for 1% of the time, Pallas kernels for 15%

commit v1 on v0

v1 whole, which is shorter than its diff:
```python
import functools

import jax
import jax.numpy as jnp
from jax import lax
from jax.experimental import pallas as pl
from jax.experimental.pallas import tpu as pltpu
from jax.sharding import PartitionSpec as P


f32 = jnp.float32
bf16 = jnp.bfloat16
LANES = 128


def swap(value, axis, mask):
    return lax.ppermute(value, axis, [(i, i ^ mask) for i in range(lax.axis_size(axis))])


def params(mib, axes=1):
    return pltpu.CompilerParams(
        dimension_semantics=("arbitrary",) * axes if axes else None,
        vmem_limit_bytes=mib * 1024 * 1024,
    )


def columns_of(w, place, group):
    sub = w.shape[1] // group
    return jnp.concatenate(
        [w[:, pl.ds(pl.multiple_of((place ^ m) * sub, sub), sub)] for m in range(group)], axis=1
    )


def project_first_body(meta, *refs, near, far, group):
    x_refs, w_ref = refs[: len(near)], refs[len(near)]
    sum_ref, ahead_ref, held, sems = refs[len(near) + 1 :]
    depth = x_refs[0].shape[1]
    count = w_ref.shape[0]

    def fetch(k, m, target, sem):
        rows = pl.ds(pl.multiple_of((meta[0] ^ m) * depth, depth), depth)
        return pltpu.make_async_copy(w_ref.at[k, rows, :], target, sem)

    first = [
        [fetch(k, m, held.at[k, pl.ds(j * depth, depth), :], sems.at[k, j]) for j, m in enumerate(near)]
        for k in range(count)
    ]
    later = [
        fetch(k, m, ahead_ref.at[j, k], sems.at[k, len(near) + j])
        for j, m in enumerate(far)
        for k in range(count)
    ]
    for copy in [copy for copies in first for copy in copies] + later:
        copy.start()
    x = jnp.concatenate([x_ref[...] for x_ref in x_refs], axis=1)
    for k in range(count):
        for copy in first[k]:
            copy.wait()
        sum_ref[k] = jnp.dot(x, columns_of(held.at[k], meta[1], group), preferred_element_type=f32)
    for copy in later:
        copy.wait()


def project_first(meta, near, far, blocks, weights, group):
    tokens, depth = blocks[0].shape
    count, _, width = weights.shape
    vmem = pl.BlockSpec(memory_space=pltpu.VMEM)
    return pl.pallas_call(
        functools.partial(project_first_body, near=near, far=far, group=group),
        in_specs=[pl.BlockSpec(memory_space=pltpu.SMEM)]
        + [vmem] * len(near)
        + [pl.BlockSpec(memory_space=pltpu.HBM)],
        out_specs=[vmem, vmem],
        scratch_shapes=[
            pltpu.VMEM((count, len(near) * depth, width), bf16),
            pltpu.SemaphoreType.DMA((count, len(near) + len(far))),
        ],
        out_shape=[
            jax.ShapeDtypeStruct((count, tokens, width), f32),
            jax.ShapeDtypeStruct((len(far), count, depth, width), bf16),
        ],
        compiler_params=params(32, 0),
        cost_estimate=pl.CostEstimate(
            flops=2 * len(near) * tokens * depth * width * count,
            bytes_accessed=2 * weights.size,
            transcendentals=0,
        ),
        name="project_first",
    )(meta, *blocks, weights)


def project_next_body(meta, x_ref, w_ref, sum_ref, *out_refs, at, group, last):
    count, _, width = sum_ref.shape
    sub = width // group
    for k in range(count):
        total = sum_ref[k] + jnp.dot(
            x_ref[...], columns_of(w_ref.at[at, k], meta[1], group), preferred_element_type=f32
        )
        if last:
            for m in range(group):
                out_refs[m][:, k * sub : (k + 1) * sub] = total[
                    :, m * sub : (m + 1) * sub
                ].astype(bf16)
        else:
            out_refs[0][k] = total


def project_next(meta, at, block, ahead, before, group, last):
    count, tokens, width = before.shape
    vmem = pl.BlockSpec(memory_space=pltpu.VMEM)
    if last:
        shape = (tokens, count * width // group)
        out_shape = [jax.ShapeDtypeStruct(shape, bf16)] * group
    else:
        out_shape = [jax.ShapeDtypeStruct(before.shape, f32)]
    return pl.pallas_call(
        functools.partial(project_next_body, at=at, group=group, last=last),
        in_specs=[pl.BlockSpec(memory_space=pltpu.SMEM)] + [vmem] * 3,
        out_specs=[vmem] * len(out_shape),
        out_shape=out_shape,
        compiler_params=params(32, 0),
        cost_estimate=pl.CostEstimate(
            flops=2 * tokens * block.shape[1] * width * count,
            bytes_accessed=2 * block.shape[1] * width * count,
            transcendentals=0,
        ),
        name="project_last" if last else "project_more",
    )(meta, block, ahead, before)


def toeplitz_body(meta, pieces_ref, out_ref, row, *, order, group):
    count, width = pieces_ref.shape[1:]
    length = len(order) * width
    step = pl.program_id(0)

    @pl.when(step == 0)
    def _():
        row[:, pl.ds(length, width)] = jnp.zeros((row.shape[0], width), f32)
        across = lax.broadcasted_iota(jnp.int32, (width, width), 0)
        along = lax.broadcasted_iota(jnp.int32, (width, width), 1)
        mirror = (across + along == width - 1).astype(bf16)
        turned = jnp.dot(
            pieces_ref[...].reshape(len(order) * count, width).astype(bf16),
            mirror,
            preferred_element_type=f32,
        )
        for at, m in enumerate(order):
            start = length - width * ((meta[3] ^ m) + 1)
            row[0:count, pl.ds(pl.multiple_of(start, width), width)] = turned[
                at * count : (at + 1) * count
            ]

    span = group * width
    start = pl.multiple_of(length - span * (step + 1), width)
    for k in range(count):
        line = jnp.broadcast_to(row[k : k + 1, pl.ds(start, span + width)], (LANES, span + width))
        turned = pltpu.roll(line, 1, 1, stride=1, stride_axis=0).astype(bf16)
        for e in range(group):
            for h in range(width // LANES):
                at = span - width * e - LANES * h
                out_ref[
                    e * width + h * LANES : e * width + (h + 1) * LANES, k * width : (k + 1) * width
                ] = turned[:, at : at + width]


def toeplitz(meta, pieces, order, group):
    blocks, count, width = pieces.shape
    rows, columns = group * width, count * width
    return pl.pallas_call(
        functools.partial(toeplitz_body, order=order, group=group),
        grid_spec=pltpu.PrefetchScalarGridSpec(
            num_scalar_prefetch=1,
            grid=(blocks // group,),
            in_specs=[pl.BlockSpec(pieces.shape, lambda i, meta: (0, 0, 0))],
            out_specs=pl.BlockSpec((rows, columns), lambda i, meta: (i, 0)),
            scratch_shapes=[pltpu.VMEM((8, (blocks + 1) * width), f32)],
        ),
        out_shape=jax.ShapeDtypeStruct((blocks * width, columns), bf16),
        compiler_params=params(16),
        cost_estimate=pl.CostEstimate(
            flops=blocks * width * columns * 8,
            bytes_accessed=2 * blocks * width * columns,
            transcendentals=0,
        ),
        name="toeplitz",
    )(meta, pieces)


def convolve_body(meta, *refs, group, sub, own, whole):
    if whole:
        rows = group * refs[1].shape[0]
        low_ref, high_ref, refs = refs[0].at[0:rows], refs[0].at[0 if own else rows :], refs[1:]
    elif own:
        low_ref, high_ref, refs = None, refs[0], refs[1:]
    else:
        low_ref, high_ref, refs = refs[0], refs[1], refs[2:]
    p_refs, out_refs, (held, placed) = refs[:group], refs[group : 2 * group], refs[2 * group :]
    width = p_refs[0].shape[0]
    count = p_refs[0].shape[1] // sub
    place = meta[1]

    @pl.when(True if whole else pl.program_id(0) == 0)
    def _():
        for m, p_ref in enumerate(p_refs):
            at = pl.multiple_of((place ^ m) * sub, sub)
            for k in range(count):
                held[k * width : (k + 1) * width, pl.ds(at, sub)] = p_ref[
                    :, k * sub : (k + 1) * sub
                ]

    sums = [None] * group
    for pair in range(0, group, 2):
        side = held[:, pair * sub : (pair + 2) * sub]
        top = group - pair
        high = jnp.dot(high_ref[0 : top * width, :], side, preferred_element_type=f32)
        if not own:
            least = group - pair - 1
            low = jnp.dot(low_ref[least * width :, :], side, preferred_element_type=f32)
        for b in (pair, pair + 1):
            lanes = slice((b - pair) * sub, (b - pair + 1) * sub)
            for r in range(group):
                e = r - b
                if e >= 0:
                    term = high[e * width : (e + 1) * width, lanes]
                elif own:
                    continue
                else:
                    e += group - least
                    term = low[e * width : (e + 1) * width, lanes]
                sums[r] = term if sums[r] is None else sums[r] + term
    for r in range(group):
        placed[place ^ r] = sums[r].astype(bf16)
    for m in range(group):
        out_refs[m][...] = placed[m]


def convolve(meta, table, parts, group, own):
    width = parts[0].shape[0]
    blocks = table.shape[0] // width
    count = table.shape[1] // width
    sub = parts[0].shape[1] // count
    rows, columns = group * width, table.shape[1]
    steps = 1 if own else blocks // group - 1
    high = pl.BlockSpec((rows, columns), lambda i, meta: (i if own else i + 1, 0))
    low = pl.BlockSpec((rows, columns), lambda i, meta: (i, 0))
    part = pl.BlockSpec(parts[0].shape, lambda i, meta: (0, 0))
    tables = [high] if own else [low, high]
    scratch = [pltpu.VMEM((columns, group * sub), bf16), pltpu.VMEM((group, width, sub), bf16)]
    call = functools.partial(
        pl.pallas_call,
        out_shape=[jax.ShapeDtypeStruct((steps * width, sub), bf16)] * group,
        cost_estimate=pl.CostEstimate(
            flops=2 * steps * rows * columns * group * sub,
            bytes_accessed=2 * (steps + 1) * rows * columns,
            transcendentals=0,
        ),
        name="convolve_own" if own else "convolve_after",
    )
    if blocks == 2 * group:
        vmem = pl.BlockSpec(memory_space=pltpu.VMEM)
        return call(
            functools.partial(convolve_body, group=group, sub=sub, own=own, whole=True),
            in_specs=[pl.BlockSpec(memory_space=pltpu.SMEM)] + [vmem] * (1 + group),
            out_specs=[vmem] * group,
            scratch_shapes=scratch,
            compiler_params=params(32, 0),
        )(meta, table, *parts)
    return call(
        functools.partial(convolve_body, group=group, sub=sub, own=own, whole=False),
        grid_spec=pltpu.PrefetchScalarGridSpec(
            num_scalar_prefetch=1,
            grid=(steps,),
            in_specs=tables + [part] * group,
            out_specs=[pl.BlockSpec((width, sub), lambda i, meta: (i, 0))] * group,
            scratch_shapes=scratch,
        ),
        compiler_params=params(32),
    )(meta, *[table] * len(tables), *parts)


def finish_body(meta, *refs, group):
    parts, out_ref = refs[:-1], refs[-1]
    sub = out_ref.shape[1] // group
    place, own = meta[1], meta[2]
    for m in range(group):
        value = parts[m][...].astype(f32)
        for far in range(1, len(parts) // group):
            other = parts[far * group + m][...].astype(f32)
            value = value + jnp.where((own ^ far) < own, other, 0.0)
        at = pl.multiple_of((place ^ m) * sub, sub)
        out_ref[:, pl.ds(at, sub)] = value.astype(bf16)


def finish(meta, parts, group):
    width, sub = parts[0].shape
    shape = (width, sub * group)
    return pl.pallas_call(
        functools.partial(finish_body, group=group),
        in_specs=[pl.BlockSpec(memory_space=pltpu.SMEM)]
        + [pl.BlockSpec(memory_space=pltpu.VMEM)] * len(parts),
        out_specs=pl.BlockSpec(memory_space=pltpu.VMEM),
        out_shape=jax.ShapeDtypeStruct(shape, bf16),
        compiler_params=params(24, 0),
        name="finish",
    )(meta, *parts)


def local(inputs, weights, filters):
    seq, chan = lax.axis_size("seq"), lax.axis_size("chan")
    group = min(4, seq)
    groups = seq // group
    width = inputs.shape[0]
    at_seq, at_chan = lax.axis_index("seq"), lax.axis_index("chan")
    lane = jnp.arange(4)
    meta = jnp.where(
        lane == 0,
        at_chan,
        jnp.where(lane == 1, at_seq % group, jnp.where(lane == 2, at_seq // group, at_seq)),
    ).astype(jnp.int32)

    far = [m for m in range(chan) if m >= 2]
    held = {0: inputs}
    held[2] = swap(inputs, "chan", 2)
    held[1] = swap(inputs, "chan", 1)
    held[3] = swap(held[2], "chan", 1)

    pieces = filters[None]
    order = [0]
    bit = seq // 2
    while bit:
        pieces = jnp.concatenate([pieces, swap(pieces, "seq", bit)])
        order += [m ^ bit for m in order]
        bit //= 2
    table = toeplitz(meta, pieces, order, group)

    before, ahead = project_first(meta, [0, 1], far, [held[0], held[1]], weights, group)
    (before,) = project_next(meta, 0, held[2], ahead, before, group, False)
    mine = project_next(meta, 1, held[3], ahead, before, group, True)
    parts = {0: mine[0]}
    for m in reversed(range(1, group)):
        parts[m] = swap(mine[m], "seq", m)
    parts = [parts[m] for m in range(group)]

    pieces = []
    if groups > 1:
        after = convolve(meta, table, parts, group, False)
        for far in range(1, groups):
            ahead = jnp.maximum(((at_seq // group) ^ far) - at_seq // group - 1, 0)
            for m in range(group):
                piece = after[m]
                if groups > 2:
                    piece = lax.dynamic_slice_in_dim(piece, ahead * width, width, 0)
                pieces.append(swap(piece, "seq", far * group + m))
    own = convolve(meta, table, parts, group, True)
    near = {0: own[0]}
    for m in range(1, group):
        near[m] = swap(own[m], "seq", m)
    return finish(meta, [near[m] for m in range(group)] + pieces, group)


def solution(mesh):
    in_specs = (P("seq", "chan"), P(None, None, "chan"), P(None, "seq"))
    out_specs = P("seq", "chan")
    return jax.shard_map(local, mesh=mesh, in_specs=in_specs, out_specs=out_specs, check_vma=False)
```

time: 64.8 us -> 60.7 us (0.937)
  waiting for transfers between devices: 22.8 us -> 21 us
  Pallas kernels: 13.6 us -> 12.7 us
  local copies, waits for them, and re-layouts: 5.22 us -> 4.33 us
    ppermute x16, waiting for transfers between devices: 22.8 us -> 21 us  [swap(): lax.ppermute(value, axis, [(i, i ^ mask) for i in range(lax.axis_size(axi...]
    pallas_call x5 -> x6, Pallas kernels: 12.2 us -> 11.1 us  [the longest x2 4.06 us: convolve(): call(functools.partial(convolve_body, group=group, sub=sub, own=own, whol...]
    rev x1 -> x0, local copies, waits for them, and re-layouts: 0.86 us -> none  [local(): pieces = jnp.flip(filters, axis=1)[None]]
  transfers between devices with their start and end apart: 16 -> 16, of which waited for: 6 -> 8; matrix products, arithmetic and copies ran while one was open for 1% -> 0% of each run, Pallas kernels for 15% -> 15%
where the time goes in v1:
time: 60.7 us; the launch traced here: 60.5 us
  starting transfers between devices  22.4 us (37%)
  waiting for transfers between devices  21 us (35%)
  Pallas kernels  12.7 us (21%)
  local copies, waits for them, and re-layouts  4.33 us (7%)
    ppermute x16, starting transfers between devices, swap(): lax.ppermute(value, axis, [(i, i ^ mask) for i in range(lax.axis_size(axi...  22.4 us
    ppermute x16, waiting for transfers between devices, swap(): lax.ppermute(value, axis, [(i, i ^ mask) for i in range(lax.axis_size(axi...  21 us
    unnamed x6, local copies, waits for them, and re-layouts  4.33 us
    pallas_call x2, Pallas kernels, convolve(): call(functools.partial(convolve_body, group=group, sub=sub, own=own, whol...  4.06 us
    pallas_call x1, Pallas kernels, project_first(): pl.pallas_call(functools.partial(project_first_body, near=near, far=far,...  3.1 us
    pallas_call x2, Pallas kernels, project_next(): pl.pallas_call(functools.partial(project_next_body, at=at, group=group, l...  2.61 us
    pallas_call x1, Pallas kernels, toeplitz(): pl.pallas_call(functools.partial(toeplitz_body, order=order, group=group)...  1.57 us
    pallas_call x1, Pallas kernels, finish(): pl.pallas_call(functools.partial(finish_body, group=group), in_specs=[pl....  1.33 us
  transfers between devices with their start and end apart: 16, of which 8 were waited for; matrix products, arithmetic and copies ran while one was open for 0% of the time, Pallas kernels for 15%

profile of v1, /device:TPU:0, one launch (start us, length us, event | category | flops | bytes accessed | tf_op | source)
XLA Modules:
  0.0 60.5 jit_solution(1385618250206930141)
XLA Ops:
  0.0 3.0 %collective-permute-start.3 = (bf16[256,512]{1,0:T(8,128)(2,1)}, bf16[256,512]{1,0:T(8,128)(2,1)S(1)}, u32[]{:S(2)}, u32[]{:S(2)}) collective-permute-start(bf16[256,512]{1,0:T(8,128)(2,1)} %refs_0_.1), channel_id=1, source_target_pairs={{0,2},{1,3},{2,0},{3,1},{4,6},{5,7},{6,4},{7,5},{8,10},{9,11},{10,... | collective-permute-start | bytes 786440 | tf_op jit(solution)/shard_map/ppermute | solution.py:17
  3.0 0.0 collective-permute-start.5
  3.0 2.6 %collective-permute-start = (f32[1,4,256]{2,1,0:T(4,128)}, f32[1,4,256]{2,1,0:T(4,128)S(1)}, u32[]{:S(2)}, u32[]{:S(2)}) collective-permute-start(f32[1,4,256]{2,1,0:T(4,128)} %bitcast.1), channel_id=1, source_target_pairs={{0,16},{4,20},{8,24},{12,28},{16,0},{20,4},{24,8},{28,12},{1,17},{... | collective-permute-start | bytes 12296 | tf_op jit(solution)/shard_map/ppermute | solution.py:17
  5.6 3.9 %collective-permute-done.3.x_ref = bf16[256,512]{1,0:T(8,128)(2,1)S(1)} collective-permute-done((bf16[256,512]{1,0:T(8,128)(2,1)}, bf16[256,512]{1,0:T(8,128)(2,1)S(1)}, u32[]{:S(2)}, u32[]{:S(2)}) %collective-permute-start.3) | collective-permute-done | bytes 262176 | tf_op jit(solution)/shard_map/ppermute | solution.py:17
  9.5 0.0 collective-permute-start.4
  9.5 0.0 collective-permute-done.5.refs_1_
  9.5 0.0 copy-start
  9.5 3.4 %copy-done = bf16[4,2048,512]{2,1,0:T(8,128)(2,1)S(1)} copy-done((bf16[4,2048,512]{2,1,0:T(8,128)(2,1)S(1)}, bf16[4,2048,512]{2,1,0:T(8,128)(2,1)}, u32[]{:S(2)}) %copy-start) | copy-done | bytes 8388632
  12.9 0.0 copy-start.1
  12.9 0.9 %copy-done.1 = bf16[256,512]{1,0:T(8,128)(2,1)S(1)} copy-done((bf16[256,512]{1,0:T(8,128)(2,1)S(1)}, bf16[256,512]{1,0:T(8,128)(2,1)}, u32[]{:S(2)}) %copy-start.1) | copy-done | bytes 262168
  13.9 3.1 %project_first.1 = (f32[4,256,512]{2,1,0:T(8,128)S(1)}, bf16[2,4,512,512]{3,2,1,0:T(8,128)(2,1)S(1)}) custom-call(s32[4]{0:T(128)S(1)} %compare_select_fusion.2.meta, bf16[256,512]{1,0:T(8,128)(2,1)S(1)} %copy-done.1, bf16[256,512]{1,0:T(8,128)(2,1)S(1)} %collective-permute-done.5.refs_1_, bf16[4,2048,512]{2,1,0:T(8,128)(2,1)S(1)} %copy-done), custom_call_target="tpu_custom_call" | custom-call | flops 1073741824 | bytes 8388608 | tf_op jit(solution)/shard_map/project_first/pallas_call | solution.py:68
  17.0 1.3 %project_more.1.sum_ref = f32[4,256,512]{2,1,0:T(8,128)S(1)} custom-call(s32[4]{0:T(128)S(1)} %compare_select_fusion.2.meta, bf16[256,512]{1,0:T(8,128)(2,1)S(1)} %collective-permute-done.3.x_ref, bf16[2,4,512,512]{3,2,1,0:T(8,128)(2,1)S(1)} %get-tuple-element.19.w_ref, f32[4,256,512]{2,1,0:T(8,128)S(1)} %get-tuple-element.20.sum_ref), custom_call_target="tpu_custom_call" | custom-call | flops 536870912 | bytes 2097152 | tf_op jit(solution)/shard_map/project_more/pallas_call | solution.py:116
  18.3 0.0 copy-start.2
  18.3 0.0 collective-permute-done.4.x_ref
  18.3 1.3 %project_last.1 = (bf16[256,512]{1,0:T(8,128)(2,1)S(1)}, bf16[256,512]{1,0:T(8,128)(2,1)S(1)}, bf16[256,512]{1,0:T(8,128)(2,1)S(1)}, bf16[256,512]{1,0:T(8,128)(2,1)S(1)}) custom-call(s32[4]{0:T(128)S(1)} %compare_select_fusion.2.meta, bf16[256,512]{1,0:T(8,128)(2,1)S(1)} %collective-permute-done.4.x_ref, ...), custom_call_target="tpu_custom_call" | custom-call | flops 536870912 | bytes 2097152 | tf_op jit(solution)/shard_map/project_last/pallas_call | solution.py:116
  19.6 1.8 %collective-permute-start.6 = (bf16[256,512]{1,0:T(8,128)(2,1)S(1)}, bf16[256,512]{1,0:T(8,128)(2,1)S(1)}, u32[]{:S(2)}, u32[]{:S(2)}) collective-permute-start(bf16[256,512]{1,0:T(8,128)(2,1)S(1)} %get-tuple-element.22), channel_id=1, source_target_pairs={{0,4},{4,0},{8,12},{12,8},{16,20},{20,16},{24,28},{28,24},{1,5},{5... | collective-permute-start | bytes 786440 | tf_op jit(solution)/shard_map/ppermute | solution.py:17
  21.4 1.6 %collective-permute-start.7 = (bf16[256,512]{1,0:T(8,128)(2,1)S(1)}, bf16[256,512]{1,0:T(8,128)(2,1)S(1)}, u32[]{:S(2)}, u32[]{:S(2)}) collective-permute-start(bf16[256,512]{1,0:T(8,128)(2,1)S(1)} %get-tuple-element.23), channel_id=1, source_target_pairs={{0,8},{4,12},{8,0},{12,4},{16,24},{20,28},{24,16},{28,20},{1,9},{5... | collective-permute-start | bytes 786440 | tf_op jit(solution)/shard_map/ppermute | solution.py:17
  23.0 0.2 collective-permute-start.8
  23.2 0.0 collective-permute-done
  23.2 0.0 copy-done.2
  23.2 1.9 %collective-permute-start.1 = (f32[2,4,256]{2,1,0:T(4,128)S(1)}, f32[2,4,256]{2,1,0:T(4,128)S(1)}, u32[]{:S(2)}, u32[]{:S(2)}) collective-permute-start(f32[2,4,256]{2,1,0:T(4,128)S(1)} %pad_maximum_fusion.2), channel_id=1, source_target_pairs={{0,8},{4,12},{8,0},{12,4},{16,24},{20,28},{24,16},{28,20},{1,9},{5... | collective-permute-start | bytes 24584 | tf_op jit(solution)/shard_map/ppermute | solution.py:17
  25.1 10.6 %collective-permute-done.1 = f32[2,4,256]{2,1,0:T(4,128)S(1)} collective-permute-done((f32[2,4,256]{2,1,0:T(4,128)S(1)}, f32[2,4,256]{2,1,0:T(4,128)S(1)}, u32[]{:S(2)}, u32[]{:S(2)}) %collective-permute-start.1) | collective-permute-done | bytes 8224 | tf_op jit(solution)/shard_map/ppermute | solution.py:17
  35.7 0.4 collective-permute-start.2
  36.0 3.4 %collective-permute-done.2 = f32[4,4,256]{2,1,0:T(4,128)S(1)} collective-permute-done((f32[4,4,256]{2,1,0:T(4,128)S(1)}, f32[4,4,256]{2,1,0:T(4,128)S(1)}, u32[]{:S(2)}, u32[]{:S(2)}) %collective-permute-start.2) | collective-permute-done | bytes 16416 | tf_op jit(solution)/shard_map/ppermute | solution.py:17
  39.4 1.6 %toeplitz.1.refs_0_ = bf16[2048,1024]{1,0:T(8,128)(2,1)S(1)} custom-call(s32[4]{0:T(128)S(1)} %compare_select_fusion.2.meta, f32[8,4,256]{2,1,0:T(4,128)S(1)} %pad_maximum_fusion.pieces_ref), custom_call_target="tpu_custom_call" | custom-call | flops 16777216 | bytes 4194304 | tf_op jit(solution)/shard_map/toeplitz/pallas_call | solution.py:169
  41.0 0.0 collective-permute-done.6.refs_2_
  41.0 0.0 collective-permute-done.7.refs_3_
  41.0 0.0 collective-permute-done.8.refs_4_
  41.0 2.3 %convolve_after.1 = (bf16[256,128]{1,0:T(8,128)(2,1)S(1)}, bf16[256,128]{1,0:T(8,128)(2,1)S(1)}, bf16[256,128]{1,0:T(8,128)(2,1)S(1)}, bf16[256,128]{1,0:T(8,128)(2,1)S(1)}) custom-call(s32[4]{0:T(128)S(1)} %compare_select_fusion.2.meta, bf16[2048,1024]{1,0:T(8,128)(2,1)S(1)} %toeplitz.1.refs_0_, bf16[256,512]{1,0:T(8,128)(2,1)S(1)} %get-tuple-element.21.refs_1_, ...), custom_call_target="tpu_custom_call" | custom-call | flops 1073741824 | bytes 4194304 | tf_op jit(solution)/shard_map/convolve_after/pallas_call | solution.py:261
  43.3 2.6 %collective-permute-start.12 = (bf16[256,128]{1,0:T(8,128)(2,1)S(1)}, bf16[256,128]{1,0:T(8,128)(2,1)S(1)}, u32[]{:S(2)}, u32[]{:S(2)}) collective-permute-start(bf16[256,128]{1,0:T(8,128)(2,1)S(1)} %get-tuple-element.29), channel_id=1, source_target_pairs={{0,16},{4,20},{8,24},{12,28},{16,0},{20,4},{24,8},{28,12},{1,17},{... | collective-permute-start | bytes 196616 | tf_op jit(solution)/shard_map/ppermute | solution.py:17
  46.0 0.1 collective-permute-start.13
  46.1 3.8 %collective-permute-start.14 = (bf16[256,128]{1,0:T(8,128)(2,1)S(1)}, bf16[256,128]{1,0:T(8,128)(2,1)S(1)}, u32[]{:S(2)}, u32[]{:S(2)}) collective-permute-start(bf16[256,128]{1,0:T(8,128)(2,1)S(1)} %get-tuple-element.31), channel_id=1, source_target_pairs={{0,24},{4,28},{8,16},{12,20},{16,8},{20,12},{24,0},{28,4},{1,25},{... | collective-permute-start | bytes 196616 | tf_op jit(solution)/shard_map/ppermute | solution.py:17
  49.9 1.2 %collective-permute-start.15 = (bf16[256,128]{1,0:T(8,128)(2,1)S(1)}, bf16[256,128]{1,0:T(8,128)(2,1)S(1)}, u32[]{:S(2)}, u32[]{:S(2)}) collective-permute-start(bf16[256,128]{1,0:T(8,128)(2,1)S(1)} %get-tuple-element.32), channel_id=1, source_target_pairs={{0,28},{4,24},{8,20},{12,16},{16,12},{20,8},{24,4},{28,0},{1,29},{... | collective-permute-start | bytes 196616 | tf_op jit(solution)/shard_map/ppermute | solution.py:17
  51.1 1.7 %convolve_own.1 = (bf16[256,128]{1,0:T(8,128)(2,1)S(1)}, bf16[256,128]{1,0:T(8,128)(2,1)S(1)}, bf16[256,128]{1,0:T(8,128)(2,1)S(1)}, bf16[256,128]{1,0:T(8,128)(2,1)S(1)}) custom-call(s32[4]{0:T(128)S(1)} %compare_select_fusion.2.meta, bf16[2048,1024]{1,0:T(8,128)(2,1)S(1)} %toeplitz.1.refs_0_, bf16[256,512]{1,0:T(8,128)(2,1)S(1)} %get-tuple-element.21.refs_1_, ...), custom_call_target="tpu_custom_call" | custom-call | flops 1073741824 | bytes 4194304 | tf_op jit(solution)/shard_map/convolve_own/pallas_call | solution.py:261
  52.8 0.1 collective-permute-start.10
  52.9 0.0 collective-permute-done.12.refs_4_
  52.9 1.8 %collective-permute-start.11 = (bf16[256,128]{1,0:T(8,128)(2,1)S(1)}, bf16[256,128]{1,0:T(8,128)(2,1)S(1)}, u32[]{:S(2)}, u32[]{:S(2)}) collective-permute-start(bf16[256,128]{1,0:T(8,128)(2,1)S(1)} %get-tuple-element.28), channel_id=1, source_target_pairs={{0,12},{4,8},{8,4},{12,0},{16,28},{20,24},{24,20},{28,16},{1,13},{... | collective-permute-start | bytes 196616 | tf_op jit(solution)/shard_map/ppermute | solution.py:17
  54.7 0.2 collective-permute-done.13.refs_5_
  54.9 1.4 %collective-permute-start.9 = (bf16[256,128]{1,0:T(8,128)(2,1)S(1)}, bf16[256,128]{1,0:T(8,128)(2,1)S(1)}, u32[]{:S(2)}, u32[]{:S(2)}) collective-permute-start(bf16[256,128]{1,0:T(8,128)(2,1)S(1)} %get-tuple-element.26), channel_id=1, source_target_pairs={{0,4},{4,0},{8,12},{12,8},{16,20},{20,16},{24,28},{28,24},{1,5},{5... | collective-permute-start | bytes 196616 | tf_op jit(solution)/shard_map/ppermute | solution.py:17
  56.4 0.0 collective-permute-done.14.refs_6_
  56.4 0.7 %collective-permute-done.15.refs_7_ = bf16[256,128]{1,0:T(8,128)(2,1)S(1)} collective-permute-done((bf16[256,128]{1,0:T(8,128)(2,1)S(1)}, bf16[256,128]{1,0:T(8,128)(2,1)S(1)}, u32[]{:S(2)}, u32[]{:S(2)}) %collective-permute-start.15) | collective-permute-done | bytes 65568 | tf_op jit(solution)/shard_map/ppermute | solution.py:17
  57.0 0.7 %collective-permute-done.10.refs_2_ = bf16[256,128]{1,0:T(8,128)(2,1)S(1)} collective-permute-done((bf16[256,128]{1,0:T(8,128)(2,1)S(1)}, bf16[256,128]{1,0:T(8,128)(2,1)S(1)}, u32[]{:S(2)}, u32[]{:S(2)}) %collective-permute-start.10) | collective-permute-done | bytes 65568 | tf_op jit(solution)/shard_map/ppermute | solution.py:17
  57.7 0.6 %collective-permute-done.11.refs_3_ = bf16[256,128]{1,0:T(8,128)(2,1)S(1)} collective-permute-done((bf16[256,128]{1,0:T(8,128)(2,1)S(1)}, bf16[256,128]{1,0:T(8,128)(2,1)S(1)}, u32[]{:S(2)}, u32[]{:S(2)}) %collective-permute-start.11) | collective-permute-done | bytes 65568 | tf_op jit(solution)/shard_map/ppermute | solution.py:17
  58.3 0.9 %collective-permute-done.9.refs_1_ = bf16[256,128]{1,0:T(8,128)(2,1)S(1)} collective-permute-done((bf16[256,128]{1,0:T(8,128)(2,1)S(1)}, bf16[256,128]{1,0:T(8,128)(2,1)S(1)}, u32[]{:S(2)}, u32[]{:S(2)}) %collective-permute-start.9) | collective-permute-done | bytes 65568 | tf_op jit(solution)/shard_map/ppermute | solution.py:17
  59.2 1.3 %finish.1 = bf16[256,512]{1,0:T(8,128)(2,1)} custom-call(s32[4]{0:T(128)S(1)} %compare_select_fusion.2.meta, bf16[256,128]{1,0:T(8,128)(2,1)S(1)} %get-tuple-element.25.refs_0_, bf16[256,128]{1,0:T(8,128)(2,1)S(1)} %collective-permute-done.9.refs_1_, bf16[256,128]{1,0:T(8,128)(2,1)S(1)} %collective-permute-done.10.refs_2_, ...), custom_call_target="tpu_custom_call" | custom-call | tf_op jit(solution)/shard_map/finish/pallas_call | solution.py:297
  (4 shorter events, 0.0 us)
Async XLA Ops:
  0.0 9.5 %collective-permute-start.3 = (bf16[256,512]{1,0:T(8,128)(2,1)}, bf16[256,512]{1,0:T(8,128)(2,1)S(1)}, u32[]{:S(2)}, u32[]{:S(2)}) collective-permute-start(bf16[256,512]{1,0:T(8,128)(2,1)} %refs_0_.1), channel_id=1, source_target_pairs={{0,2},{1,3},{2,0},{3,1},{4,6},{5,7},{6,4},{7,5},{8,10},{9,11},{10,... | collective-permute-start | bytes 786440 | tf_op jit(solution)/shard_map/ppermute | solution.py:17
  3.0 6.5 %collective-permute-start.5 = (bf16[256,512]{1,0:T(8,128)(2,1)}, bf16[256,512]{1,0:T(8,128)(2,1)S(1)}, u32[]{:S(2)}, u32[]{:S(2)}) collective-permute-start(bf16[256,512]{1,0:T(8,128)(2,1)} %refs_0_.1), channel_id=1, source_target_pairs={{0,1},{1,0},{2,3},{3,2},{4,5},{5,4},{6,7},{7,6},{8,9},{9,8},{10,11... | collective-permute-start | bytes 786440 | tf_op jit(solution)/shard_map/ppermute | solution.py:17
  3.0 20.2 %collective-permute-start = (f32[1,4,256]{2,1,0:T(4,128)}, f32[1,4,256]{2,1,0:T(4,128)S(1)}, u32[]{:S(2)}, u32[]{:S(2)}) collective-permute-start(f32[1,4,256]{2,1,0:T(4,128)} %bitcast.1), channel_id=1, source_target_pairs={{0,16},{4,20},{8,24},{12,28},{16,0},{20,4},{24,8},{28,12},{1,17},{... | collective-permute-start | bytes 12296 | tf_op jit(solution)/shard_map/ppermute | solution.py:17
  9.5 8.8 %collective-permute-start.4 = (bf16[256,512]{1,0:T(8,128)(2,1)S(1)}, bf16[256,512]{1,0:T(8,128)(2,1)S(1)}, u32[]{:S(2)}, u32[]{:S(2)}) collective-permute-start(bf16[256,512]{1,0:T(8,128)(2,1)S(1)} %collective-permute-done.3.x_ref), channel_id=1, source_target_pairs={{0,1},{1,0},{2,3},{3,2},{4,5},{5,4},{6,7},{7,6},{8,9},{9,8},{10,11... | collective-permute-start | bytes 786440 | tf_op jit(solution)/shard_map/ppermute | solution.py:17
  9.5 3.4 %copy-start = (bf16[4,2048,512]{2,1,0:T(8,128)(2,1)S(1)}, bf16[4,2048,512]{2,1,0:T(8,128)(2,1)}, u32[]{:S(2)}) copy-start(bf16[4,2048,512]{2,1,0:T(8,128)(2,1)} %refs_2_.1) | copy-start | bytes 25165828
  12.9 0.9 %copy-start.1 = (bf16[256,512]{1,0:T(8,128)(2,1)S(1)}, bf16[256,512]{1,0:T(8,128)(2,1)}, u32[]{:S(2)}) copy-start(bf16[256,512]{1,0:T(8,128)(2,1)} %refs_0_.1) | copy-start | bytes 786436
  18.3 4.9 %copy-start.2 = (f32[4,256]{1,0:T(4,128)S(1)}, f32[4,256]{1,0:T(4,128)}, u32[]{:S(2)}) copy-start(f32[4,256]{1,0:T(4,128)} %param.5) | copy-start | bytes 12292
  19.6 21.4 %collective-permute-start.6 = (bf16[256,512]{1,0:T(8,128)(2,1)S(1)}, bf16[256,512]{1,0:T(8,128)(2,1)S(1)}, u32[]{:S(2)}, u32[]{:S(2)}) collective-permute-start(bf16[256,512]{1,0:T(8,128)(2,1)S(1)} %get-tuple-element.22), channel_id=1, source_target_pairs={{0,4},{4,0},{8,12},{12,8},{16,20},{20,16},{24,28},{28,24},{1,5},{5... | collective-permute-start | bytes 786440 | tf_op jit(solution)/shard_map/ppermute | solution.py:17
  21.4 19.6 %collective-permute-start.7 = (bf16[256,512]{1,0:T(8,128)(2,1)S(1)}, bf16[256,512]{1,0:T(8,128)(2,1)S(1)}, u32[]{:S(2)}, u32[]{:S(2)}) collective-permute-start(bf16[256,512]{1,0:T(8,128)(2,1)S(1)} %get-tuple-element.23), channel_id=1, source_target_pairs={{0,8},{4,12},{8,0},{12,4},{16,24},{20,28},{24,16},{28,20},{1,9},{5... | collective-permute-start | bytes 786440 | tf_op jit(solution)/shard_map/ppermute | solution.py:17
  23.0 18.0 %collective-permute-start.8 = (bf16[256,512]{1,0:T(8,128)(2,1)S(1)}, bf16[256,512]{1,0:T(8,128)(2,1)S(1)}, u32[]{:S(2)}, u32[]{:S(2)}) collective-permute-start(bf16[256,512]{1,0:T(8,128)(2,1)S(1)} %get-tuple-element.24), channel_id=1, source_target_pairs={{0,12},{4,8},{8,4},{12,0},{16,28},{20,24},{24,20},{28,16},{1,13},{... | collective-permute-start | bytes 786440 | tf_op jit(solution)/shard_map/ppermute | solution.py:17
  23.2 12.5 %collective-permute-start.1 = (f32[2,4,256]{2,1,0:T(4,128)S(1)}, f32[2,4,256]{2,1,0:T(4,128)S(1)}, u32[]{:S(2)}, u32[]{:S(2)}) collective-permute-start(f32[2,4,256]{2,1,0:T(4,128)S(1)} %pad_maximum_fusion.2), channel_id=1, source_target_pairs={{0,8},{4,12},{8,0},{12,4},{16,24},{20,28},{24,16},{28,20},{1,9},{5... | collective-permute-start | bytes 24584 | tf_op jit(solution)/shard_map/ppermute | solution.py:17
  35.7 3.7 %collective-permute-start.2 = (f32[4,4,256]{2,1,0:T(4,128)S(1)}, f32[4,4,256]{2,1,0:T(4,128)S(1)}, u32[]{:S(2)}, u32[]{:S(2)}) collective-permute-start(f32[4,4,256]{2,1,0:T(4,128)S(1)} %pad_maximum_fusion.1), channel_id=1, source_target_pairs={{0,4},{4,0},{8,12},{12,8},{16,20},{20,16},{24,28},{28,24},{1,5},{5... | collective-permute-start | bytes 49160 | tf_op jit(solution)/shard_map/ppermute | solution.py:17
  43.3 9.5 %collective-permute-start.12 = (bf16[256,128]{1,0:T(8,128)(2,1)S(1)}, bf16[256,128]{1,0:T(8,128)(2,1)S(1)}, u32[]{:S(2)}, u32[]{:S(2)}) collective-permute-start(bf16[256,128]{1,0:T(8,128)(2,1)S(1)} %get-tuple-element.29), channel_id=1, source_target_pairs={{0,16},{4,20},{8,24},{12,28},{16,0},{20,4},{24,8},{28,12},{1,17},{... | collective-permute-start | bytes 196616 | tf_op jit(solution)/shard_map/ppermute | solution.py:17
  46.0 9.0 %collective-permute-start.13 = (bf16[256,128]{1,0:T(8,128)(2,1)S(1)}, bf16[256,128]{1,0:T(8,128)(2,1)S(1)}, u32[]{:S(2)}, u32[]{:S(2)}) collective-permute-start(bf16[256,128]{1,0:T(8,128)(2,1)S(1)} %get-tuple-element.30), channel_id=1, source_target_pairs={{0,20},{4,16},{8,28},{12,24},{16,4},{20,0},{24,12},{28,8},{1,21},{... | collective-permute-start | bytes 196616 | tf_op jit(solution)/shard_map/ppermute | solution.py:17
  46.1 10.2 %collective-permute-start.14 = (bf16[256,128]{1,0:T(8,128)(2,1)S(1)}, bf16[256,128]{1,0:T(8,128)(2,1)S(1)}, u32[]{:S(2)}, u32[]{:S(2)}) collective-permute-start(bf16[256,128]{1,0:T(8,128)(2,1)S(1)} %get-tuple-element.31), channel_id=1, source_target_pairs={{0,24},{4,28},{8,16},{12,20},{16,8},{20,12},{24,0},{28,4},{1,25},{... | collective-permute-start | bytes 196616 | tf_op jit(solution)/shard_map/ppermute | solution.py:17
  49.9 7.2 %collective-permute-start.15 = (bf16[256,128]{1,0:T(8,128)(2,1)S(1)}, bf16[256,128]{1,0:T(8,128)(2,1)S(1)}, u32[]{:S(2)}, u32[]{:S(2)}) collective-permute-start(bf16[256,128]{1,0:T(8,128)(2,1)S(1)} %get-tuple-element.32), channel_id=1, source_target_pairs={{0,28},{4,24},{8,20},{12,16},{16,12},{20,8},{24,4},{28,0},{1,29},{... | collective-permute-start | bytes 196616 | tf_op jit(solution)/shard_map/ppermute | solution.py:17
  52.8 4.9 %collective-permute-start.10 = (bf16[256,128]{1,0:T(8,128)(2,1)S(1)}, bf16[256,128]{1,0:T(8,128)(2,1)S(1)}, u32[]{:S(2)}, u32[]{:S(2)}) collective-permute-start(bf16[256,128]{1,0:T(8,128)(2,1)S(1)} %get-tuple-element.27), channel_id=1, source_target_pairs={{0,8},{4,12},{8,0},{12,4},{16,24},{20,28},{24,16},{28,20},{1,9},{5... | collective-permute-start | bytes 196616 | tf_op jit(solution)/shard_map/ppermute | solution.py:17
  52.9 5.4 %collective-permute-start.11 = (bf16[256,128]{1,0:T(8,128)(2,1)S(1)}, bf16[256,128]{1,0:T(8,128)(2,1)S(1)}, u32[]{:S(2)}, u32[]{:S(2)}) collective-permute-start(bf16[256,128]{1,0:T(8,128)(2,1)S(1)} %get-tuple-element.28), channel_id=1, source_target_pairs={{0,12},{4,8},{8,4},{12,0},{16,28},{20,24},{24,20},{28,16},{1,13},{... | collective-permute-start | bytes 196616 | tf_op jit(solution)/shard_map/ppermute | solution.py:17
  54.9 4.3 %collective-permute-start.9 = (bf16[256,128]{1,0:T(8,128)(2,1)S(1)}, bf16[256,128]{1,0:T(8,128)(2,1)S(1)}, u32[]{:S(2)}, u32[]{:S(2)}) collective-permute-start(bf16[256,128]{1,0:T(8,128)(2,1)S(1)} %get-tuple-element.26), channel_id=1, source_target_pairs={{0,4},{4,0},{8,12},{12,8},{16,20},{20,16},{24,28},{28,24},{1,5},{5... | collective-permute-start | bytes 196616 | tf_op jit(solution)/shard_map/ppermute | solution.py:17

commit v2 on v1

v2 whole, which is shorter than its diff:
```python
import functools

import jax
import jax.numpy as jnp
from jax import lax
from jax.experimental import pallas as pl
from jax.experimental.pallas import tpu as pltpu
from jax.sharding import PartitionSpec as P


f32 = jnp.float32
bf16 = jnp.bfloat16
LANES = 128


def swap(value, axis, mask):
    return lax.ppermute(value, axis, [(i, i ^ mask) for i in range(lax.axis_size(axis))])


def advance(value, axis, mask, group):
    pairs = [(i, i ^ mask) for i in range(lax.axis_size(axis))]
    return lax.ppermute(value, axis, [(i, j) for i, j in pairs if i // group < j // group])


def params(mib, axes=1):
    return pltpu.CompilerParams(
        dimension_semantics=("arbitrary",) * axes if axes else None,
        vmem_limit_bytes=mib * 1024 * 1024,
    )


def columns_of(w, place, group, targets):
    sub = w.shape[1] // group
    return jnp.concatenate(
        [w[:, pl.ds(pl.multiple_of((place ^ m) * sub, sub), sub)] for m in targets], axis=1
    )


def project_first_body(meta, mine_ref, w_ref, *refs, group, targets):
    sum_refs, (ahead_ref, mine, held, sems, sem) = refs[:-5], refs[-5:]
    depth = mine_ref.shape[1]
    count = w_ref.shape[0]
    own = pltpu.make_async_copy(mine_ref, mine, sem)
    own.start()

    def fetch(m, k):
        rows = pl.ds(pl.multiple_of((meta[0] ^ m) * depth, depth), depth)
        target = ahead_ref.at[m - 1, k] if m else held.at[k]
        return pltpu.make_async_copy(w_ref.at[k, rows, :], target, sems.at[m, k])

    copies = [[fetch(m, k) for k in range(count)] for m in range(sems.shape[0])]
    for copy in copies[0] + copies[1]:
        copy.start()
    own.wait()
    for k in range(count):
        copies[0][k].wait()
        for later in copies[2:]:
            later[k].start()
        for sum_ref, places in zip(sum_refs, targets, strict=True):
            sum_ref[k] = jnp.dot(
                mine[...],
                columns_of(held.at[k], meta[1], group, places),
                preferred_element_type=f32,
            )
    for copy in [copy for later in copies[1:] for copy in later]:
        copy.wait()


def project_first(meta, mine, weights, chan, group, targets):
    tokens, depth = mine.shape
    count, _, width = weights.shape
    sub = width // group
    vmem, hbm = pl.BlockSpec(memory_space=pltpu.VMEM), pl.BlockSpec(memory_space=pltpu.HBM)
    return pl.pallas_call(
        functools.partial(project_first_body, group=group, targets=targets),
        in_specs=[pl.BlockSpec(memory_space=pltpu.SMEM), hbm, hbm],
        out_specs=[vmem] * (len(targets) + 1),
        scratch_shapes=[
            pltpu.VMEM((tokens, depth), bf16),
            pltpu.VMEM((count, depth, width), bf16),
            pltpu.SemaphoreType.DMA((chan, count)),
            pltpu.SemaphoreType.DMA,
        ],
        out_shape=[
            jax.ShapeDtypeStruct((count, tokens, len(places) * sub), f32) for places in targets
        ]
        + [jax.ShapeDtypeStruct((chan - 1, count, depth, width), bf16)],
        compiler_params=params(32, 0),
        cost_estimate=pl.CostEstimate(
            flops=2 * tokens * depth * width * count,
            bytes_accessed=2 * weights.size,
            transcendentals=0,
        ),
        name="project_first",
    )(meta, pltpu.with_memory_space_constraint(mine, pltpu.HBM), weights)


def project_body(meta, *refs, blocks, group, places, last, riders):
    x_refs, (w_ref, before_ref) = refs[: len(blocks)], refs[len(blocks) : len(blocks) + 2]
    out_refs = refs[len(blocks) + 2 :]
    count, tokens, _ = before_ref.shape
    sub = w_ref.shape[3] // group
    if riders:
        pieces_ref, out_refs = out_refs[0], out_refs[1:]
        pieces = jnp.concatenate([pieces_ref[i] for i in range(pieces_ref.shape[0])])
        out_refs[0][tokens:, :] = jnp.zeros((pieces.shape[0], out_refs[0].shape[1]), bf16)
        out_refs[0][tokens:, 0 : pieces.shape[1]] = pieces.astype(bf16)
    x = jnp.concatenate([x_ref[...] for x_ref in x_refs], axis=1)
    for k in range(count):
        rows = [columns_of(w_ref.at[m - 1, k], meta[1], group, places) for m in blocks]
        total = before_ref[k] + jnp.dot(
            x, jnp.concatenate(rows, axis=0), preferred_element_type=f32
        )
        if last:
            for i, out_ref in enumerate(out_refs):
                out_ref[0:tokens, k * sub : (k + 1) * sub] = total[
                    :, i * sub : (i + 1) * sub
                ].astype(bf16)
        else:
            out_refs[0][k] = total


def project(meta, held, blocks, ahead, before, group, places, last, riders):
    count, tokens, columns = before.shape
    depth = ahead.shape[2]
    width = count * columns // len(places)
    vmem = pl.BlockSpec(memory_space=pltpu.VMEM)
    extra = 0 if riders is None else riders.shape[0] * riders.shape[1]
    if last:
        out_shape = [
            jax.ShapeDtypeStruct((tokens + (0 if i else extra), width), bf16)
            for i in range(len(places))
        ]
    else:
        out_shape = [jax.ShapeDtypeStruct(before.shape, f32)]
    args = [held[m] for m in blocks] + [ahead, before] + ([] if riders is None else [riders])
    return pl.pallas_call(
        functools.partial(
            project_body,
            blocks=blocks,
            group=group,
            places=places,
            last=last,
            riders=riders is not None,
        ),
        in_specs=[pl.BlockSpec(memory_space=pltpu.SMEM)] + [vmem] * len(args),
        out_specs=[vmem] * len(out_shape),
        out_shape=out_shape,
        compiler_params=params(32, 0),
        cost_estimate=pl.CostEstimate(
            flops=2 * tokens * depth * len(blocks) * columns * count,
            bytes_accessed=2 * depth * len(blocks) * columns * count,
            transcendentals=0,
        ),
    )(meta, *args)


def toeplitz_body(meta, pieces_ref, other_ref, out_ref, row, *, order, group):
    count, width = pieces_ref.shape[1:]
    tokens = other_ref.shape[0] - pieces_ref.shape[0] * count
    length = len(order) * width
    step = pl.program_id(0)

    @pl.when(step == 0)
    def _():
        row[:, pl.ds(length, width)] = jnp.zeros((row.shape[0], width), f32)
        across = lax.broadcasted_iota(jnp.int32, (width, width), 0)
        along = lax.broadcasted_iota(jnp.int32, (width, width), 1)
        mirror = (across + along == width - 1).astype(bf16)
        pieces = jnp.concatenate([pieces_ref[i] for i in range(pieces_ref.shape[0])])
        pieces = jnp.concatenate([pieces.astype(bf16), other_ref[tokens:, 0:width]])
        turned = jnp.dot(pieces, mirror, preferred_element_type=f32)
        for at, m in enumerate(order):
            start = length - width * ((meta[3] ^ m) + 1)
            row[0:count, pl.ds(pl.multiple_of(start, width), width)] = turned[
                at * count : (at + 1) * count
            ]

    span = group * width

    @pl.when(step == 0)
    def _():
        out_ref[...] = jnp.zeros(out_ref.shape, bf16)

    @pl.when(step > 0)
    def _():
        start = pl.multiple_of(length - span * step, width)
        for k in range(count):
            line = jnp.broadcast_to(
                row[k : k + 1, pl.ds(start, span + width)], (LANES, span + width)
            )
            turned = pltpu.roll(line, 1, 1, stride=1, stride_axis=0).astype(bf16)
            for e in range(group):
                for h in range(width // LANES):
                    at = span - width * e - LANES * h
                    out_ref[
                        e * width + h * LANES : e * width + (h + 1) * LANES,
                        k * width : (k + 1) * width,
                    ] = turned[:, at : at + width]


def toeplitz(meta, pieces, other, order, group):
    _, count, width = pieces.shape
    blocks = len(order)
    rows, columns = group * width, count * width
    return pl.pallas_call(
        functools.partial(toeplitz_body, order=order, group=group),
        grid_spec=pltpu.PrefetchScalarGridSpec(
            num_scalar_prefetch=1,
            grid=(blocks // group + 1,),
            in_specs=[pl.BlockSpec(memory_space=pltpu.VMEM)] * 2,
            out_specs=pl.BlockSpec((rows, columns), lambda i, meta: (i, 0)),
            scratch_shapes=[pltpu.VMEM((8, (blocks + 1) * width), f32)],
        ),
        out_shape=jax.ShapeDtypeStruct(((blocks + group) * width, columns), bf16),
        compiler_params=params(16),
        cost_estimate=pl.CostEstimate(
            flops=blocks * width * columns * 8,
            bytes_accessed=2 * blocks * width * columns,
            transcendentals=0,
        ),
        name="toeplitz",
    )(meta, pieces, other)


def place_parts(held, p_refs, places, sub, width):
    for p_ref, place in zip(p_refs, places, strict=True):
        at = pl.multiple_of(place * sub, sub)
        for k in range(p_ref.shape[1] // sub):
            held[k * width : (k + 1) * width, pl.ds(at, sub)] = p_ref[0:width, k * sub : (k + 1) * sub]


def pair_sums(rows, group, width, sub):
    return [
        rows[(r + 1) * width : (r + 2) * width, :sub] + rows[r * width : (r + 1) * width, sub:]
        for r in range(group)
    ]


def store_parts(out_refs, placed, sums, place):
    for r, value in enumerate(sums):
        placed[place ^ r] = value.astype(bf16)
    for m, out_ref in enumerate(out_refs):
        out_ref[...] = placed[m]


def convolve_pair_body(meta, table_ref, *refs, at, ahead, group, sub, last):
    p_refs, refs = refs[:2], refs[2:]
    width = p_refs[0].shape[0]
    if last:
        sum_refs, out_refs, (held, placed) = refs[:1], refs[1:-2], refs[-2:]
    else:
        sum_refs, out_refs, (held,) = (), refs[:-1], refs[-1:]
    place = meta[1]
    place_parts(held, p_refs, [place & 1, 1 - (place & 1)], sub, width)
    for i, far in enumerate(ahead):
        start = (far + 1) * group - 1 - 2 * ((place // 2) ^ at)
        rows = table_ref[pl.ds(pl.multiple_of(start * width, width), (group + 1) * width), :]
        sums = pair_sums(
            jnp.dot(rows, held[...], preferred_element_type=f32), group, width, sub
        )
        if last:
            sums = [value + sum_refs[0][r] for r, value in enumerate(sums)]
            store_parts(out_refs, placed, sums, place)
        else:
            for r, value in enumerate(sums):
                out_refs[i][r] = value


def convolve_pair(meta, table, parts, before, at, ahead, group):
    width = parts[0].shape[0]
    columns = table.shape[1]
    sub = parts[0].shape[1] * width // columns
    last = before is not None
    vmem = pl.BlockSpec(memory_space=pltpu.VMEM)
    if last:
        out_shape = [jax.ShapeDtypeStruct((width, sub), bf16)] * group
        scratch = [pltpu.VMEM((group, width, sub), bf16)]
    else:
        out_shape = [jax.ShapeDtypeStruct((group, width, sub), f32)] * len(ahead)
        scratch = []
    args = [table, *parts] + ([before] if last else [])
    return pl.pallas_call(
        functools.partial(
            convolve_pair_body, at=at, ahead=ahead, group=group, sub=sub, last=last
        ),
        in_specs=[pl.BlockSpec(memory_space=pltpu.SMEM)] + [vmem] * len(args),
        out_specs=[vmem] * len(out_shape),
        out_shape=out_shape,
        scratch_shapes=[pltpu.VMEM((columns, 2 * sub), bf16), *scratch],
        compiler_params=params(32, 0),
        cost_estimate=pl.CostEstimate(
            flops=4 * len(ahead) * (group + 1) * width * columns * sub,
            bytes_accessed=2 * width * columns,
            transcendentals=0,
        ),
    )(meta, *args)


def convolve_all_body(meta, low_ref, high_ref, *refs, group, sub):
    p_refs, out_refs, (held, placed) = refs[:group], refs[group : 2 * group], refs[2 * group :]
    width = p_refs[0].shape[0]

    @pl.when(pl.program_id(0) == 0)
    def _():
        place_parts(held, p_refs, [meta[1] ^ m for m in range(group)], sub, width)

    sums = None
    for at in range(0, group, 2):
        side = held[:, at * sub : (at + 2) * sub]
        split = (group - 1 - at) * width
        rows = jnp.concatenate(
            [
                jnp.dot(low_ref[split:, :], side, preferred_element_type=f32),
                jnp.dot(high_ref[: (group - at) * width, :], side, preferred_element_type=f32),
            ]
        )
        more = pair_sums(rows, group, width, sub)
        sums = more if sums is None else [a + b for a, b in zip(sums, more, strict=True)]
    store_parts(out_refs, placed, sums, meta[1])


def convolve_all(meta, table, parts, group):
    width = parts[0].shape[0]
    columns = table.shape[1]
    sub = parts[0].shape[1] * width // columns
    rows = group * width
    steps = table.shape[0] // rows - 1
    return pl.pallas_call(
        functools.partial(convolve_all_body, group=group, sub=sub),
        grid_spec=pltpu.PrefetchScalarGridSpec(
            num_scalar_prefetch=1,
            grid=(steps,),
            in_specs=[
                pl.BlockSpec((rows, columns), lambda i, meta: (i, 0)),
                pl.BlockSpec((rows, columns), lambda i, meta: (i + 1, 0)),
            ]
            + [pl.BlockSpec(part.shape, lambda i, meta: (0, 0)) for part in parts],
            out_specs=[pl.BlockSpec((width, sub), lambda i, meta: (i, 0))] * group,
            scratch_shapes=[
                pltpu.VMEM((columns, group * sub), bf16),
                pltpu.VMEM((group, width, sub), bf16),
            ],
        ),
        out_shape=[jax.ShapeDtypeStruct((steps * width, sub), bf16)] * group,
        compiler_params=params(32),
        cost_estimate=pl.CostEstimate(
            flops=2 * steps * rows * columns * group * sub,
            bytes_accessed=2 * steps * rows * columns,
            transcendentals=0,
        ),
        name="convolve_all",
    )(meta, table, table, *parts)


def finish_body(meta, *refs, group):
    parts, out_ref = refs[:-1], refs[-1]
    sub = out_ref.shape[1] // group
    place = meta[1]
    for m in range(group):
        value = parts[m][...].astype(f32)
        for far in range(1, len(parts) // group):
            value = value + parts[far * group + m][...].astype(f32)
        at = pl.multiple_of((place ^ m) * sub, sub)
        out_ref[:, pl.ds(at, sub)] = value.astype(bf16)


def finish(meta, parts, group):
    width, sub = parts[0].shape
    shape = (width, sub * group)
    return pl.pallas_call(
        functools.partial(finish_body, group=group),
        in_specs=[pl.BlockSpec(memory_space=pltpu.SMEM)]
        + [pl.BlockSpec(memory_space=pltpu.VMEM)] * len(parts),
        out_specs=pl.BlockSpec(memory_space=pltpu.VMEM),
        out_shape=jax.ShapeDtypeStruct(shape, bf16),
        compiler_params=params(24, 0),
        name="finish",
    )(meta, *parts)


def local(inputs, weights, filters):
    seq, chan = lax.axis_size("seq"), lax.axis_size("chan")
    group = min(4, seq)
    groups = seq // group
    width = inputs.shape[0]
    at_seq, at_chan = lax.axis_index("seq"), lax.axis_index("chan")
    lane = jnp.arange(4)
    meta = jnp.where(
        lane == 0,
        at_chan,
        jnp.where(lane == 1, at_seq % group, jnp.where(lane == 2, at_seq // group, at_seq)),
    ).astype(jnp.int32)

    held = {0: inputs}
    held[2] = swap(inputs, "chan", 2)
    held[1] = swap(inputs, "chan", 1)
    held[3] = swap(held[2], "chan", 1)

    weights = pltpu.with_memory_space_constraint(weights, pltpu.HBM)
    pieces = filters[None]
    order = [0]
    bit = seq // 2
    while bit > 1:
        pieces = jnp.concatenate([pieces, swap(pieces, "seq", bit)])
        order += [m ^ bit for m in order]
        bit //= 2
    order += [m ^ 1 for m in order]

    soon = [m for m in range(1, group) if m < 3]
    late = [m for m in range(group) if m not in soon]
    to_soon, to_late, ahead = project_first(meta, inputs, weights, chan, group, [soon, late])
    (to_soon,) = project(meta, held, [1, 2], ahead, to_soon, group, soon, False, None)
    mine = project(meta, held, [3], ahead, to_soon, group, soon, True, pieces)
    mine += project(meta, held, [1, 2, 3], ahead, to_late, group, late, True, None)
    mine = dict(zip(soon + late, mine, strict=True))
    parts = {0: mine[0]}
    for m in range(1, group):
        parts[m] = swap(mine[m], "seq", m)
    parts = [parts[m] for m in range(group)]
    table = toeplitz(meta, pieces, parts[1], order, group)

    if groups == 2 and group == 4:
        sides = [[parts[0], parts[1]], [parts[2], parts[3]]]
        own, after = convolve_pair(meta, table, sides[0], None, 0, (0, 1), group)
        after = convolve_pair(meta, table, sides[1], after, 1, (1,), group)
        own = convolve_pair(meta, table, sides[1], own, 1, (0,), group)
        ahead = {1: after}
    else:
        every = convolve_all(meta, table, [parts[m] for m in range(group)], group)
        own = [every[m][:width] for m in range(group)]
        here = at_seq // group
        ahead = {
            far: [
                lax.dynamic_slice_in_dim(
                    every[m], jnp.maximum((here ^ far) - here, 0) * width, width, 0
                )
                for m in range(group)
            ]
            for far in range(1, groups)
        }
    pieces = [own[0]]
    for m in range(1, group):
        pieces.append(swap(own[m], "seq", m))
    for far in range(1, groups):
        for m in range(group):
            pieces.append(advance(ahead[far][m], "seq", far * group + m, group))
    return finish(meta, pieces, group)


def solution(mesh):
    in_specs = (P("seq", "chan"), P(None, None, "chan"), P(None, "seq"))
    out_specs = P("seq", "chan")
    return jax.shard_map(local, mesh=mesh, in_specs=in_specs, out_specs=out_specs, check_vma=False)
```

time: 60.7 us -> 58 us (0.956)
  waiting for transfers between devices: 21 us -> 16 us
  local copies, waits for them, and re-layouts: 4.33 us -> 0.01 us
  Pallas kernels: 12.7 us -> 17 us
  starting transfers between devices: 22.4 us -> 23.9 us
  other arithmetic: 0.02 us -> 0.7 us
    ppermute x0 -> x4, starting transfers between devices: none -> 9.31 us  [advance(): lax.ppermute(value, axis, [(i, j) for i, j in pairs if i // group < j //...]
    ppermute x16 -> x11, starting transfers between devices: 22.4 us -> 14.5 us  [swap(): lax.ppermute(value, axis, [(i, i ^ mask) for i in range(lax.axis_size(axi...]
    ppermute x16 -> x11, waiting for transfers between devices: 21 us -> 16 us  [swap(): lax.ppermute(value, axis, [(i, i ^ mask) for i in range(lax.axis_size(axi...]
    unnamed x6 -> x2, local copies, waits for them, and re-layouts: 4.33 us -> 0.01 us
    pallas_call x5 -> x7, Pallas kernels: 9.77 us -> 14.1 us  [the longest x3 5.11 us: convolve_pair(): pl.pallas_call(functools.partial(convolve_pair_body, at=at, ahead=ahead,...]
    concatenate x3 -> x2, other arithmetic: 0.02 us -> 0.7 us  [local(): pieces = jnp.concatenate([pieces, swap(pieces, 'seq', bit)])]
  transfers between devices with their start and end apart: 16 -> 15, of which waited for: 8 -> 5; matrix products, arithmetic and copies ran while one was open for 0% -> 1% of each run, Pallas kernels for 15% -> 23%
where the time goes in v2:
time: 58 us; the launch traced here: 57.7 us
  starting transfers between devices  23.9 us (41%)
  Pallas kernels  17 us (29%)
  waiting for transfers between devices  16 us (28%)
  other arithmetic  0.7 us (1%)
    ppermute x11, waiting for transfers between devices, swap(): lax.ppermute(value, axis, [(i, i ^ mask) for i in range(lax.axis_size(axi...  16 us
    ppermute x11, starting transfers between devices, swap(): lax.ppermute(value, axis, [(i, i ^ mask) for i in range(lax.axis_size(axi...  14.5 us
    ppermute x4, starting transfers between devices, advance(): lax.ppermute(value, axis, [(i, j) for i, j in pairs if i // group < j //...  9.31 us
    pallas_call x3, Pallas kernels, convolve_pair(): pl.pallas_call(functools.partial(convolve_pair_body, at=at, ahead=ahead,...  5.11 us
    pallas_call x1, Pallas kernels, project_first(): pl.pallas_call(functools.partial(project_first_body, group=group, targets...  5.09 us
    pallas_call x3, Pallas kernels, project(): pl.pallas_call(functools.partial(project_body, blocks=blocks, group=group...  3.87 us
    pallas_call x1, Pallas kernels, toeplitz(): pl.pallas_call(functools.partial(toeplitz_body, order=order, group=group)...  1.58 us
    pallas_call x1, Pallas kernels, finish(): pl.pallas_call(functools.partial(finish_body, group=group), in_specs=[pl....  1.31 us
  transfers between devices with their start and end apart: 15, of which 5 were waited for; matrix products, arithmetic and copies ran while one was open for 1% of the time, Pallas kernels for 23%

profile of v2, /device:TPU:0, one launch (start us, length us, event | category | flops | bytes accessed | tf_op | source)
XLA Modules:
  0.0 57.7 jit_solution(17363399585584421709)
XLA Ops:
  0.0 0.0 copy-start
  0.0 3.0 %collective-permute-start.2 = (bf16[256,512]{1,0:T(8,128)(2,1)}, bf16[256,512]{1,0:T(8,128)(2,1)S(1)}, u32[]{:S(2)}, u32[]{:S(2)}) collective-permute-start(bf16[256,512]{1,0:T(8,128)(2,1)} %mine_ref.1), channel_id=1, source_target_pairs={{0,2},{1,3},{2,0},{3,1},{4,6},{5,7},{6,4},{7,5},{8,10},{9,11},{10,... | collective-permute-start | bytes 786440 | tf_op jit(solution)/shard_map/ppermute | solution.py:17
  3.0 0.0 collective-permute-start.4
  3.0 2.6 %collective-permute-start = (f32[1,4,256]{2,1,0:T(4,128)}, f32[1,4,256]{2,1,0:T(4,128)S(1)}, u32[]{:S(2)}, u32[]{:S(2)}) collective-permute-start(f32[1,4,256]{2,1,0:T(4,128)} %bitcast.1), channel_id=1, source_target_pairs={{0,16},{4,20},{8,24},{12,28},{16,0},{20,4},{24,8},{28,12},{1,17},{... | collective-permute-start | bytes 12296 | tf_op jit(solution)/shard_map/ppermute | solution.py:17
  5.6 3.9 %collective-permute-done.2.refs_1_ = bf16[256,512]{1,0:T(8,128)(2,1)S(1)} collective-permute-done((bf16[256,512]{1,0:T(8,128)(2,1)}, bf16[256,512]{1,0:T(8,128)(2,1)S(1)}, u32[]{:S(2)}, u32[]{:S(2)}) %collective-permute-start.2) | collective-permute-done | bytes 262176 | tf_op jit(solution)/shard_map/ppermute | solution.py:17
  9.5 0.0 collective-permute-start.3
  9.5 0.0 collective-permute-done
  9.5 0.7 %pad_maximum_fusion.1 = f32[2,4,256]{2,1,0:T(4,128)S(1)} fusion(f32[1,4,256]{2,1,0:T(4,128)S(1)} %collective-permute-done, f32[1,4,256]{2,1,0:T(4,128)} %bitcast.2), kind=kLoop, calls=%fused_computation.1 | loop fusion | flops 2048 | bytes 16384 | tf_op jit(solution)/shard_map/concatenate | solution.py:405
  10.2 1.8 %collective-permute-start.1 = (f32[2,4,256]{2,1,0:T(4,128)S(1)}, f32[2,4,256]{2,1,0:T(4,128)S(1)}, u32[]{:S(2)}, u32[]{:S(2)}) collective-permute-start(f32[2,4,256]{2,1,0:T(4,128)S(1)} %pad_maximum_fusion.1), channel_id=1, source_target_pairs={{0,8},{4,12},{8,0},{12,4},{16,24},{20,28},{24,16},{28,20},{1,9},{5... | collective-permute-start | bytes 24584 | tf_op jit(solution)/shard_map/ppermute | solution.py:17
  12.0 5.1 %project_first.1 = (f32[4,256,256]{2,1,0:T(8,128)S(1)}, f32[4,256,256]{2,1,0:T(8,128)S(1)}, bf16[3,4,512,512]{3,2,1,0:T(8,128)(2,1)S(1)}) custom-call(s32[4]{0:T(128)S(1)} %compare_select_fusion.2.meta, bf16[256,512]{1,0:T(8,128)(2,1)} %mine_ref.1, bf16[4,2048,512]{2,1,0:T(8,128)(2,1)} %w_ref.1), custom_call_target="tpu_custom_call" | custom-call | flops 536870912 | bytes 8388608 | tf_op jit(solution)/shard_map/project_first/pallas_call | solution.py:74
  17.1 0.0 collective-permute-done.1
  17.1 0.0 copy-done
  17.1 0.0 collective-permute-done.4.refs_0_
  17.2 1.3 %shard_map.37.refs_2_ = f32[4,256,256]{2,1,0:T(8,128)S(1)} custom-call(s32[4]{0:T(128)S(1)} %compare_select_fusion.2.meta, bf16[256,512]{1,0:T(8,128)(2,1)S(1)} %collective-permute-done.4.refs_0_, bf16[256,512]{1,0:T(8,128)(2,1)S(1)} %collective-permute-done.2.refs_1_, bf16[3,4,512,512]{3,2,1,0:T(8,128)(2,1)S(1)} %get-tuple-element.22.refs_2_.refs_1_.refs_3_, ...), custom_call_target="tpu_custom_call" | custom-call | flops 536870912 | bytes 2097152 | tf_op jit(solution)/shard_map/pallas_call | solution.py:137
  18.5 0.0 collective-permute-done.3.refs_0_.refs_2_
  18.5 1.0 %shard_map.38 = (bf16[272,512]{1,0:T(8,128)(2,1)S(1)}, bf16[256,512]{1,0:T(8,128)(2,1)S(1)}) custom-call(s32[4]{0:T(128)S(1)} %compare_select_fusion.2.meta, bf16[256,512]{1,0:T(8,128)(2,1)S(1)} %collective-permute-done.3.refs_0_.refs_2_, bf16[3,4,512,512]{3,2,1,0:T(8,128)(2,1)S(1)} %get-tuple-element.22.refs_2_.refs_1_.refs_3_, ...), custom_call_target="tpu_custom_call" | custom-call | flops 268435456 | bytes 1048576 | tf_op jit(solution)/shard_map/pallas_call | solution.py:137
  19.5 1.6 %collective-permute-start.5 = (bf16[272,512]{1,0:T(8,128)(2,1)S(1)}, bf16[272,512]{1,0:T(8,128)(2,1)S(1)}, u32[]{:S(2)}, u32[]{:S(2)}) collective-permute-start(bf16[272,512]{1,0:T(8,128)(2,1)S(1)} %get-tuple-element.24), channel_id=1, source_target_pairs={{0,4},{4,0},{8,12},{12,8},{16,20},{20,16},{24,28},{28,24},{1,5},{5... | collective-permute-start | bytes 835592 | tf_op jit(solution)/shard_map/ppermute | solution.py:17
  21.1 1.6 %shard_map.39 = (bf16[256,512]{1,0:T(8,128)(2,1)S(1)}, bf16[256,512]{1,0:T(8,128)(2,1)S(1)}) custom-call(s32[4]{0:T(128)S(1)} %compare_select_fusion.2.meta, bf16[256,512]{1,0:T(8,128)(2,1)S(1)} %collective-permute-done.4.refs_0_, bf16[256,512]{1,0:T(8,128)(2,1)S(1)} %collective-permute-done.2.refs_1_, ...), custom_call_target="tpu_custom_call" | custom-call | flops 805306368 | bytes 3145728 | tf_op jit(solution)/shard_map/pallas_call | solution.py:137
  22.6 0.2 collective-permute-start.7
  22.9 1.8 %collective-permute-start.6 = (bf16[256,512]{1,0:T(8,128)(2,1)S(1)}, bf16[256,512]{1,0:T(8,128)(2,1)S(1)}, u32[]{:S(2)}, u32[]{:S(2)}) collective-permute-start(bf16[256,512]{1,0:T(8,128)(2,1)S(1)} %get-tuple-element.25), channel_id=1, source_target_pairs={{0,8},{4,12},{8,0},{12,4},{16,24},{20,28},{24,16},{28,20},{1,9},{5... | collective-permute-start | bytes 786440 | tf_op jit(solution)/shard_map/ppermute | solution.py:17
  24.7 9.3 %collective-permute-done.5.other_ref.refs_1_ = bf16[272,512]{1,0:T(8,128)(2,1)S(1)} collective-permute-done((bf16[272,512]{1,0:T(8,128)(2,1)S(1)}, bf16[272,512]{1,0:T(8,128)(2,1)S(1)}, u32[]{:S(2)}, u32[]{:S(2)}) %collective-permute-start.5) | collective-permute-done | bytes 278560 | tf_op jit(solution)/shard_map/ppermute | solution.py:17
  33.9 1.6 %toeplitz.1.table_ref = bf16[3072,1024]{1,0:T(8,128)(2,1)S(1)} custom-call(s32[4]{0:T(128)S(1)} %compare_select_fusion.2.meta, f32[4,4,256]{2,1,0:T(4,128)S(1)} %pad_maximum_fusion.refs_3_.pieces_ref, bf16[272,512]{1,0:T(8,128)(2,1)S(1)} %collective-permute-done.5.other_ref.refs_1_), custom_call_target="tpu_custom_call" | custom-call | flops 16777216 | bytes 4194304 | tf_op jit(solution)/shard_map/toeplitz/pallas_call | solution.py:206
  35.5 2.1 %shard_map.40 = (f32[4,256,128]{2,1,0:T(8,128)S(1)}, f32[4,256,128]{2,1,0:T(8,128)S(1)}) custom-call(s32[4]{0:T(128)S(1)} %compare_select_fusion.2.meta, bf16[3072,1024]{1,0:T(8,128)(2,1)S(1)} %toeplitz.1.table_ref, bf16[256,512]{1,0:T(8,128)(2,1)S(1)} %get-tuple-element.28.refs_0_, bf16[272,512]{1,0:T(8,128)(2,1)S(1)} %collective-permute-done.5.other_ref.refs_1_), custom_call_target="tpu_custom_call" | custom-call | flops 1342177280 | bytes 524288 | tf_op jit(solution)/shard_map/pallas_call | solution.py:283
  37.7 0.0 collective-permute-done.7.refs_1_
  37.7 0.0 collective-permute-done.6.refs_0_
  37.7 1.5 %shard_map.42 = (bf16[256,128]{1,0:T(8,128)(2,1)S(1)}, bf16[256,128]{1,0:T(8,128)(2,1)S(1)}, bf16[256,128]{1,0:T(8,128)(2,1)S(1)}, bf16[256,128]{1,0:T(8,128)(2,1)S(1)}) custom-call(s32[4]{0:T(128)S(1)} %compare_select_fusion.2.meta, bf16[3072,1024]{1,0:T(8,128)(2,1)S(1)} %toeplitz.1.table_ref, bf16[256,512]{1,0:T(8,128)(2,1)S(1)} %collective-permute-done.6.refs_0_, ...), custom_call_target="tpu_custom_call" | custom-call | flops 671088640 | bytes 524288 | tf_op jit(solution)/shard_map/pallas_call | solution.py:283
  39.2 4.5 %collective-permute-start.11 = (bf16[256,128]{1,0:T(8,128)(2,1)S(1)}, bf16[256,128]{1,0:T(8,128)(2,1)S(1)}, u32[]{:S(2)}, u32[]{:S(2)}) collective-permute-start(bf16[256,128]{1,0:T(8,128)(2,1)S(1)} %get-tuple-element.35), channel_id=1, source_target_pairs={{0,16},{4,20},{8,24},{12,28},{1,17},{5,21},{9,25},{13,29},{2,18},{... | collective-permute-start | bytes 196616 | tf_op jit(solution)/shard_map/ppermute | solution.py:22
  43.7 2.2 %collective-permute-start.12 = (bf16[256,128]{1,0:T(8,128)(2,1)S(1)}, bf16[256,128]{1,0:T(8,128)(2,1)S(1)}, u32[]{:S(2)}, u32[]{:S(2)}) collective-permute-start(bf16[256,128]{1,0:T(8,128)(2,1)S(1)} %get-tuple-element.36), channel_id=1, source_target_pairs={{0,20},{4,16},{8,28},{12,24},{1,21},{5,17},{9,29},{13,25},{2,22},{... | collective-permute-start | bytes 196616 | tf_op jit(solution)/shard_map/ppermute | solution.py:22
  45.9 1.3 %collective-permute-start.13 = (bf16[256,128]{1,0:T(8,128)(2,1)S(1)}, bf16[256,128]{1,0:T(8,128)(2,1)S(1)}, u32[]{:S(2)}, u32[]{:S(2)}) collective-permute-start(bf16[256,128]{1,0:T(8,128)(2,1)S(1)} %get-tuple-element.37), channel_id=1, source_target_pairs={{0,24},{4,28},{8,16},{12,20},{1,25},{5,29},{9,17},{13,21},{2,26},{... | collective-permute-start | bytes 196616 | tf_op jit(solution)/shard_map/ppermute | solution.py:22
  47.2 1.3 %collective-permute-start.14 = (bf16[256,128]{1,0:T(8,128)(2,1)S(1)}, bf16[256,128]{1,0:T(8,128)(2,1)S(1)}, u32[]{:S(2)}, u32[]{:S(2)}) collective-permute-start(bf16[256,128]{1,0:T(8,128)(2,1)S(1)} %get-tuple-element.38), channel_id=1, source_target_pairs={{0,28},{4,24},{8,20},{12,16},{1,29},{5,25},{9,21},{13,17},{2,30},{... | collective-permute-start | bytes 196616 | tf_op jit(solution)/shard_map/ppermute | solution.py:22
  48.5 1.5 %shard_map.41 = (bf16[256,128]{1,0:T(8,128)(2,1)S(1)}, bf16[256,128]{1,0:T(8,128)(2,1)S(1)}, bf16[256,128]{1,0:T(8,128)(2,1)S(1)}, bf16[256,128]{1,0:T(8,128)(2,1)S(1)}) custom-call(s32[4]{0:T(128)S(1)} %compare_select_fusion.2.meta, bf16[3072,1024]{1,0:T(8,128)(2,1)S(1)} %toeplitz.1.table_ref, bf16[256,512]{1,0:T(8,128)(2,1)S(1)} %collective-permute-done.6.refs_0_, ...), custom_call_target="tpu_custom_call" | custom-call | flops 671088640 | bytes 524288 | tf_op jit(solution)/shard_map/pallas_call | solution.py:283
  50.0 0.6 %collective-permute-start.10 = (bf16[256,128]{1,0:T(8,128)(2,1)S(1)}, bf16[256,128]{1,0:T(8,128)(2,1)S(1)}, u32[]{:S(2)}, u32[]{:S(2)}) collective-permute-start(bf16[256,128]{1,0:T(8,128)(2,1)S(1)} %get-tuple-element.33), channel_id=1, source_target_pairs={{0,12},{4,8},{8,4},{12,0},{16,28},{20,24},{24,20},{28,16},{1,13},{... | collective-permute-start | bytes 196616 | tf_op jit(solution)/shard_map/ppermute | solution.py:17
  50.7 0.0 collective-permute-done.11.refs_4_
  50.7 1.5 %collective-permute-start.8 = (bf16[256,128]{1,0:T(8,128)(2,1)S(1)}, bf16[256,128]{1,0:T(8,128)(2,1)S(1)}, u32[]{:S(2)}, u32[]{:S(2)}) collective-permute-start(bf16[256,128]{1,0:T(8,128)(2,1)S(1)} %get-tuple-element.31), channel_id=1, source_target_pairs={{0,4},{4,0},{8,12},{12,8},{16,20},{20,16},{24,28},{28,24},{1,5},{5... | collective-permute-start | bytes 196616 | tf_op jit(solution)/shard_map/ppermute | solution.py:17
  52.1 0.0 collective-permute-done.12.refs_5_
  52.1 1.5 %collective-permute-start.9 = (bf16[256,128]{1,0:T(8,128)(2,1)S(1)}, bf16[256,128]{1,0:T(8,128)(2,1)S(1)}, u32[]{:S(2)}, u32[]{:S(2)}) collective-permute-start(bf16[256,128]{1,0:T(8,128)(2,1)S(1)} %get-tuple-element.32), channel_id=1, source_target_pairs={{0,8},{4,12},{8,0},{12,4},{16,24},{20,28},{24,16},{28,20},{1,9},{5... | collective-permute-start | bytes 196616 | tf_op jit(solution)/shard_map/ppermute | solution.py:17
  53.6 0.0 collective-permute-done.13.refs_6_
  53.6 0.0 collective-permute-done.14.refs_7_
  53.6 1.8 %collective-permute-done.10.refs_3_ = bf16[256,128]{1,0:T(8,128)(2,1)S(1)} collective-permute-done((bf16[256,128]{1,0:T(8,128)(2,1)S(1)}, bf16[256,128]{1,0:T(8,128)(2,1)S(1)}, u32[]{:S(2)}, u32[]{:S(2)}) %collective-permute-start.10) | collective-permute-done | bytes 65568 | tf_op jit(solution)/shard_map/ppermute | solution.py:17
  55.4 0.3 collective-permute-done.8.refs_1_
  55.6 0.8 %collective-permute-done.9.refs_2_ = bf16[256,128]{1,0:T(8,128)(2,1)S(1)} collective-permute-done((bf16[256,128]{1,0:T(8,128)(2,1)S(1)}, bf16[256,128]{1,0:T(8,128)(2,1)S(1)}, u32[]{:S(2)}, u32[]{:S(2)}) %collective-permute-start.9) | collective-permute-done | bytes 65568 | tf_op jit(solution)/shard_map/ppermute | solution.py:17
  56.4 1.3 %finish.1 = bf16[256,512]{1,0:T(8,128)(2,1)} custom-call(s32[4]{0:T(128)S(1)} %compare_select_fusion.2.meta, bf16[256,128]{1,0:T(8,128)(2,1)S(1)} %get-tuple-element.30.refs_0_, bf16[256,128]{1,0:T(8,128)(2,1)S(1)} %collective-permute-done.8.refs_1_, bf16[256,128]{1,0:T(8,128)(2,1)S(1)} %collective-permute-done.9.refs_2_, ...), custom_call_target="tpu_custom_call" | custom-call | tf_op jit(solution)/shard_map/finish/pallas_call | solution.py:371
  (2 shorter events, 0.0 us)
Async XLA Ops:
  0.0 17.1 %copy-start = (f32[4,256]{1,0:T(4,128)S(1)}, f32[4,256]{1,0:T(4,128)}, u32[]{:S(2)}) copy-start(f32[4,256]{1,0:T(4,128)} %param.5) | copy-start | bytes 12292
  0.0 9.5 %collective-permute-start.2 = (bf16[256,512]{1,0:T(8,128)(2,1)}, bf16[256,512]{1,0:T(8,128)(2,1)S(1)}, u32[]{:S(2)}, u32[]{:S(2)}) collective-permute-start(bf16[256,512]{1,0:T(8,128)(2,1)} %mine_ref.1), channel_id=1, source_target_pairs={{0,2},{1,3},{2,0},{3,1},{4,6},{5,7},{6,4},{7,5},{8,10},{9,11},{10,... | collective-permute-start | bytes 786440 | tf_op jit(solution)/shard_map/ppermute | solution.py:17
  3.0 14.2 %collective-permute-start.4 = (bf16[256,512]{1,0:T(8,128)(2,1)}, bf16[256,512]{1,0:T(8,128)(2,1)S(1)}, u32[]{:S(2)}, u32[]{:S(2)}) collective-permute-start(bf16[256,512]{1,0:T(8,128)(2,1)} %mine_ref.1), channel_id=1, source_target_pairs={{0,1},{1,0},{2,3},{3,2},{4,5},{5,4},{6,7},{7,6},{8,9},{9,8},{10,11... | collective-permute-start | bytes 786440 | tf_op jit(solution)/shard_map/ppermute | solution.py:17
  3.0 6.5 %collective-permute-start = (f32[1,4,256]{2,1,0:T(4,128)}, f32[1,4,256]{2,1,0:T(4,128)S(1)}, u32[]{:S(2)}, u32[]{:S(2)}) collective-permute-start(f32[1,4,256]{2,1,0:T(4,128)} %bitcast.1), channel_id=1, source_target_pairs={{0,16},{4,20},{8,24},{12,28},{16,0},{20,4},{24,8},{28,12},{1,17},{... | collective-permute-start | bytes 12296 | tf_op jit(solution)/shard_map/ppermute | solution.py:17
  9.5 8.9 %collective-permute-start.3 = (bf16[256,512]{1,0:T(8,128)(2,1)S(1)}, bf16[256,512]{1,0:T(8,128)(2,1)S(1)}, u32[]{:S(2)}, u32[]{:S(2)}) collective-permute-start(bf16[256,512]{1,0:T(8,128)(2,1)S(1)} %collective-permute-done.2.refs_1_), channel_id=1, source_target_pairs={{0,1},{1,0},{2,3},{3,2},{4,5},{5,4},{6,7},{7,6},{8,9},{9,8},{10,11... | collective-permute-start | bytes 786440 | tf_op jit(solution)/shard_map/ppermute | solution.py:17
  10.2 6.9 %collective-permute-start.1 = (f32[2,4,256]{2,1,0:T(4,128)S(1)}, f32[2,4,256]{2,1,0:T(4,128)S(1)}, u32[]{:S(2)}, u32[]{:S(2)}) collective-permute-start(f32[2,4,256]{2,1,0:T(4,128)S(1)} %pad_maximum_fusion.1), channel_id=1, source_target_pairs={{0,8},{4,12},{8,0},{12,4},{16,24},{20,28},{24,16},{28,20},{1,9},{5... | collective-permute-start | bytes 24584 | tf_op jit(solution)/shard_map/ppermute | solution.py:17
  19.5 14.5 %collective-permute-start.5 = (bf16[272,512]{1,0:T(8,128)(2,1)S(1)}, bf16[272,512]{1,0:T(8,128)(2,1)S(1)}, u32[]{:S(2)}, u32[]{:S(2)}) collective-permute-start(bf16[272,512]{1,0:T(8,128)(2,1)S(1)} %get-tuple-element.24), channel_id=1, source_target_pairs={{0,4},{4,0},{8,12},{12,8},{16,20},{20,16},{24,28},{28,24},{1,5},{5... | collective-permute-start | bytes 835592 | tf_op jit(solution)/shard_map/ppermute | solution.py:17
  22.6 15.1 %collective-permute-start.7 = (bf16[256,512]{1,0:T(8,128)(2,1)S(1)}, bf16[256,512]{1,0:T(8,128)(2,1)S(1)}, u32[]{:S(2)}, u32[]{:S(2)}) collective-permute-start(bf16[256,512]{1,0:T(8,128)(2,1)S(1)} %get-tuple-element.27), channel_id=1, source_target_pairs={{0,12},{4,8},{8,4},{12,0},{16,28},{20,24},{24,20},{28,16},{1,13},{... | collective-permute-start | bytes 786440 | tf_op jit(solution)/shard_map/ppermute | solution.py:17
  22.9 14.8 %collective-permute-start.6 = (bf16[256,512]{1,0:T(8,128)(2,1)S(1)}, bf16[256,512]{1,0:T(8,128)(2,1)S(1)}, u32[]{:S(2)}, u32[]{:S(2)}) collective-permute-start(bf16[256,512]{1,0:T(8,128)(2,1)S(1)} %get-tuple-element.25), channel_id=1, source_target_pairs={{0,8},{4,12},{8,0},{12,4},{16,24},{20,28},{24,16},{28,20},{1,9},{5... | collective-permute-start | bytes 786440 | tf_op jit(solution)/shard_map/ppermute | solution.py:17
  39.2 11.5 %collective-permute-start.11 = (bf16[256,128]{1,0:T(8,128)(2,1)S(1)}, bf16[256,128]{1,0:T(8,128)(2,1)S(1)}, u32[]{:S(2)}, u32[]{:S(2)}) collective-permute-start(bf16[256,128]{1,0:T(8,128)(2,1)S(1)} %get-tuple-element.35), channel_id=1, source_target_pairs={{0,16},{4,20},{8,24},{12,28},{1,17},{5,21},{9,25},{13,29},{2,18},{... | collective-permute-start | bytes 196616 | tf_op jit(solution)/shard_map/ppermute | solution.py:22
  43.7 8.4 %collective-permute-start.12 = (bf16[256,128]{1,0:T(8,128)(2,1)S(1)}, bf16[256,128]{1,0:T(8,128)(2,1)S(1)}, u32[]{:S(2)}, u32[]{:S(2)}) collective-permute-start(bf16[256,128]{1,0:T(8,128)(2,1)S(1)} %get-tuple-element.36), channel_id=1, source_target_pairs={{0,20},{4,16},{8,28},{12,24},{1,21},{5,17},{9,29},{13,25},{2,22},{... | collective-permute-start | bytes 196616 | tf_op jit(solution)/shard_map/ppermute | solution.py:22
  45.9 7.7 %collective-permute-start.13 = (bf16[256,128]{1,0:T(8,128)(2,1)S(1)}, bf16[256,128]{1,0:T(8,128)(2,1)S(1)}, u32[]{:S(2)}, u32[]{:S(2)}) collective-permute-start(bf16[256,128]{1,0:T(8,128)(2,1)S(1)} %get-tuple-element.37), channel_id=1, source_target_pairs={{0,24},{4,28},{8,16},{12,20},{1,25},{5,29},{9,17},{13,21},{2,26},{... | collective-permute-start | bytes 196616 | tf_op jit(solution)/shard_map/ppermute | solution.py:22
  47.2 6.4 %collective-permute-start.14 = (bf16[256,128]{1,0:T(8,128)(2,1)S(1)}, bf16[256,128]{1,0:T(8,128)(2,1)S(1)}, u32[]{:S(2)}, u32[]{:S(2)}) collective-permute-start(bf16[256,128]{1,0:T(8,128)(2,1)S(1)} %get-tuple-element.38), channel_id=1, source_target_pairs={{0,28},{4,24},{8,20},{12,16},{1,29},{5,25},{9,21},{13,17},{2,30},{... | collective-permute-start | bytes 196616 | tf_op jit(solution)/shard_map/ppermute | solution.py:22
  50.0 5.3 %collective-permute-start.10 = (bf16[256,128]{1,0:T(8,128)(2,1)S(1)}, bf16[256,128]{1,0:T(8,128)(2,1)S(1)}, u32[]{:S(2)}, u32[]{:S(2)}) collective-permute-start(bf16[256,128]{1,0:T(8,128)(2,1)S(1)} %get-tuple-element.33), channel_id=1, source_target_pairs={{0,12},{4,8},{8,4},{12,0},{16,28},{20,24},{24,20},{28,16},{1,13},{... | collective-permute-start | bytes 196616 | tf_op jit(solution)/shard_map/ppermute | solution.py:17
  50.7 5.0 %collective-permute-start.8 = (bf16[256,128]{1,0:T(8,128)(2,1)S(1)}, bf16[256,128]{1,0:T(8,128)(2,1)S(1)}, u32[]{:S(2)}, u32[]{:S(2)}) collective-permute-start(bf16[256,128]{1,0:T(8,128)(2,1)S(1)} %get-tuple-element.31), channel_id=1, source_target_pairs={{0,4},{4,0},{8,12},{12,8},{16,20},{20,16},{24,28},{28,24},{1,5},{5... | collective-permute-start | bytes 196616 | tf_op jit(solution)/shard_map/ppermute | solution.py:17
  52.1 4.3 %collective-permute-start.9 = (bf16[256,128]{1,0:T(8,128)(2,1)S(1)}, bf16[256,128]{1,0:T(8,128)(2,1)S(1)}, u32[]{:S(2)}, u32[]{:S(2)}) collective-permute-start(bf16[256,128]{1,0:T(8,128)(2,1)S(1)} %get-tuple-element.32), channel_id=1, source_target_pairs={{0,8},{4,12},{8,0},{12,4},{16,24},{20,28},{24,16},{28,20},{1,9},{5... | collective-permute-start | bytes 196616 | tf_op jit(solution)/shard_map/ppermute | solution.py:17

commit v3 on v2

--- a/solution.py
+++ b/solution.py
@@ -17,11 +17,6 @@
     return lax.ppermute(value, axis, [(i, i ^ mask) for i in range(lax.axis_size(axis))])
 
 
-def advance(value, axis, mask, group):
-    pairs = [(i, i ^ mask) for i in range(lax.axis_size(axis))]
-    return lax.ppermute(value, axis, [(i, j) for i, j in pairs if i // group < j // group])
-
-
 def params(mib, axes=1):
     return pltpu.CompilerParams(
         dimension_semantics=("arbitrary",) * axes if axes else None,
@@ -49,13 +44,14 @@
         return pltpu.make_async_copy(w_ref.at[k, rows, :], target, sems.at[m, k])
 
     copies = [[fetch(m, k) for k in range(count)] for m in range(sems.shape[0])]
-    for copy in copies[0] + copies[1]:
+    for copy in copies[0]:
         copy.start()
     own.wait()
     for k in range(count):
         copies[0][k].wait()
-        for later in copies[2:]:
-            later[k].start()
+        if k == 0:
+            for copy in [copy for later in copies[1:] for copy in later]:
+                copy.start()
         for sum_ref, places in zip(sum_refs, targets, strict=True):
             sum_ref[k] = jnp.dot(
                 mine[...],
@@ -103,8 +99,9 @@
     if riders:
         pieces_ref, out_refs = out_refs[0], out_refs[1:]
         pieces = jnp.concatenate([pieces_ref[i] for i in range(pieces_ref.shape[0])])
-        out_refs[0][tokens:, :] = jnp.zeros((pieces.shape[0], out_refs[0].shape[1]), bf16)
-        out_refs[0][tokens:, 0 : pieces.shape[1]] = pieces.astype(bf16)
+        for out_ref in out_refs:
+            out_ref[tokens:, :] = jnp.zeros((pieces.shape[0], out_ref.shape[1]), bf16)
+            out_ref[tokens:, 0 : pieces.shape[1]] = pieces.astype(bf16)
     x = jnp.concatenate([x_ref[...] for x_ref in x_refs], axis=1)
     for k in range(count):
         rows = [columns_of(w_ref.at[m - 1, k], meta[1], group, places) for m in blocks]
@@ -128,8 +125,7 @@
     extra = 0 if riders is None else riders.shape[0] * riders.shape[1]
     if last:
         out_shape = [
-            jax.ShapeDtypeStruct((tokens + (0 if i else extra), width), bf16)
-            for i in range(len(places))
+            jax.ShapeDtypeStruct((tokens + extra, width), bf16) for _ in places
         ]
     else:
         out_shape = [jax.ShapeDtypeStruct(before.shape, f32)]
@@ -155,9 +151,11 @@
     )(meta, *args)
 
 
-def toeplitz_body(meta, pieces_ref, other_ref, out_ref, row, *, order, group):
+def toeplitz_body(meta, *refs, order, group):
+    (pieces_ref, far_ref), rider_refs, (out_ref, row) = refs[:2], refs[2:-2], refs[-2:]
     count, width = pieces_ref.shape[1:]
-    tokens = other_ref.shape[0] - pieces_ref.shape[0] * count
+    slices = pieces_ref.shape[0]
+    tokens = rider_refs[0].shape[0] - slices * count
     length = len(order) * width
     step = pl.program_id(0)
 
@@ -167,8 +165,12 @@
         across = lax.broadcasted_iota(jnp.int32, (width, width), 0)
         along = lax.broadcasted_iota(jnp.int32, (width, width), 1)
         mirror = (across + along == width - 1).astype(bf16)
-        pieces = jnp.concatenate([pieces_ref[i] for i in range(pieces_ref.shape[0])])
-        pieces = jnp.concatenate([pieces.astype(bf16), other_ref[tokens:, 0:width]])
+        near, far = [
+            jnp.concatenate([ref[i] for i in range(slices)]).astype(bf16)
+            for ref in (pieces_ref, far_ref)
+        ]
+        riders = [ref[tokens:, 0:width] for ref in rider_refs]
+        pieces = jnp.concatenate([near, *riders, far])
         turned = jnp.dot(pieces, mirror, preferred_element_type=f32)
         for at, m in enumerate(order):
             start = length - width * ((meta[3] ^ m) + 1)
@@ -199,7 +201,7 @@
                     ] = turned[:, at : at + width]
 
 
-def toeplitz(meta, pieces, other, order, group):
+def toeplitz(meta, pieces, far, riders, order, group):
     _, count, width = pieces.shape
     blocks = len(order)
     rows, columns = group * width, count * width
@@ -208,7 +210,7 @@
         grid_spec=pltpu.PrefetchScalarGridSpec(
             num_scalar_prefetch=1,
             grid=(blocks // group + 1,),
-            in_specs=[pl.BlockSpec(memory_space=pltpu.VMEM)] * 2,
+            in_specs=[pl.BlockSpec(memory_space=pltpu.VMEM)] * (2 + len(riders)),
             out_specs=pl.BlockSpec((rows, columns), lambda i, meta: (i, 0)),
             scratch_shapes=[pltpu.VMEM((8, (blocks + 1) * width), f32)],
         ),
@@ -220,7 +222,7 @@
             transcendentals=0,
         ),
         name="toeplitz",
-    )(meta, pieces, other)
+    )(meta, pieces, far, *riders)
 
 
 def place_parts(held, p_refs, places, sub, width):
@@ -246,7 +248,7 @@
 
 def convolve_pair_body(meta, table_ref, *refs, at, ahead, group, sub, last):
     p_refs, refs = refs[:2], refs[2:]
-    width = p_refs[0].shape[0]
+    width = min(p_ref.shape[0] for p_ref in p_refs)
     if last:
         sum_refs, out_refs, (held, placed) = refs[:1], refs[1:-2], refs[-2:]
     else:
@@ -268,7 +270,7 @@
 
 
 def convolve_pair(meta, table, parts, before, at, ahead, group):
-    width = parts[0].shape[0]
+    width = min(part.shape[0] for part in parts)
     columns = table.shape[1]
     sub = parts[0].shape[1] * width // columns
     last = before is not None
@@ -356,11 +358,12 @@
 def finish_body(meta, *refs, group):
     parts, out_ref = refs[:-1], refs[-1]
     sub = out_ref.shape[1] // group
-    place = meta[1]
+    place, own = meta[1], meta[2]
     for m in range(group):
         value = parts[m][...].astype(f32)
         for far in range(1, len(parts) // group):
-            value = value + parts[far * group + m][...].astype(f32)
+            other = parts[far * group + m][...].astype(f32)
+            value = value + jnp.where((own ^ far) < own, other, 0.0)
         at = pl.multiple_of((place ^ m) * sub, sub)
         out_ref[:, pl.ds(at, sub)] = value.astype(bf16)
 
@@ -401,11 +404,11 @@
     pieces = filters[None]
     order = [0]
     bit = seq // 2
-    while bit > 1:
+    while bit >= group:
         pieces = jnp.concatenate([pieces, swap(pieces, "seq", bit)])
         order += [m ^ bit for m in order]
         bit //= 2
-    order += [m ^ 1 for m in order]
+    order = [m ^ near for near in range(group) for m in order]
 
     soon = [m for m in range(1, group) if m < 3]
     late = [m for m in range(group) if m not in soon]
@@ -418,7 +421,8 @@
     for m in range(1, group):
         parts[m] = swap(mine[m], "seq", m)
     parts = [parts[m] for m in range(group)]
-    table = toeplitz(meta, pieces, parts[1], order, group)
+    far_pieces = swap(pieces, "seq", 3)
+    table = toeplitz(meta, pieces, far_pieces, parts[1:3], order, group)
 
     if groups == 2 and group == 4:
         sides = [[parts[0], parts[1]], [parts[2], parts[3]]]
@@ -444,7 +448,7 @@
         pieces.append(swap(own[m], "seq", m))
     for far in range(1, groups):
         for m in range(group):
-            pieces.append(advance(ahead[far][m], "seq", far * group + m, group))
+            pieces.append(swap(ahead[far][m], "seq", far * group + m))
     return finish(meta, pieces, group)
 
 

time: 58 us -> 55.9 us (0.964)
  starting transfers between devices: 23.9 us -> 21.9 us
  waiting for transfers between devices: 16 us -> 17.2 us
  other arithmetic: 0.7 us -> 0.01 us
    ppermute x4 -> x0, starting transfers between devices: 9.31 us -> none  [advance(): lax.ppermute(value, axis, [(i, j) for i, j in pairs if i // group < j //...]
    ppermute x11 -> x15, starting transfers between devices: 14.5 us -> 21.9 us  [swap(): lax.ppermute(value, axis, [(i, i ^ mask) for i in range(lax.axis_size(axi...]
    ppermute x11 -> x15, waiting for transfers between devices: 16 us -> 17.2 us  [swap(): lax.ppermute(value, axis, [(i, i ^ mask) for i in range(lax.axis_size(axi...]
    concatenate x2 -> x1, other arithmetic: 0.7 us -> 0.01 us  [local(): pieces = jnp.concatenate([pieces, swap(pieces, 'seq', bit)])]
  transfers between devices with their start and end apart: 15 -> 15, of which waited for: 5 -> 6; matrix products, arithmetic and copies ran while one was open for 1% -> 0% of each run, Pallas kernels for 23% -> 23%
where the time goes in v3:
time: 55.9 us; the launch traced here: 55.8 us
  starting transfers between devices  21.9 us (39%)
  waiting for transfers between devices  17.2 us (31%)
  Pallas kernels  16.6 us (30%)
    ppermute x15, starting transfers between devices, swap(): lax.ppermute(value, axis, [(i, i ^ mask) for i in range(lax.axis_size(axi...  21.9 us
    ppermute x15, waiting for transfers between devices, swap(): lax.ppermute(value, axis, [(i, i ^ mask) for i in range(lax.axis_size(axi...  17.2 us
    pallas_call x3, Pallas kernels, convolve_pair(): pl.pallas_call(functools.partial(convolve_pair_body, at=at, ahead=ahead,...  5.11 us
    pallas_call x1, Pallas kernels, project_first(): pl.pallas_call(functools.partial(project_first_body, group=group, targets...  4.66 us
    pallas_call x3, Pallas kernels, project(): pl.pallas_call(functools.partial(project_body, blocks=blocks, group=group...  3.86 us
    pallas_call x1, Pallas kernels, toeplitz(): pl.pallas_call(functools.partial(toeplitz_body, order=order, group=group)...  1.6 us
    pallas_call x1, Pallas kernels, finish(): pl.pallas_call(functools.partial(finish_body, group=group), in_specs=[pl....  1.33 us
  transfers between devices with their start and end apart: 15, of which 6 were waited for; matrix products, arithmetic and copies ran while one was open for 0% of the time, Pallas kernels for 23%

profile of v3, /device:TPU:0, one launch (start us, length us, event | category | flops | bytes accessed | tf_op | source)
XLA Modules:
  0.0 55.8 jit_solution(5072343077136979379)
XLA Ops:
  0.0 0.0 copy-start
  0.0 3.0 %collective-permute-start.2 = (bf16[256,512]{1,0:T(8,128)(2,1)}, bf16[256,512]{1,0:T(8,128)(2,1)S(1)}, u32[]{:S(2)}, u32[]{:S(2)}) collective-permute-start(bf16[256,512]{1,0:T(8,128)(2,1)} %mine_ref.1), channel_id=1, source_target_pairs={{0,2},{1,3},{2,0},{3,1},{4,6},{5,7},{6,4},{7,5},{8,10},{9,11},{10,... | collective-permute-start | bytes 786440 | tf_op jit(solution)/shard_map/ppermute | solution.py:17
  3.0 0.0 collective-permute-start.4
  3.0 2.6 %collective-permute-start = (f32[1,4,256]{2,1,0:T(4,128)}, f32[1,4,256]{2,1,0:T(4,128)S(1)}, u32[]{:S(2)}, u32[]{:S(2)}) collective-permute-start(f32[1,4,256]{2,1,0:T(4,128)} %bitcast.1), channel_id=1, source_target_pairs={{0,16},{4,20},{8,24},{12,28},{16,0},{20,4},{24,8},{28,12},{1,17},{... | collective-permute-start | bytes 12296 | tf_op jit(solution)/shard_map/ppermute | solution.py:17
  5.6 3.9 %collective-permute-done.2.refs_1_ = bf16[256,512]{1,0:T(8,128)(2,1)S(1)} collective-permute-done((bf16[256,512]{1,0:T(8,128)(2,1)}, bf16[256,512]{1,0:T(8,128)(2,1)S(1)}, u32[]{:S(2)}, u32[]{:S(2)}) %collective-permute-start.2) | collective-permute-done | bytes 262176 | tf_op jit(solution)/shard_map/ppermute | solution.py:17
  9.5 0.0 collective-permute-start.3
  9.5 4.7 %project_first.1 = (f32[4,256,256]{2,1,0:T(8,128)S(1)}, f32[4,256,256]{2,1,0:T(8,128)S(1)}, bf16[3,4,512,512]{3,2,1,0:T(8,128)(2,1)S(1)}) custom-call(s32[4]{0:T(128)S(1)} %compare_select_fusion.2.meta, bf16[256,512]{1,0:T(8,128)(2,1)} %mine_ref.1, bf16[4,2048,512]{2,1,0:T(8,128)(2,1)} %w_ref.1), custom_call_target="tpu_custom_call" | custom-call | flops 536870912 | bytes 8388608 | tf_op jit(solution)/shard_map/project_first/pallas_call | solution.py:70
  14.2 0.0 collective-permute-done
  14.2 0.0 copy-done
  14.2 0.0 collective-permute-done.4.refs_0_
  14.2 1.3 %shard_map.37.refs_2_ = f32[4,256,256]{2,1,0:T(8,128)S(1)} custom-call(s32[4]{0:T(128)S(1)} %compare_select_fusion.2.meta, bf16[256,512]{1,0:T(8,128)(2,1)S(1)} %collective-permute-done.4.refs_0_, bf16[256,512]{1,0:T(8,128)(2,1)S(1)} %collective-permute-done.2.refs_1_, bf16[3,4,512,512]{3,2,1,0:T(8,128)(2,1)S(1)} %get-tuple-element.22.refs_2_.refs_1_.refs_3_, ...), custom_call_target="tpu_custom_call" | custom-call | flops 536870912 | bytes 2097152 | tf_op jit(solution)/shard_map/pallas_call | solution.py:133
  15.5 0.0 collective-permute-done.3.refs_0_.refs_2_
  15.5 1.0 %shard_map.38 = (bf16[264,512]{1,0:T(8,128)(2,1)S(1)}, bf16[264,512]{1,0:T(8,128)(2,1)S(1)}) custom-call(s32[4]{0:T(128)S(1)} %compare_select_fusion.2.meta, bf16[256,512]{1,0:T(8,128)(2,1)S(1)} %collective-permute-done.3.refs_0_.refs_2_, bf16[3,4,512,512]{3,2,1,0:T(8,128)(2,1)S(1)} %get-tuple-element.22.refs_2_.refs_1_.refs_3_, ...), custom_call_target="tpu_custom_call" | custom-call | flops 268435456 | bytes 1048576 | tf_op jit(solution)/shard_map/pallas_call | solution.py:133
  16.6 1.8 %collective-permute-start.5 = (bf16[264,512]{1,0:T(8,128)(2,1)S(1)}, bf16[264,512]{1,0:T(8,128)(2,1)S(1)}, u32[]{:S(2)}, u32[]{:S(2)}) collective-permute-start(bf16[264,512]{1,0:T(8,128)(2,1)S(1)} %get-tuple-element.24), channel_id=1, source_target_pairs={{0,4},{4,0},{8,12},{12,8},{16,20},{20,16},{24,28},{28,24},{1,5},{5... | collective-permute-start | bytes 811016 | tf_op jit(solution)/shard_map/ppermute | solution.py:17
  18.3 1.6 %collective-permute-start.6 = (bf16[264,512]{1,0:T(8,128)(2,1)S(1)}, bf16[264,512]{1,0:T(8,128)(2,1)S(1)}, u32[]{:S(2)}, u32[]{:S(2)}) collective-permute-start(bf16[264,512]{1,0:T(8,128)(2,1)S(1)} %get-tuple-element.25), channel_id=1, source_target_pairs={{0,8},{4,12},{8,0},{12,4},{16,24},{20,28},{24,16},{28,20},{1,9},{5... | collective-permute-start | bytes 811016 | tf_op jit(solution)/shard_map/ppermute | solution.py:17
  19.9 1.6 %shard_map.39 = (bf16[256,512]{1,0:T(8,128)(2,1)S(1)}, bf16[256,512]{1,0:T(8,128)(2,1)S(1)}) custom-call(s32[4]{0:T(128)S(1)} %compare_select_fusion.2.meta, bf16[256,512]{1,0:T(8,128)(2,1)S(1)} %collective-permute-done.4.refs_0_, bf16[256,512]{1,0:T(8,128)(2,1)S(1)} %collective-permute-done.2.refs_1_, ...), custom_call_target="tpu_custom_call" | custom-call | flops 805306368 | bytes 3145728 | tf_op jit(solution)/shard_map/pallas_call | solution.py:133
  21.5 0.3 collective-permute-start.7
  21.7 2.7 %collective-permute-start.1 = (f32[2,4,256]{2,1,0:T(4,128)S(1)}, f32[2,4,256]{2,1,0:T(4,128)S(1)}, u32[]{:S(2)}, u32[]{:S(2)}) collective-permute-start(f32[2,4,256]{2,1,0:T(4,128)S(1)} %pad_maximum_fusion.refs_3_.refs_0_), channel_id=1, source_target_pairs={{0,12},{4,8},{8,4},{12,0},{16,28},{20,24},{24,20},{28,16},{1,13},{... | collective-permute-start | bytes 24584 | tf_op jit(solution)/shard_map/ppermute | solution.py:17
  24.5 8.1 %collective-permute-done.1.refs_1_ = f32[2,4,256]{2,1,0:T(4,128)S(1)} collective-permute-done((f32[2,4,256]{2,1,0:T(4,128)S(1)}, f32[2,4,256]{2,1,0:T(4,128)S(1)}, u32[]{:S(2)}, u32[]{:S(2)}) %collective-permute-start.1) | collective-permute-done | bytes 8224 | tf_op jit(solution)/shard_map/ppermute | solution.py:17
  32.5 0.0 collective-permute-done.5.refs_2_.refs_1_
  32.5 0.0 collective-permute-done.6.refs_3_.refs_0_
  32.6 1.6 %toeplitz.1.table_ref = bf16[3072,1024]{1,0:T(8,128)(2,1)S(1)} custom-call(s32[4]{0:T(128)S(1)} %compare_select_fusion.2.meta, f32[2,4,256]{2,1,0:T(4,128)S(1)} %pad_maximum_fusion.refs_3_.refs_0_, f32[2,4,256]{2,1,0:T(4,128)S(1)} %collective-permute-done.1.refs_1_, bf16[264,512]{1,0:T(8,128)(2,1)S(1)} %collective-permute-done.5.refs_2_.refs_1_, ...), custom_call_target="tpu_custom_call" | custom-call | flops 16777216 | bytes 4194304 | tf_op jit(solution)/shard_map/toeplitz/pallas_call | solution.py:208
  34.2 2.1 %shard_map.40 = (f32[4,256,128]{2,1,0:T(8,128)S(1)}, f32[4,256,128]{2,1,0:T(8,128)S(1)}) custom-call(s32[4]{0:T(128)S(1)} %compare_select_fusion.2.meta, bf16[3072,1024]{1,0:T(8,128)(2,1)S(1)} %toeplitz.1.table_ref, bf16[256,512]{1,0:T(8,128)(2,1)S(1)} %get-tuple-element.28.refs_0_, bf16[264,512]{1,0:T(8,128)(2,1)S(1)} %collective-permute-done.5.refs_2_.refs_1_), custom_call_target="tpu_custom_call" | custom-call | flops 1342177280 | bytes 524288 | tf_op jit(solution)/shard_map/pallas_call | solution.py:285
  36.3 0.0 collective-permute-done.7.refs_1_
  36.3 1.5 %shard_map.42 = (bf16[256,128]{1,0:T(8,128)(2,1)S(1)}, bf16[256,128]{1,0:T(8,128)(2,1)S(1)}, bf16[256,128]{1,0:T(8,128)(2,1)S(1)}, bf16[256,128]{1,0:T(8,128)(2,1)S(1)}) custom-call(s32[4]{0:T(128)S(1)} %compare_select_fusion.2.meta, bf16[3072,1024]{1,0:T(8,128)(2,1)S(1)} %toeplitz.1.table_ref, bf16[264,512]{1,0:T(8,128)(2,1)S(1)} %collective-permute-done.6.refs_3_.refs_0_, ...), custom_call_target="tpu_custom_call" | custom-call | flops 671088640 | bytes 524288 | tf_op jit(solution)/shard_map/pallas_call | solution.py:285
  37.8 2.8 %collective-permute-start.11 = (bf16[256,128]{1,0:T(8,128)(2,1)S(1)}, bf16[256,128]{1,0:T(8,128)(2,1)S(1)}, u32[]{:S(2)}, u32[]{:S(2)}) collective-permute-start(bf16[256,128]{1,0:T(8,128)(2,1)S(1)} %get-tuple-element.35), channel_id=1, source_target_pairs={{0,16},{4,20},{8,24},{12,28},{16,0},{20,4},{24,8},{28,12},{1,17},{... | collective-permute-start | bytes 196616 | tf_op jit(solution)/shard_map/ppermute | solution.py:17
  40.6 1.3 %collective-permute-start.12 = (bf16[256,128]{1,0:T(8,128)(2,1)S(1)}, bf16[256,128]{1,0:T(8,128)(2,1)S(1)}, u32[]{:S(2)}, u32[]{:S(2)}) collective-permute-start(bf16[256,128]{1,0:T(8,128)(2,1)S(1)} %get-tuple-element.36), channel_id=1, source_target_pairs={{0,20},{4,16},{8,28},{12,24},{16,4},{20,0},{24,12},{28,8},{1,21},{... | collective-permute-start | bytes 196616 | tf_op jit(solution)/shard_map/ppermute | solution.py:17
  41.9 3.6 %collective-permute-start.13 = (bf16[256,128]{1,0:T(8,128)(2,1)S(1)}, bf16[256,128]{1,0:T(8,128)(2,1)S(1)}, u32[]{:S(2)}, u32[]{:S(2)}) collective-permute-start(bf16[256,128]{1,0:T(8,128)(2,1)S(1)} %get-tuple-element.37), channel_id=1, source_target_pairs={{0,24},{4,28},{8,16},{12,20},{16,8},{20,12},{24,0},{28,4},{1,25},{... | collective-permute-start | bytes 196616 | tf_op jit(solution)/shard_map/ppermute | solution.py:17
  45.5 0.0 collective-permute-start.14
  45.5 1.5 %shard_map.41 = (bf16[256,128]{1,0:T(8,128)(2,1)S(1)}, bf16[256,128]{1,0:T(8,128)(2,1)S(1)}, bf16[256,128]{1,0:T(8,128)(2,1)S(1)}, bf16[256,128]{1,0:T(8,128)(2,1)S(1)}) custom-call(s32[4]{0:T(128)S(1)} %compare_select_fusion.2.meta, bf16[3072,1024]{1,0:T(8,128)(2,1)S(1)} %toeplitz.1.table_ref, bf16[264,512]{1,0:T(8,128)(2,1)S(1)} %collective-permute-done.6.refs_3_.refs_0_, ...), custom_call_target="tpu_custom_call" | custom-call | flops 671088640 | bytes 524288 | tf_op jit(solution)/shard_map/pallas_call | solution.py:285
  47.0 0.9 %collective-permute-start.10 = (bf16[256,128]{1,0:T(8,128)(2,1)S(1)}, bf16[256,128]{1,0:T(8,128)(2,1)S(1)}, u32[]{:S(2)}, u32[]{:S(2)}) collective-permute-start(bf16[256,128]{1,0:T(8,128)(2,1)S(1)} %get-tuple-element.33), channel_id=1, source_target_pairs={{0,12},{4,8},{8,4},{12,0},{16,28},{20,24},{24,20},{28,16},{1,13},{... | collective-permute-start | bytes 196616 | tf_op jit(solution)/shard_map/ppermute | solution.py:17
  48.0 0.0 collective-permute-done.11.refs_4_
  48.0 0.9 %collective-permute-start.8 = (bf16[256,128]{1,0:T(8,128)(2,1)S(1)}, bf16[256,128]{1,0:T(8,128)(2,1)S(1)}, u32[]{:S(2)}, u32[]{:S(2)}) collective-permute-start(bf16[256,128]{1,0:T(8,128)(2,1)S(1)} %get-tuple-element.31), channel_id=1, source_target_pairs={{0,4},{4,0},{8,12},{12,8},{16,20},{20,16},{24,28},{28,24},{1,5},{5... | collective-permute-start | bytes 196616 | tf_op jit(solution)/shard_map/ppermute | solution.py:17
  48.8 1.4 %collective-permute-done.12.refs_5_ = bf16[256,128]{1,0:T(8,128)(2,1)S(1)} collective-permute-done((bf16[256,128]{1,0:T(8,128)(2,1)S(1)}, bf16[256,128]{1,0:T(8,128)(2,1)S(1)}, u32[]{:S(2)}, u32[]{:S(2)}) %collective-permute-start.12) | collective-permute-done | bytes 65568 | tf_op jit(solution)/shard_map/ppermute | solution.py:17
  50.2 0.4 collective-permute-start.9
  50.6 0.0 collective-permute-done.13.refs_6_
  50.6 2.0 %collective-permute-done.14.refs_7_ = bf16[256,128]{1,0:T(8,128)(2,1)S(1)} collective-permute-done((bf16[256,128]{1,0:T(8,128)(2,1)S(1)}, bf16[256,128]{1,0:T(8,128)(2,1)S(1)}, u32[]{:S(2)}, u32[]{:S(2)}) %collective-permute-start.14) | collective-permute-done | bytes 65568 | tf_op jit(solution)/shard_map/ppermute | solution.py:17
  52.6 1.1 %collective-permute-done.10.refs_3_ = bf16[256,128]{1,0:T(8,128)(2,1)S(1)} collective-permute-done((bf16[256,128]{1,0:T(8,128)(2,1)S(1)}, bf16[256,128]{1,0:T(8,128)(2,1)S(1)}, u32[]{:S(2)}, u32[]{:S(2)}) %collective-permute-start.10) | collective-permute-done | bytes 65568 | tf_op jit(solution)/shard_map/ppermute | solution.py:17
  53.6 0.0 collective-permute-done.8.refs_1_
  53.6 0.8 %collective-permute-done.9.refs_2_ = bf16[256,128]{1,0:T(8,128)(2,1)S(1)} collective-permute-done((bf16[256,128]{1,0:T(8,128)(2,1)S(1)}, bf16[256,128]{1,0:T(8,128)(2,1)S(1)}, u32[]{:S(2)}, u32[]{:S(2)}) %collective-permute-start.9) | collective-permute-done | bytes 65568 | tf_op jit(solution)/shard_map/ppermute | solution.py:17
  54.5 1.3 %finish.1 = bf16[256,512]{1,0:T(8,128)(2,1)} custom-call(s32[4]{0:T(128)S(1)} %compare_select_fusion.2.meta, bf16[256,128]{1,0:T(8,128)(2,1)S(1)} %get-tuple-element.30.refs_0_, bf16[256,128]{1,0:T(8,128)(2,1)S(1)} %collective-permute-done.8.refs_1_, bf16[256,128]{1,0:T(8,128)(2,1)S(1)} %collective-permute-done.9.refs_2_, ...), custom_call_target="tpu_custom_call" | custom-call | tf_op jit(solution)/shard_map/finish/pallas_call | solution.py:374
  (2 shorter events, 0.0 us)
Async XLA Ops:
  0.0 14.2 %copy-start = (f32[4,256]{1,0:T(4,128)S(1)}, f32[4,256]{1,0:T(4,128)}, u32[]{:S(2)}) copy-start(f32[4,256]{1,0:T(4,128)} %param.5) | copy-start | bytes 12292
  0.0 9.5 %collective-permute-start.2 = (bf16[256,512]{1,0:T(8,128)(2,1)}, bf16[256,512]{1,0:T(8,128)(2,1)S(1)}, u32[]{:S(2)}, u32[]{:S(2)}) collective-permute-start(bf16[256,512]{1,0:T(8,128)(2,1)} %mine_ref.1), channel_id=1, source_target_pairs={{0,2},{1,3},{2,0},{3,1},{4,6},{5,7},{6,4},{7,5},{8,10},{9,11},{10,... | collective-permute-start | bytes 786440 | tf_op jit(solution)/shard_map/ppermute | solution.py:17
  3.0 11.2 %collective-permute-start.4 = (bf16[256,512]{1,0:T(8,128)(2,1)}, bf16[256,512]{1,0:T(8,128)(2,1)S(1)}, u32[]{:S(2)}, u32[]{:S(2)}) collective-permute-start(bf16[256,512]{1,0:T(8,128)(2,1)} %mine_ref.1), channel_id=1, source_target_pairs={{0,1},{1,0},{2,3},{3,2},{4,5},{5,4},{6,7},{7,6},{8,9},{9,8},{10,11... | collective-permute-start | bytes 786440 | tf_op jit(solution)/shard_map/ppermute | solution.py:17
  3.0 11.2 %collective-permute-start = (f32[1,4,256]{2,1,0:T(4,128)}, f32[1,4,256]{2,1,0:T(4,128)S(1)}, u32[]{:S(2)}, u32[]{:S(2)}) collective-permute-start(f32[1,4,256]{2,1,0:T(4,128)} %bitcast.1), channel_id=1, source_target_pairs={{0,16},{4,20},{8,24},{12,28},{16,0},{20,4},{24,8},{28,12},{1,17},{... | collective-permute-start | bytes 12296 | tf_op jit(solution)/shard_map/ppermute | solution.py:17
  9.5 6.0 %collective-permute-start.3 = (bf16[256,512]{1,0:T(8,128)(2,1)S(1)}, bf16[256,512]{1,0:T(8,128)(2,1)S(1)}, u32[]{:S(2)}, u32[]{:S(2)}) collective-permute-start(bf16[256,512]{1,0:T(8,128)(2,1)S(1)} %collective-permute-done.2.refs_1_), channel_id=1, source_target_pairs={{0,1},{1,0},{2,3},{3,2},{4,5},{5,4},{6,7},{7,6},{8,9},{9,8},{10,11... | collective-permute-start | bytes 786440 | tf_op jit(solution)/shard_map/ppermute | solution.py:17
  16.6 16.0 %collective-permute-start.5 = (bf16[264,512]{1,0:T(8,128)(2,1)S(1)}, bf16[264,512]{1,0:T(8,128)(2,1)S(1)}, u32[]{:S(2)}, u32[]{:S(2)}) collective-permute-start(bf16[264,512]{1,0:T(8,128)(2,1)S(1)} %get-tuple-element.24), channel_id=1, source_target_pairs={{0,4},{4,0},{8,12},{12,8},{16,20},{20,16},{24,28},{28,24},{1,5},{5... | collective-permute-start | bytes 811016 | tf_op jit(solution)/shard_map/ppermute | solution.py:17
  18.3 14.2 %collective-permute-start.6 = (bf16[264,512]{1,0:T(8,128)(2,1)S(1)}, bf16[264,512]{1,0:T(8,128)(2,1)S(1)}, u32[]{:S(2)}, u32[]{:S(2)}) collective-permute-start(bf16[264,512]{1,0:T(8,128)(2,1)S(1)} %get-tuple-element.25), channel_id=1, source_target_pairs={{0,8},{4,12},{8,0},{12,4},{16,24},{20,28},{24,16},{28,20},{1,9},{5... | collective-permute-start | bytes 811016 | tf_op jit(solution)/shard_map/ppermute | solution.py:17
  21.5 14.8 %collective-permute-start.7 = (bf16[256,512]{1,0:T(8,128)(2,1)S(1)}, bf16[256,512]{1,0:T(8,128)(2,1)S(1)}, u32[]{:S(2)}, u32[]{:S(2)}) collective-permute-start(bf16[256,512]{1,0:T(8,128)(2,1)S(1)} %get-tuple-element.27), channel_id=1, source_target_pairs={{0,12},{4,8},{8,4},{12,0},{16,28},{20,24},{24,20},{28,16},{1,13},{... | collective-permute-start | bytes 786440 | tf_op jit(solution)/shard_map/ppermute | solution.py:17
  21.7 10.8 %collective-permute-start.1 = (f32[2,4,256]{2,1,0:T(4,128)S(1)}, f32[2,4,256]{2,1,0:T(4,128)S(1)}, u32[]{:S(2)}, u32[]{:S(2)}) collective-permute-start(f32[2,4,256]{2,1,0:T(4,128)S(1)} %pad_maximum_fusion.refs_3_.refs_0_), channel_id=1, source_target_pairs={{0,12},{4,8},{8,4},{12,0},{16,28},{20,24},{24,20},{28,16},{1,13},{... | collective-permute-start | bytes 24584 | tf_op jit(solution)/shard_map/ppermute | solution.py:17
  37.8 10.1 %collective-permute-start.11 = (bf16[256,128]{1,0:T(8,128)(2,1)S(1)}, bf16[256,128]{1,0:T(8,128)(2,1)S(1)}, u32[]{:S(2)}, u32[]{:S(2)}) collective-permute-start(bf16[256,128]{1,0:T(8,128)(2,1)S(1)} %get-tuple-element.35), channel_id=1, source_target_pairs={{0,16},{4,20},{8,24},{12,28},{16,0},{20,4},{24,8},{28,12},{1,17},{... | collective-permute-start | bytes 196616 | tf_op jit(solution)/shard_map/ppermute | solution.py:17
  40.6 9.6 %collective-permute-start.12 = (bf16[256,128]{1,0:T(8,128)(2,1)S(1)}, bf16[256,128]{1,0:T(8,128)(2,1)S(1)}, u32[]{:S(2)}, u32[]{:S(2)}) collective-permute-start(bf16[256,128]{1,0:T(8,128)(2,1)S(1)} %get-tuple-element.36), channel_id=1, source_target_pairs={{0,20},{4,16},{8,28},{12,24},{16,4},{20,0},{24,12},{28,8},{1,21},{... | collective-permute-start | bytes 196616 | tf_op jit(solution)/shard_map/ppermute | solution.py:17
  41.9 8.7 %collective-permute-start.13 = (bf16[256,128]{1,0:T(8,128)(2,1)S(1)}, bf16[256,128]{1,0:T(8,128)(2,1)S(1)}, u32[]{:S(2)}, u32[]{:S(2)}) collective-permute-start(bf16[256,128]{1,0:T(8,128)(2,1)S(1)} %get-tuple-element.37), channel_id=1, source_target_pairs={{0,24},{4,28},{8,16},{12,20},{16,8},{20,12},{24,0},{28,4},{1,25},{... | collective-permute-start | bytes 196616 | tf_op jit(solution)/shard_map/ppermute | solution.py:17
  45.5 7.1 %collective-permute-start.14 = (bf16[256,128]{1,0:T(8,128)(2,1)S(1)}, bf16[256,128]{1,0:T(8,128)(2,1)S(1)}, u32[]{:S(2)}, u32[]{:S(2)}) collective-permute-start(bf16[256,128]{1,0:T(8,128)(2,1)S(1)} %get-tuple-element.38), channel_id=1, source_target_pairs={{0,28},{4,24},{8,20},{12,16},{16,12},{20,8},{24,4},{28,0},{1,29},{... | collective-permute-start | bytes 196616 | tf_op jit(solution)/shard_map/ppermute | solution.py:17
  47.0 6.6 %collective-permute-start.10 = (bf16[256,128]{1,0:T(8,128)(2,1)S(1)}, bf16[256,128]{1,0:T(8,128)(2,1)S(1)}, u32[]{:S(2)}, u32[]{:S(2)}) collective-permute-start(bf16[256,128]{1,0:T(8,128)(2,1)S(1)} %get-tuple-element.33), channel_id=1, source_target_pairs={{0,12},{4,8},{8,4},{12,0},{16,28},{20,24},{24,20},{28,16},{1,13},{... | collective-permute-start | bytes 196616 | tf_op jit(solution)/shard_map/ppermute | solution.py:17
  48.0 5.7 %collective-permute-start.8 = (bf16[256,128]{1,0:T(8,128)(2,1)S(1)}, bf16[256,128]{1,0:T(8,128)(2,1)S(1)}, u32[]{:S(2)}, u32[]{:S(2)}) collective-permute-start(bf16[256,128]{1,0:T(8,128)(2,1)S(1)} %get-tuple-element.31), channel_id=1, source_target_pairs={{0,4},{4,0},{8,12},{12,8},{16,20},{20,16},{24,28},{28,24},{1,5},{5... | collective-permute-start | bytes 196616 | tf_op jit(solution)/shard_map/ppermute | solution.py:17
  50.2 4.3 %collective-permute-start.9 = (bf16[256,128]{1,0:T(8,128)(2,1)S(1)}, bf16[256,128]{1,0:T(8,128)(2,1)S(1)}, u32[]{:S(2)}, u32[]{:S(2)}) collective-permute-start(bf16[256,128]{1,0:T(8,128)(2,1)S(1)} %get-tuple-element.32), channel_id=1, source_target_pairs={{0,8},{4,12},{8,0},{12,4},{16,24},{20,28},{24,16},{28,20},{1,9},{5... | collective-permute-start | bytes 196616 | tf_op jit(solution)/shard_map/ppermute | solution.py:17

commit v4 on v3

--- a/solution.py
+++ b/solution.py
@@ -1,5 +1,3 @@
-import functools
-
 import jax
 import jax.numpy as jnp
 from jax import lax
@@ -22,6 +20,15 @@
         dimension_semantics=("arbitrary",) * axes if axes else None,
         vmem_limit_bytes=mib * 1024 * 1024,
     )
+
+
+def on_device(body, group, **settings):
+    def kernel(*refs):
+        seq = lax.axis_index("seq")
+        place, own = seq & (group - 1), lax.shift_right_logical(seq, group.bit_length() - 1)
+        body((lax.axis_index("chan"), place, own, seq), *refs, group=group, **settings)
+
+    return kernel
 
 
 def columns_of(w, place, group, targets):
@@ -62,14 +69,14 @@
         copy.wait()
 
 
-def project_first(meta, mine, weights, chan, group, targets):
+def project_first(mine, weights, chan, group, targets):
     tokens, depth = mine.shape
     count, _, width = weights.shape
     sub = width // group
     vmem, hbm = pl.BlockSpec(memory_space=pltpu.VMEM), pl.BlockSpec(memory_space=pltpu.HBM)
     return pl.pallas_call(
-        functools.partial(project_first_body, group=group, targets=targets),
-        in_specs=[pl.BlockSpec(memory_space=pltpu.SMEM), hbm, hbm],
+        on_device(project_first_body, group=group, targets=targets),
+        in_specs=[hbm, hbm],
         out_specs=[vmem] * (len(targets) + 1),
         scratch_shapes=[
             pltpu.VMEM((tokens, depth), bf16),
@@ -88,7 +95,7 @@
             transcendentals=0,
         ),
         name="project_first",
-    )(meta, pltpu.with_memory_space_constraint(mine, pltpu.HBM), weights)
+    )(pltpu.with_memory_space_constraint(mine, pltpu.HBM), weights)
 
 
 def project_body(meta, *refs, blocks, group, places, last, riders):
@@ -117,7 +124,7 @@
             out_refs[0][k] = total
 
 
-def project(meta, held, blocks, ahead, before, group, places, last, riders):
+def project(held, blocks, ahead, before, group, places, last, riders):
     count, tokens, columns = before.shape
     depth = ahead.shape[2]
     width = count * columns // len(places)
@@ -131,15 +138,13 @@
         out_shape = [jax.ShapeDtypeStruct(before.shape, f32)]
     args = [held[m] for m in blocks] + [ahead, before] + ([] if riders is None else [riders])
     return pl.pallas_call(
-        functools.partial(
-            project_body,
-            blocks=blocks,
+        on_device(project_body, blocks=blocks,
             group=group,
             places=places,
             last=last,
             riders=riders is not None,
         ),
-        in_specs=[pl.BlockSpec(memory_space=pltpu.SMEM)] + [vmem] * len(args),
+        in_specs=[vmem] * len(args),
         out_specs=[vmem] * len(out_shape),
         out_shape=out_shape,
         compiler_params=params(32, 0),
@@ -148,7 +153,7 @@
             bytes_accessed=2 * depth * len(blocks) * columns * count,
             transcendentals=0,
         ),
-    )(meta, *args)
+    )(*args)
 
 
 def toeplitz_body(meta, *refs, order, group):
@@ -201,17 +206,17 @@
                     ] = turned[:, at : at + width]
 
 
-def toeplitz(meta, pieces, far, riders, order, group):
+def toeplitz(pieces, far, riders, order, group):
     _, count, width = pieces.shape
     blocks = len(order)
     rows, columns = group * width, count * width
     return pl.pallas_call(
-        functools.partial(toeplitz_body, order=order, group=group),
+        on_device(toeplitz_body, order=order, group=group),
         grid_spec=pltpu.PrefetchScalarGridSpec(
-            num_scalar_prefetch=1,
+            num_scalar_prefetch=0,
             grid=(blocks // group + 1,),
             in_specs=[pl.BlockSpec(memory_space=pltpu.VMEM)] * (2 + len(riders)),
-            out_specs=pl.BlockSpec((rows, columns), lambda i, meta: (i, 0)),
+            out_specs=pl.BlockSpec((rows, columns), lambda i: (i, 0)),
             scratch_shapes=[pltpu.VMEM((8, (blocks + 1) * width), f32)],
         ),
         out_shape=jax.ShapeDtypeStruct(((blocks + group) * width, columns), bf16),
@@ -222,7 +227,7 @@
             transcendentals=0,
         ),
         name="toeplitz",
-    )(meta, pieces, far, *riders)
+    )(pieces, far, *riders)
 
 
 def place_parts(held, p_refs, places, sub, width):
@@ -269,7 +274,7 @@
                 out_refs[i][r] = value
 
 
-def convolve_pair(meta, table, parts, before, at, ahead, group):
+def convolve_pair(table, parts, before, at, ahead, group):
     width = min(part.shape[0] for part in parts)
     columns = table.shape[1]
     sub = parts[0].shape[1] * width // columns
@@ -283,10 +288,9 @@
         scratch = []
     args = [table, *parts] + ([before] if last else [])
     return pl.pallas_call(
-        functools.partial(
-            convolve_pair_body, at=at, ahead=ahead, group=group, sub=sub, last=last
-        ),
-        in_specs=[pl.BlockSpec(memory_space=pltpu.SMEM)] + [vmem] * len(args),
+        on_device(convolve_pair_body, at=at, ahead=ahead, group=group, sub=sub, last=last
+        ),
+        in_specs=[vmem] * len(args),
         out_specs=[vmem] * len(out_shape),
         out_shape=out_shape,
         scratch_shapes=[pltpu.VMEM((columns, 2 * sub), bf16), *scratch],
@@ -296,7 +300,7 @@
             bytes_accessed=2 * width * columns,
             transcendentals=0,
         ),
-    )(meta, *args)
+    )(*args)
 
 
 def convolve_all_body(meta, low_ref, high_ref, *refs, group, sub):
@@ -322,23 +326,23 @@
     store_parts(out_refs, placed, sums, meta[1])
 
 
-def convolve_all(meta, table, parts, group):
+def convolve_all(table, parts, group):
     width = parts[0].shape[0]
     columns = table.shape[1]
     sub = parts[0].shape[1] * width // columns
     rows = group * width
     steps = table.shape[0] // rows - 1
     return pl.pallas_call(
-        functools.partial(convolve_all_body, group=group, sub=sub),
+        on_device(convolve_all_body, group=group, sub=sub),
         grid_spec=pltpu.PrefetchScalarGridSpec(
-            num_scalar_prefetch=1,
+            num_scalar_prefetch=0,
             grid=(steps,),
             in_specs=[
-                pl.BlockSpec((rows, columns), lambda i, meta: (i, 0)),
-                pl.BlockSpec((rows, columns), lambda i, meta: (i + 1, 0)),
+                pl.BlockSpec((rows, columns), lambda i: (i, 0)),
+                pl.BlockSpec((rows, columns), lambda i: (i + 1, 0)),
             ]
-            + [pl.BlockSpec(part.shape, lambda i, meta: (0, 0)) for part in parts],
-            out_specs=[pl.BlockSpec((width, sub), lambda i, meta: (i, 0))] * group,
+            + [pl.BlockSpec(part.shape, lambda i: (0, 0)) for part in parts],
+            out_specs=[pl.BlockSpec((width, sub), lambda i: (i, 0))] * group,
             scratch_shapes=[
                 pltpu.VMEM((columns, group * sub), bf16),
                 pltpu.VMEM((group, width, sub), bf16),
@@ -352,7 +356,7 @@
             transcendentals=0,
         ),
         name="convolve_all",
-    )(meta, table, table, *parts)
+    )(table, table, *parts)
 
 
 def finish_body(meta, *refs, group):
@@ -368,18 +372,17 @@
         out_ref[:, pl.ds(at, sub)] = value.astype(bf16)
 
 
-def finish(meta, parts, group):
+def finish(parts, group):
     width, sub = parts[0].shape
     shape = (width, sub * group)
     return pl.pallas_call(
-        functools.partial(finish_body, group=group),
-        in_specs=[pl.BlockSpec(memory_space=pltpu.SMEM)]
-        + [pl.BlockSpec(memory_space=pltpu.VMEM)] * len(parts),
+        on_device(finish_body, group=group),
+        in_specs=[pl.BlockSpec(memory_space=pltpu.VMEM)] * len(parts),
         out_specs=pl.BlockSpec(memory_space=pltpu.VMEM),
         out_shape=jax.ShapeDtypeStruct(shape, bf16),
         compiler_params=params(24, 0),
         name="finish",
-    )(meta, *parts)
+    )(*parts)
 
 
 def local(inputs, weights, filters):
@@ -387,14 +390,7 @@
     group = min(4, seq)
     groups = seq // group
     width = inputs.shape[0]
-    at_seq, at_chan = lax.axis_index("seq"), lax.axis_index("chan")
-    lane = jnp.arange(4)
-    meta = jnp.where(
-        lane == 0,
-        at_chan,
-        jnp.where(lane == 1, at_seq % group, jnp.where(lane == 2, at_seq // group, at_seq)),
-    ).astype(jnp.int32)
-
+    at_seq = lax.axis_index("seq")
     held = {0: inputs}
     held[2] = swap(inputs, "chan", 2)
     held[1] = swap(inputs, "chan", 1)
@@ -412,26 +408,26 @@
 
     soon = [m for m in range(1, group) if m < 3]
     late = [m for m in range(group) if m not in soon]
-    to_soon, to_late, ahead = project_first(meta, inputs, weights, chan, group, [soon, late])
-    (to_soon,) = project(meta, held, [1, 2], ahead, to_soon, group, soon, False, None)
-    mine = project(meta, held, [3], ahead, to_soon, group, soon, True, pieces)
-    mine += project(meta, held, [1, 2, 3], ahead, to_late, group, late, True, None)
+    to_soon, to_late, ahead = project_first(inputs, weights, chan, group, [soon, late])
+    (to_soon,) = project(held, [1, 2], ahead, to_soon, group, soon, False, None)
+    mine = project(held, [3], ahead, to_soon, group, soon, True, pieces)
+    mine += project(held, [1, 2, 3], ahead, to_late, group, late, True, None)
     mine = dict(zip(soon + late, mine, strict=True))
     parts = {0: mine[0]}
     for m in range(1, group):
         parts[m] = swap(mine[m], "seq", m)
     parts = [parts[m] for m in range(group)]
     far_pieces = swap(pieces, "seq", 3)
-    table = toeplitz(meta, pieces, far_pieces, parts[1:3], order, group)
+    table = toeplitz(pieces, far_pieces, parts[1:3], order, group)
 
     if groups == 2 and group == 4:
         sides = [[parts[0], parts[1]], [parts[2], parts[3]]]
-        own, after = convolve_pair(meta, table, sides[0], None, 0, (0, 1), group)
-        after = convolve_pair(meta, table, sides[1], after, 1, (1,), group)
-        own = convolve_pair(meta, table, sides[1], own, 1, (0,), group)
+        own, after = convolve_pair(table, sides[0], None, 0, (0, 1), group)
+        after = convolve_pair(table, sides[1], after, 1, (1,), group)
+        own = convolve_pair(table, sides[1], own, 1, (0,), group)
         ahead = {1: after}
     else:
-        every = convolve_all(meta, table, [parts[m] for m in range(group)], group)
+        every = convolve_all(table, [parts[m] for m in range(group)], group)
         own = [every[m][:width] for m in range(group)]
         here = at_seq // group
         ahead = {
@@ -449,7 +445,7 @@
     for far in range(1, groups):
         for m in range(group):
             pieces.append(swap(ahead[far][m], "seq", far * group + m))
-    return finish(meta, pieces, group)
+    return finish(pieces, group)
 
 
 def solution(mesh):

time: 55.9 us -> 55 us (0.984)
  Pallas kernels: 16.6 us -> 11.8 us
  waiting for transfers between devices: 17.2 us -> 19.8 us
  starting transfers between devices: 21.9 us -> 23.2 us
    pallas_call x9, Pallas kernels: 16.6 us -> 11.8 us  [the longest x1 4.13 us: project_first(): pl.pallas_call(on_device(project_first_body, group=group, targets=targets...]
    ppermute x15, waiting for transfers between devices: 17.2 us -> 19.8 us  [swap(): lax.ppermute(value, axis, [(i, i ^ mask) for i in range(lax.axis_size(axi...]
    ppermute x15, starting transfers between devices: 21.9 us -> 23.2 us  [swap(): lax.ppermute(value, axis, [(i, i ^ mask) for i in range(lax.axis_size(axi...]
  transfers between devices with their start and end apart: 15 -> 15, of which waited for: 6 -> 4; matrix products, arithmetic and copies ran while one was open for 0% -> 0% of each run, Pallas kernels for 23% -> 17%
where the time goes in v4:
time: 55 us; the launch traced here: 54.9 us
  starting transfers between devices  23.2 us (42%)
  waiting for transfers between devices  19.8 us (36%)
  Pallas kernels  11.8 us (21%)
    ppermute x15, starting transfers between devices, swap(): lax.ppermute(value, axis, [(i, i ^ mask) for i in range(lax.axis_size(axi...  23.2 us
    ppermute x15, waiting for transfers between devices, swap(): lax.ppermute(value, axis, [(i, i ^ mask) for i in range(lax.axis_size(axi...  19.8 us
    pallas_call x1, Pallas kernels, project_first(): pl.pallas_call(on_device(project_first_body, group=group, targets=targets...  4.13 us
    pallas_call x3, Pallas kernels, convolve_pair(): pl.pallas_call(on_device(convolve_pair_body, at=at, ahead=ahead, group=gr...  3.51 us
    pallas_call x3, Pallas kernels, project(): pl.pallas_call(on_device(project_body, blocks=blocks, group=group, places...  2.25 us
  transfers between devices with their start and end apart: 15, of which 4 were waited for; matrix products, arithmetic and copies ran while one was open for 0% of the time, Pallas kernels for 17%

profile of v4, /device:TPU:0, one launch (start us, length us, event | category | flops | bytes accessed | tf_op | source)
XLA Modules:
  0.0 54.9 jit_solution(10922224182817392133)
XLA Ops:
  0.0 0.0 copy-start
  0.0 3.0 %collective-permute-start.2 = (bf16[256,512]{1,0:T(8,128)(2,1)}, bf16[256,512]{1,0:T(8,128)(2,1)S(1)}, u32[]{:S(2)}, u32[]{:S(2)}) collective-permute-start(bf16[256,512]{1,0:T(8,128)(2,1)} %refs_0_.1), channel_id=1, source_target_pairs={{0,2},{1,3},{2,0},{3,1},{4,6},{5,7},{6,4},{7,5},{8,10},{9,11},{10,... | collective-permute-start | bytes 786440 | tf_op jit(solution)/shard_map/ppermute | solution.py:15
  3.0 0.0 collective-permute-start.4
  3.0 6.5 %collective-permute-done.2.refs_1_ = bf16[256,512]{1,0:T(8,128)(2,1)S(1)} collective-permute-done((bf16[256,512]{1,0:T(8,128)(2,1)}, bf16[256,512]{1,0:T(8,128)(2,1)S(1)}, u32[]{:S(2)}, u32[]{:S(2)}) %collective-permute-start.2) | collective-permute-done | bytes 262176 | tf_op jit(solution)/shard_map/ppermute | solution.py:15
  9.5 0.0 collective-permute-start.3
  9.5 2.8 %collective-permute-start = (f32[1,4,256]{2,1,0:T(4,128)}, f32[1,4,256]{2,1,0:T(4,128)S(1)}, u32[]{:S(2)}, u32[]{:S(2)}) collective-permute-start(f32[1,4,256]{2,1,0:T(4,128)} %bitcast.1), channel_id=1, source_target_pairs={{0,16},{4,20},{8,24},{12,28},{16,0},{20,4},{24,8},{28,12},{1,17},{... | collective-permute-start | bytes 12296 | tf_op jit(solution)/shard_map/ppermute | solution.py:15
  12.3 4.1 %project_first.1 = (f32[4,256,256]{2,1,0:T(8,128)S(1)}, f32[4,256,256]{2,1,0:T(8,128)S(1)}, bf16[3,4,512,512]{3,2,1,0:T(8,128)(2,1)S(1)}) custom-call(bf16[256,512]{1,0:T(8,128)(2,1)} %refs_0_.1, bf16[4,2048,512]{2,1,0:T(8,128)(2,1)} %refs_1_.1), custom_call_target="tpu_custom_call" | custom-call | flops 536870912 | bytes 8388608 | tf_op jit(solution)/shard_map/project_first/pallas_call | solution.py:77
  16.5 0.0 collective-permute-done
  16.5 0.0 copy-done
  16.5 0.0 collective-permute-done.4.refs_0_
  16.5 0.8 %shard_map.37.refs_2_ = f32[4,256,256]{2,1,0:T(8,128)S(1)} custom-call(bf16[256,512]{1,0:T(8,128)(2,1)S(1)} %collective-permute-done.4.refs_0_, bf16[256,512]{1,0:T(8,128)(2,1)S(1)} %collective-permute-done.2.refs_1_, bf16[3,4,512,512]{3,2,1,0:T(8,128)(2,1)S(1)} %get-tuple-element.22.refs_2_.refs_1_.refs_3_, f32[4,256,256]{2,1,0:T(8,128)S(1)} %get-tuple-element.23.refs_3_), custom_call_target="tpu_custom_call" | custom-call | flops 536870912 | bytes 2097152 | tf_op jit(solution)/shard_map/pallas_call | solution.py:140
  17.3 0.0 collective-permute-done.3.refs_0_.refs_2_
  17.3 0.5 shard_map.38
  17.8 1.5 %collective-permute-start.5 = (bf16[264,512]{1,0:T(8,128)(2,1)S(1)}, bf16[264,512]{1,0:T(8,128)(2,1)S(1)}, u32[]{:S(2)}, u32[]{:S(2)}) collective-permute-start(bf16[264,512]{1,0:T(8,128)(2,1)S(1)} %get-tuple-element.24), channel_id=1, source_target_pairs={{0,4},{4,0},{8,12},{12,8},{16,20},{20,16},{24,28},{28,24},{1,5},{5... | collective-permute-start | bytes 811016 | tf_op jit(solution)/shard_map/ppermute | solution.py:15
  19.3 1.6 %collective-permute-start.6 = (bf16[264,512]{1,0:T(8,128)(2,1)S(1)}, bf16[264,512]{1,0:T(8,128)(2,1)S(1)}, u32[]{:S(2)}, u32[]{:S(2)}) collective-permute-start(bf16[264,512]{1,0:T(8,128)(2,1)S(1)} %get-tuple-element.25), channel_id=1, source_target_pairs={{0,8},{4,12},{8,0},{12,4},{16,24},{20,28},{24,16},{28,20},{1,9},{5... | collective-permute-start | bytes 811016 | tf_op jit(solution)/shard_map/ppermute | solution.py:15
  20.9 1.0 %shard_map.39 = (bf16[256,512]{1,0:T(8,128)(2,1)S(1)}, bf16[256,512]{1,0:T(8,128)(2,1)S(1)}) custom-call(bf16[256,512]{1,0:T(8,128)(2,1)S(1)} %collective-permute-done.4.refs_0_, bf16[256,512]{1,0:T(8,128)(2,1)S(1)} %collective-permute-done.2.refs_1_, bf16[256,512]{1,0:T(8,128)(2,1)S(1)} %collective-permute-done.3.refs_0_.refs_2_, ...), custom_call_target="tpu_custom_call" | custom-call | flops 805306368 | bytes 3145728 | tf_op jit(solution)/shard_map/pallas_call | solution.py:140
  21.9 0.5 collective-permute-start.7
  22.4 2.5 %collective-permute-start.1 = (f32[2,4,256]{2,1,0:T(4,128)S(1)}, f32[2,4,256]{2,1,0:T(4,128)S(1)}, u32[]{:S(2)}, u32[]{:S(2)}) collective-permute-start(f32[2,4,256]{2,1,0:T(4,128)S(1)} %pad_maximum_fusion.refs_3_.refs_0_), channel_id=1, source_target_pairs={{0,12},{4,8},{8,4},{12,0},{16,28},{20,24},{24,20},{28,16},{1,13},{... | collective-permute-start | bytes 24584 | tf_op jit(solution)/shard_map/ppermute | solution.py:15
  24.9 8.5 %collective-permute-done.1.refs_1_ = f32[2,4,256]{2,1,0:T(4,128)S(1)} collective-permute-done((f32[2,4,256]{2,1,0:T(4,128)S(1)}, f32[2,4,256]{2,1,0:T(4,128)S(1)}, u32[]{:S(2)}, u32[]{:S(2)}) %collective-permute-start.1) | collective-permute-done | bytes 8224 | tf_op jit(solution)/shard_map/ppermute | solution.py:15
  33.4 0.0 collective-permute-done.5.refs_2_
  33.4 0.0 collective-permute-done.6.refs_3_.refs_1_
  33.4 1.1 %toeplitz.1.refs_0_ = bf16[3072,1024]{1,0:T(8,128)(2,1)S(1)} custom-call(f32[2,4,256]{2,1,0:T(4,128)S(1)} %pad_maximum_fusion.refs_3_.refs_0_, f32[2,4,256]{2,1,0:T(4,128)S(1)} %collective-permute-done.1.refs_1_, bf16[264,512]{1,0:T(8,128)(2,1)S(1)} %collective-permute-done.5.refs_2_, bf16[264,512]{1,0:T(8,128)(2,1)S(1)} %collective-permute-done.6.refs_3_.refs_1_), custom_call_target="tpu_custom_call" | custom-call | flops 16777216 | bytes 4194304 | tf_op jit(solution)/shard_map/toeplitz/pallas_call | solution.py:213
  34.5 1.6 %shard_map.40 = (f32[4,256,128]{2,1,0:T(8,128)S(1)}, f32[4,256,128]{2,1,0:T(8,128)S(1)}) custom-call(bf16[3072,1024]{1,0:T(8,128)(2,1)S(1)} %toeplitz.1.refs_0_, bf16[256,512]{1,0:T(8,128)(2,1)S(1)} %get-tuple-element.28.refs_1_, bf16[264,512]{1,0:T(8,128)(2,1)S(1)} %collective-permute-done.5.refs_2_), custom_call_target="tpu_custom_call" | custom-call | flops 1342177280 | bytes 524288 | tf_op jit(solution)/shard_map/pallas_call | solution.py:290
  36.1 0.0 collective-permute-done.7.refs_2_
  36.1 1.0 %shard_map.41 = (bf16[256,128]{1,0:T(8,128)(2,1)S(1)}, bf16[256,128]{1,0:T(8,128)(2,1)S(1)}, bf16[256,128]{1,0:T(8,128)(2,1)S(1)}, bf16[256,128]{1,0:T(8,128)(2,1)S(1)}) custom-call(bf16[3072,1024]{1,0:T(8,128)(2,1)S(1)} %toeplitz.1.refs_0_, bf16[264,512]{1,0:T(8,128)(2,1)S(1)} %collective-permute-done.6.refs_3_.refs_1_, ...), custom_call_target="tpu_custom_call" | custom-call | flops 671088640 | bytes 524288 | tf_op jit(solution)/shard_map/pallas_call | solution.py:290
  37.1 1.5 %collective-permute-start.8 = (bf16[256,128]{1,0:T(8,128)(2,1)S(1)}, bf16[256,128]{1,0:T(8,128)(2,1)S(1)}, u32[]{:S(2)}, u32[]{:S(2)}) collective-permute-start(bf16[256,128]{1,0:T(8,128)(2,1)S(1)} %get-tuple-element.31), channel_id=1, source_target_pairs={{0,4},{4,0},{8,12},{12,8},{16,20},{20,16},{24,28},{28,24},{1,5},{5... | collective-permute-start | bytes 196616 | tf_op jit(solution)/shard_map/ppermute | solution.py:15
  38.6 1.6 %collective-permute-start.9 = (bf16[256,128]{1,0:T(8,128)(2,1)S(1)}, bf16[256,128]{1,0:T(8,128)(2,1)S(1)}, u32[]{:S(2)}, u32[]{:S(2)}) collective-permute-start(bf16[256,128]{1,0:T(8,128)(2,1)S(1)} %get-tuple-element.32), channel_id=1, source_target_pairs={{0,8},{4,12},{8,0},{12,4},{16,24},{20,28},{24,16},{28,20},{1,9},{5... | collective-permute-start | bytes 196616 | tf_op jit(solution)/shard_map/ppermute | solution.py:15
  40.2 0.4 collective-permute-start.10
  40.6 0.9 %shard_map.42 = (bf16[256,128]{1,0:T(8,128)(2,1)S(1)}, bf16[256,128]{1,0:T(8,128)(2,1)S(1)}, bf16[256,128]{1,0:T(8,128)(2,1)S(1)}, bf16[256,128]{1,0:T(8,128)(2,1)S(1)}) custom-call(bf16[3072,1024]{1,0:T(8,128)(2,1)S(1)} %toeplitz.1.refs_0_, bf16[264,512]{1,0:T(8,128)(2,1)S(1)} %collective-permute-done.6.refs_3_.refs_1_, ...), custom_call_target="tpu_custom_call" | custom-call | flops 671088640 | bytes 524288 | tf_op jit(solution)/shard_map/pallas_call | solution.py:290
  41.6 0.3 collective-permute-start.11
  41.9 3.6 %collective-permute-start.12 = (bf16[256,128]{1,0:T(8,128)(2,1)S(1)}, bf16[256,128]{1,0:T(8,128)(2,1)S(1)}, u32[]{:S(2)}, u32[]{:S(2)}) collective-permute-start(bf16[256,128]{1,0:T(8,128)(2,1)S(1)} %get-tuple-element.36), channel_id=1, source_target_pairs={{0,20},{4,16},{8,28},{12,24},{16,4},{20,0},{24,12},{28,8},{1,21},{... | collective-permute-start | bytes 196616 | tf_op jit(solution)/shard_map/ppermute | solution.py:15
  45.5 0.0 collective-permute-done.8.refs_1_
  45.5 1.4 %collective-permute-start.13 = (bf16[256,128]{1,0:T(8,128)(2,1)S(1)}, bf16[256,128]{1,0:T(8,128)(2,1)S(1)}, u32[]{:S(2)}, u32[]{:S(2)}) collective-permute-start(bf16[256,128]{1,0:T(8,128)(2,1)S(1)} %get-tuple-element.37), channel_id=1, source_target_pairs={{0,24},{4,28},{8,16},{12,20},{16,8},{20,12},{24,0},{28,4},{1,25},{... | collective-permute-start | bytes 196616 | tf_op jit(solution)/shard_map/ppermute | solution.py:15
  46.9 0.0 collective-permute-done.9.refs_2_
  46.9 2.4 %collective-permute-start.14 = (bf16[256,128]{1,0:T(8,128)(2,1)S(1)}, bf16[256,128]{1,0:T(8,128)(2,1)S(1)}, u32[]{:S(2)}, u32[]{:S(2)}) collective-permute-start(bf16[256,128]{1,0:T(8,128)(2,1)S(1)} %get-tuple-element.38), channel_id=1, source_target_pairs={{0,28},{4,24},{8,20},{12,16},{16,12},{20,8},{24,4},{28,0},{1,29},{... | collective-permute-start | bytes 196616 | tf_op jit(solution)/shard_map/ppermute | solution.py:15
  49.3 0.0 collective-permute-done.10.refs_3_
  49.3 1.0 %collective-permute-done.11.refs_4_ = bf16[256,128]{1,0:T(8,128)(2,1)S(1)} collective-permute-done((bf16[256,128]{1,0:T(8,128)(2,1)S(1)}, bf16[256,128]{1,0:T(8,128)(2,1)S(1)}, u32[]{:S(2)}, u32[]{:S(2)}) %collective-permute-start.11) | collective-permute-done | bytes 65568 | tf_op jit(solution)/shard_map/ppermute | solution.py:15
  50.3 3.7 %collective-permute-done.12.refs_5_ = bf16[256,128]{1,0:T(8,128)(2,1)S(1)} collective-permute-done((bf16[256,128]{1,0:T(8,128)(2,1)S(1)}, bf16[256,128]{1,0:T(8,128)(2,1)S(1)}, u32[]{:S(2)}, u32[]{:S(2)}) %collective-permute-start.12) | collective-permute-done | bytes 65568 | tf_op jit(solution)/shard_map/ppermute | solution.py:15
  54.1 0.0 collective-permute-done.13.refs_6_
  54.1 0.0 collective-permute-done.14.refs_7_
  54.1 0.8 %finish.1 = bf16[256,512]{1,0:T(8,128)(2,1)} custom-call(bf16[256,128]{1,0:T(8,128)(2,1)S(1)} %get-tuple-element.30.refs_0_, bf16[256,128]{1,0:T(8,128)(2,1)S(1)} %collective-permute-done.8.refs_1_, bf16[256,128]{1,0:T(8,128)(2,1)S(1)} %collective-permute-done.9.refs_2_, bf16[256,128]{1,0:T(8,128)(2,1)S(1)} %collective-permute-done.10.refs_3_, ...), custom_call_target="tpu_custom_call" | custom-call | tf_op jit(solution)/shard_map/finish/pallas_call | solution.py:378
  (1 shorter events, 0.0 us)
Async XLA Ops:
  0.0 16.5 %copy-start = (f32[4,256]{1,0:T(4,128)S(1)}, f32[4,256]{1,0:T(4,128)}, u32[]{:S(2)}) copy-start(f32[4,256]{1,0:T(4,128)} %param.5) | copy-start | bytes 12292
  0.0 9.5 %collective-permute-start.2 = (bf16[256,512]{1,0:T(8,128)(2,1)}, bf16[256,512]{1,0:T(8,128)(2,1)S(1)}, u32[]{:S(2)}, u32[]{:S(2)}) collective-permute-start(bf16[256,512]{1,0:T(8,128)(2,1)} %refs_0_.1), channel_id=1, source_target_pairs={{0,2},{1,3},{2,0},{3,1},{4,6},{5,7},{6,4},{7,5},{8,10},{9,11},{10,... | collective-permute-start | bytes 786440 | tf_op jit(solution)/shard_map/ppermute | solution.py:15
  3.0 13.5 %collective-permute-start.4 = (bf16[256,512]{1,0:T(8,128)(2,1)}, bf16[256,512]{1,0:T(8,128)(2,1)S(1)}, u32[]{:S(2)}, u32[]{:S(2)}) collective-permute-start(bf16[256,512]{1,0:T(8,128)(2,1)} %refs_0_.1), channel_id=1, source_target_pairs={{0,1},{1,0},{2,3},{3,2},{4,5},{5,4},{6,7},{7,6},{8,9},{9,8},{10,11... | collective-permute-start | bytes 786440 | tf_op jit(solution)/shard_map/ppermute | solution.py:15
  9.5 7.8 %collective-permute-start.3 = (bf16[256,512]{1,0:T(8,128)(2,1)S(1)}, bf16[256,512]{1,0:T(8,128)(2,1)S(1)}, u32[]{:S(2)}, u32[]{:S(2)}) collective-permute-start(bf16[256,512]{1,0:T(8,128)(2,1)S(1)} %collective-permute-done.2.refs_1_), channel_id=1, source_target_pairs={{0,1},{1,0},{2,3},{3,2},{4,5},{5,4},{6,7},{7,6},{8,9},{9,8},{10,11... | collective-permute-start | bytes 786440 | tf_op jit(solution)/shard_map/ppermute | solution.py:15
  9.5 7.0 %collective-permute-start = (f32[1,4,256]{2,1,0:T(4,128)}, f32[1,4,256]{2,1,0:T(4,128)S(1)}, u32[]{:S(2)}, u32[]{:S(2)}) collective-permute-start(f32[1,4,256]{2,1,0:T(4,128)} %bitcast.1), channel_id=1, source_target_pairs={{0,16},{4,20},{8,24},{12,28},{16,0},{20,4},{24,8},{28,12},{1,17},{... | collective-permute-start | bytes 12296 | tf_op jit(solution)/shard_map/ppermute | solution.py:15
  17.8 15.7 %collective-permute-start.5 = (bf16[264,512]{1,0:T(8,128)(2,1)S(1)}, bf16[264,512]{1,0:T(8,128)(2,1)S(1)}, u32[]{:S(2)}, u32[]{:S(2)}) collective-permute-start(bf16[264,512]{1,0:T(8,128)(2,1)S(1)} %get-tuple-element.24), channel_id=1, source_target_pairs={{0,4},{4,0},{8,12},{12,8},{16,20},{20,16},{24,28},{28,24},{1,5},{5... | collective-permute-start | bytes 811016 | tf_op jit(solution)/shard_map/ppermute | solution.py:15
  19.3 14.1 %collective-permute-start.6 = (bf16[264,512]{1,0:T(8,128)(2,1)S(1)}, bf16[264,512]{1,0:T(8,128)(2,1)S(1)}, u32[]{:S(2)}, u32[]{:S(2)}) collective-permute-start(bf16[264,512]{1,0:T(8,128)(2,1)S(1)} %get-tuple-element.25), channel_id=1, source_target_pairs={{0,8},{4,12},{8,0},{12,4},{16,24},{20,28},{24,16},{28,20},{1,9},{5... | collective-permute-start | bytes 811016 | tf_op jit(solution)/shard_map/ppermute | solution.py:15
  21.9 14.2 %collective-permute-start.7 = (bf16[256,512]{1,0:T(8,128)(2,1)S(1)}, bf16[256,512]{1,0:T(8,128)(2,1)S(1)}, u32[]{:S(2)}, u32[]{:S(2)}) collective-permute-start(bf16[256,512]{1,0:T(8,128)(2,1)S(1)} %get-tuple-element.27), channel_id=1, source_target_pairs={{0,12},{4,8},{8,4},{12,0},{16,28},{20,24},{24,20},{28,16},{1,13},{... | collective-permute-start | bytes 786440 | tf_op jit(solution)/shard_map/ppermute | solution.py:15
  22.4 11.0 %collective-permute-start.1 = (f32[2,4,256]{2,1,0:T(4,128)S(1)}, f32[2,4,256]{2,1,0:T(4,128)S(1)}, u32[]{:S(2)}, u32[]{:S(2)}) collective-permute-start(f32[2,4,256]{2,1,0:T(4,128)S(1)} %pad_maximum_fusion.refs_3_.refs_0_), channel_id=1, source_target_pairs={{0,12},{4,8},{8,4},{12,0},{16,28},{20,24},{24,20},{28,16},{1,13},{... | collective-permute-start | bytes 24584 | tf_op jit(solution)/shard_map/ppermute | solution.py:15
  37.1 8.4 %collective-permute-start.8 = (bf16[256,128]{1,0:T(8,128)(2,1)S(1)}, bf16[256,128]{1,0:T(8,128)(2,1)S(1)}, u32[]{:S(2)}, u32[]{:S(2)}) collective-permute-start(bf16[256,128]{1,0:T(8,128)(2,1)S(1)} %get-tuple-element.31), channel_id=1, source_target_pairs={{0,4},{4,0},{8,12},{12,8},{16,20},{20,16},{24,28},{28,24},{1,5},{5... | collective-permute-start | bytes 196616 | tf_op jit(solution)/shard_map/ppermute | solution.py:15
  38.6 8.3 %collective-permute-start.9 = (bf16[256,128]{1,0:T(8,128)(2,1)S(1)}, bf16[256,128]{1,0:T(8,128)(2,1)S(1)}, u32[]{:S(2)}, u32[]{:S(2)}) collective-permute-start(bf16[256,128]{1,0:T(8,128)(2,1)S(1)} %get-tuple-element.32), channel_id=1, source_target_pairs={{0,8},{4,12},{8,0},{12,4},{16,24},{20,28},{24,16},{28,20},{1,9},{5... | collective-permute-start | bytes 196616 | tf_op jit(solution)/shard_map/ppermute | solution.py:15
  40.2 9.1 %collective-permute-start.10 = (bf16[256,128]{1,0:T(8,128)(2,1)S(1)}, bf16[256,128]{1,0:T(8,128)(2,1)S(1)}, u32[]{:S(2)}, u32[]{:S(2)}) collective-permute-start(bf16[256,128]{1,0:T(8,128)(2,1)S(1)} %get-tuple-element.33), channel_id=1, source_target_pairs={{0,12},{4,8},{8,4},{12,0},{16,28},{20,24},{24,20},{28,16},{1,13},{... | collective-permute-start | bytes 196616 | tf_op jit(solution)/shard_map/ppermute | solution.py:15
  41.6 8.7 %collective-permute-start.11 = (bf16[256,128]{1,0:T(8,128)(2,1)S(1)}, bf16[256,128]{1,0:T(8,128)(2,1)S(1)}, u32[]{:S(2)}, u32[]{:S(2)}) collective-permute-start(bf16[256,128]{1,0:T(8,128)(2,1)S(1)} %get-tuple-element.35), channel_id=1, source_target_pairs={{0,16},{4,20},{8,24},{12,28},{16,0},{20,4},{24,8},{28,12},{1,17},{... | collective-permute-start | bytes 196616 | tf_op jit(solution)/shard_map/ppermute | solution.py:15
  41.9 12.1 %collective-permute-start.12 = (bf16[256,128]{1,0:T(8,128)(2,1)S(1)}, bf16[256,128]{1,0:T(8,128)(2,1)S(1)}, u32[]{:S(2)}, u32[]{:S(2)}) collective-permute-start(bf16[256,128]{1,0:T(8,128)(2,1)S(1)} %get-tuple-element.36), channel_id=1, source_target_pairs={{0,20},{4,16},{8,28},{12,24},{16,4},{20,0},{24,12},{28,8},{1,21},{... | collective-permute-start | bytes 196616 | tf_op jit(solution)/shard_map/ppermute | solution.py:15
  45.5 8.6 %collective-permute-start.13 = (bf16[256,128]{1,0:T(8,128)(2,1)S(1)}, bf16[256,128]{1,0:T(8,128)(2,1)S(1)}, u32[]{:S(2)}, u32[]{:S(2)}) collective-permute-start(bf16[256,128]{1,0:T(8,128)(2,1)S(1)} %get-tuple-element.37), channel_id=1, source_target_pairs={{0,24},{4,28},{8,16},{12,20},{16,8},{20,12},{24,0},{28,4},{1,25},{... | collective-permute-start | bytes 196616 | tf_op jit(solution)/shard_map/ppermute | solution.py:15
  46.9 7.2 %collective-permute-start.14 = (bf16[256,128]{1,0:T(8,128)(2,1)S(1)}, bf16[256,128]{1,0:T(8,128)(2,1)S(1)}, u32[]{:S(2)}, u32[]{:S(2)}) collective-permute-start(bf16[256,128]{1,0:T(8,128)(2,1)S(1)} %get-tuple-element.38), channel_id=1, source_target_pairs={{0,28},{4,24},{8,20},{12,16},{16,12},{20,8},{24,4},{28,0},{1,29},{... | collective-permute-start | bytes 196616 | tf_op jit(solution)/shard_map/ppermute | solution.py:15

commit v5 on v4

--- a/solution.py
+++ b/solution.py
@@ -303,6 +303,51 @@
     )(*args)
 
 
+def convolve_one_body(meta, table_ref, p_ref, *refs, m, ahead, group, width, sub, last):
+    count = len(ahead)
+    sum_refs, refs = refs[:count], refs[count:]
+    out_refs, (held, placed) = refs[:-2], refs[-2:]
+    place = meta[1]
+    for k in range(held.shape[0] // width):
+        held[k * width : (k + 1) * width, :] = p_ref[0:width, k * sub : (k + 1) * sub]
+    for i, far in enumerate(ahead):
+        start = (far + 1) * group - (place ^ m)
+        rows = table_ref[pl.ds(pl.multiple_of(start * width, width), group * width), :]
+        value = jnp.dot(rows, held[...], preferred_element_type=f32)
+        sums = [value[r * width : (r + 1) * width] + sum_refs[i][r] for r in range(group)]
+        if last:
+            store_parts(out_refs, placed, sums, place)
+        else:
+            for r, total in enumerate(sums):
+                out_refs[i][r] = total
+
+
+def convolve_one(table, part, befores, m, ahead, group, last):
+    _, width, sub = befores[0].shape
+    columns = table.shape[1]
+    vmem = pl.BlockSpec(memory_space=pltpu.VMEM)
+    if last:
+        out_shape = [jax.ShapeDtypeStruct((width, sub), bf16)] * group
+    else:
+        out_shape = [jax.ShapeDtypeStruct(before.shape, f32) for before in befores]
+    args = [table, part, *befores]
+    return pl.pallas_call(
+        on_device(
+            convolve_one_body, m=m, ahead=ahead, group=group, width=width, sub=sub, last=last
+        ),
+        in_specs=[vmem] * len(args),
+        out_specs=[vmem] * len(out_shape),
+        out_shape=out_shape,
+        scratch_shapes=[pltpu.VMEM((columns, sub), bf16), pltpu.VMEM((group, width, sub), bf16)],
+        compiler_params=params(32, 0),
+        cost_estimate=pl.CostEstimate(
+            flops=2 * len(ahead) * group * width * columns * sub,
+            bytes_accessed=2 * width * columns,
+            transcendentals=0,
+        ),
+    )(*args)
+
+
 def convolve_all_body(meta, low_ref, high_ref, *refs, group, sub):
     p_refs, out_refs, (held, placed) = refs[:group], refs[group : 2 * group], refs[2 * group :]
     width = p_refs[0].shape[0]
@@ -421,10 +466,10 @@
     table = toeplitz(pieces, far_pieces, parts[1:3], order, group)
 
     if groups == 2 and group == 4:
-        sides = [[parts[0], parts[1]], [parts[2], parts[3]]]
-        own, after = convolve_pair(table, sides[0], None, 0, (0, 1), group)
-        after = convolve_pair(table, sides[1], after, 1, (1,), group)
-        own = convolve_pair(table, sides[1], own, 1, (0,), group)
+        sums = convolve_pair(table, parts[:2], None, 0, (0, 1), group)
+        own, after = convolve_one(table, parts[2], sums, 2, (0, 1), group, False)
+        after = convolve_one(table, parts[3], [after], 3, (1,), group, True)
+        own = convolve_one(table, parts[3], [own], 3, (0,), group, True)
         ahead = {1: after}
     else:
         every = convolve_all(table, [parts[m] for m in range(group)], group)

time: 55 us -> 55.9 us (1.016)
  Pallas kernels: 11.8 us -> 12.7 us
    pallas_call x0 -> x3, Pallas kernels: none -> 2.82 us  [convolve_one(): pl.pallas_call(on_device(convolve_one_body, m=m, ahead=ahead, group=group...]
    pallas_call x3 -> x1, Pallas kernels: 3.51 us -> 1.61 us  [convolve_pair(): pl.pallas_call(on_device(convolve_pair_body, at=at, ahead=ahead, group=gr...]
  transfers between devices with their start and end apart: 15 -> 15, of which waited for: 4 -> 4; matrix products, arithmetic and copies ran while one was open for 0% -> 0% of each run, Pallas kernels for 17% -> 19%
where the time goes in v5:
time: 55.9 us; the launch traced here: 55.8 us
  starting transfers between devices  23.2 us (42%)
  waiting for transfers between devices  19.8 us (35%)
  Pallas kernels  12.7 us (23%)
    ppermute x15, starting transfers between devices, swap(): lax.ppermute(value, axis, [(i, i ^ mask) for i in range(lax.axis_size(axi...  23.2 us
    ppermute x15, waiting for transfers between devices, swap(): lax.ppermute(value, axis, [(i, i ^ mask) for i in range(lax.axis_size(axi...  19.8 us
    pallas_call x1, Pallas kernels, project_first(): pl.pallas_call(on_device(project_first_body, group=group, targets=targets...  4.13 us
    pallas_call x3, Pallas kernels, convolve_one(): pl.pallas_call(on_device(convolve_one_body, m=m, ahead=ahead, group=group...  2.82 us
    pallas_call x3, Pallas kernels, project(): pl.pallas_call(on_device(project_body, blocks=blocks, group=group, places...  2.25 us
    pallas_call x1, Pallas kernels, convolve_pair(): pl.pallas_call(on_device(convolve_pair_body, at=at, ahead=ahead, group=gr...  1.61 us
  transfers between devices with their start and end apart: 15, of which 4 were waited for; matrix products, arithmetic and copies ran while one was open for 0% of the time, Pallas kernels for 19%

profile of v5, /device:TPU:0, one launch (start us, length us, event | category | flops | bytes accessed | tf_op | source)
XLA Modules:
  0.0 55.8 jit_solution(16275203134455024244)
XLA Ops:
  0.0 0.0 copy-start
  0.0 3.0 %collective-permute-start.2 = (bf16[256,512]{1,0:T(8,128)(2,1)}, bf16[256,512]{1,0:T(8,128)(2,1)S(1)}, u32[]{:S(2)}, u32[]{:S(2)}) collective-permute-start(bf16[256,512]{1,0:T(8,128)(2,1)} %refs_0_.1), channel_id=1, source_target_pairs={{0,2},{1,3},{2,0},{3,1},{4,6},{5,7},{6,4},{7,5},{8,10},{9,11},{10,... | collective-permute-start | bytes 786440 | tf_op jit(solution)/shard_map/ppermute | solution.py:15
  3.0 0.0 collective-permute-start.4
  3.0 6.5 %collective-permute-done.2.refs_1_ = bf16[256,512]{1,0:T(8,128)(2,1)S(1)} collective-permute-done((bf16[256,512]{1,0:T(8,128)(2,1)}, bf16[256,512]{1,0:T(8,128)(2,1)S(1)}, u32[]{:S(2)}, u32[]{:S(2)}) %collective-permute-start.2) | collective-permute-done | bytes 262176 | tf_op jit(solution)/shard_map/ppermute | solution.py:15
  9.5 0.0 collective-permute-start.3
  9.5 2.8 %collective-permute-start = (f32[1,4,256]{2,1,0:T(4,128)}, f32[1,4,256]{2,1,0:T(4,128)S(1)}, u32[]{:S(2)}, u32[]{:S(2)}) collective-permute-start(f32[1,4,256]{2,1,0:T(4,128)} %bitcast.1), channel_id=1, source_target_pairs={{0,16},{4,20},{8,24},{12,28},{16,0},{20,4},{24,8},{28,12},{1,17},{... | collective-permute-start | bytes 12296 | tf_op jit(solution)/shard_map/ppermute | solution.py:15
  12.3 4.1 %project_first.1 = (f32[4,256,256]{2,1,0:T(8,128)S(1)}, f32[4,256,256]{2,1,0:T(8,128)S(1)}, bf16[3,4,512,512]{3,2,1,0:T(8,128)(2,1)S(1)}) custom-call(bf16[256,512]{1,0:T(8,128)(2,1)} %refs_0_.1, bf16[4,2048,512]{2,1,0:T(8,128)(2,1)} %refs_1_.1), custom_call_target="tpu_custom_call" | custom-call | flops 536870912 | bytes 8388608 | tf_op jit(solution)/shard_map/project_first/pallas_call | solution.py:77
  16.5 0.0 collective-permute-done
  16.5 0.0 copy-done
  16.5 0.0 collective-permute-done.4.refs_0_
  16.5 0.8 %shard_map.37.refs_2_ = f32[4,256,256]{2,1,0:T(8,128)S(1)} custom-call(bf16[256,512]{1,0:T(8,128)(2,1)S(1)} %collective-permute-done.4.refs_0_, bf16[256,512]{1,0:T(8,128)(2,1)S(1)} %collective-permute-done.2.refs_1_, bf16[3,4,512,512]{3,2,1,0:T(8,128)(2,1)S(1)} %get-tuple-element.24.refs_2_.refs_1_.refs_3_, f32[4,256,256]{2,1,0:T(8,128)S(1)} %get-tuple-element.25.refs_3_), custom_call_target="tpu_custom_call" | custom-call | flops 536870912 | bytes 2097152 | tf_op jit(solution)/shard_map/pallas_call | solution.py:140
  17.3 0.0 collective-permute-done.3.refs_0_.refs_2_
  17.3 0.5 shard_map.38
  17.8 1.5 %collective-permute-start.5 = (bf16[264,512]{1,0:T(8,128)(2,1)S(1)}, bf16[264,512]{1,0:T(8,128)(2,1)S(1)}, u32[]{:S(2)}, u32[]{:S(2)}) collective-permute-start(bf16[264,512]{1,0:T(8,128)(2,1)S(1)} %get-tuple-element.26), channel_id=1, source_target_pairs={{0,4},{4,0},{8,12},{12,8},{16,20},{20,16},{24,28},{28,24},{1,5},{5... | collective-permute-start | bytes 811016 | tf_op jit(solution)/shard_map/ppermute | solution.py:15
  19.3 1.6 %collective-permute-start.6 = (bf16[264,512]{1,0:T(8,128)(2,1)S(1)}, bf16[264,512]{1,0:T(8,128)(2,1)S(1)}, u32[]{:S(2)}, u32[]{:S(2)}) collective-permute-start(bf16[264,512]{1,0:T(8,128)(2,1)S(1)} %get-tuple-element.27), channel_id=1, source_target_pairs={{0,8},{4,12},{8,0},{12,4},{16,24},{20,28},{24,16},{28,20},{1,9},{5... | collective-permute-start | bytes 811016 | tf_op jit(solution)/shard_map/ppermute | solution.py:15
  20.9 1.0 %shard_map.39 = (bf16[256,512]{1,0:T(8,128)(2,1)S(1)}, bf16[256,512]{1,0:T(8,128)(2,1)S(1)}) custom-call(bf16[256,512]{1,0:T(8,128)(2,1)S(1)} %collective-permute-done.4.refs_0_, bf16[256,512]{1,0:T(8,128)(2,1)S(1)} %collective-permute-done.2.refs_1_, bf16[256,512]{1,0:T(8,128)(2,1)S(1)} %collective-permute-done.3.refs_0_.refs_2_, ...), custom_call_target="tpu_custom_call" | custom-call | flops 805306368 | bytes 3145728 | tf_op jit(solution)/shard_map/pallas_call | solution.py:140
  21.9 0.5 collective-permute-start.7
  22.4 2.5 %collective-permute-start.1 = (f32[2,4,256]{2,1,0:T(4,128)S(1)}, f32[2,4,256]{2,1,0:T(4,128)S(1)}, u32[]{:S(2)}, u32[]{:S(2)}) collective-permute-start(f32[2,4,256]{2,1,0:T(4,128)S(1)} %pad_maximum_fusion.refs_3_.refs_0_), channel_id=1, source_target_pairs={{0,12},{4,8},{8,4},{12,0},{16,28},{20,24},{24,20},{28,16},{1,13},{... | collective-permute-start | bytes 24584 | tf_op jit(solution)/shard_map/ppermute | solution.py:15
  24.9 8.5 %collective-permute-done.1.refs_1_ = f32[2,4,256]{2,1,0:T(4,128)S(1)} collective-permute-done((f32[2,4,256]{2,1,0:T(4,128)S(1)}, f32[2,4,256]{2,1,0:T(4,128)S(1)}, u32[]{:S(2)}, u32[]{:S(2)}) %collective-permute-start.1) | collective-permute-done | bytes 8224 | tf_op jit(solution)/shard_map/ppermute | solution.py:15
  33.4 0.0 collective-permute-done.5.refs_2_
  33.4 0.0 collective-permute-done.6.refs_3_.refs_1_
  33.4 1.1 %toeplitz.1.refs_0_ = bf16[3072,1024]{1,0:T(8,128)(2,1)S(1)} custom-call(f32[2,4,256]{2,1,0:T(4,128)S(1)} %pad_maximum_fusion.refs_3_.refs_0_, f32[2,4,256]{2,1,0:T(4,128)S(1)} %collective-permute-done.1.refs_1_, bf16[264,512]{1,0:T(8,128)(2,1)S(1)} %collective-permute-done.5.refs_2_, bf16[264,512]{1,0:T(8,128)(2,1)S(1)} %collective-permute-done.6.refs_3_.refs_1_), custom_call_target="tpu_custom_call" | custom-call | flops 16777216 | bytes 4194304 | tf_op jit(solution)/shard_map/toeplitz/pallas_call | solution.py:213
  34.5 1.6 %shard_map.40 = (f32[4,256,128]{2,1,0:T(8,128)S(1)}, f32[4,256,128]{2,1,0:T(8,128)S(1)}) custom-call(bf16[3072,1024]{1,0:T(8,128)(2,1)S(1)} %toeplitz.1.refs_0_, bf16[256,512]{1,0:T(8,128)(2,1)S(1)} %get-tuple-element.30.refs_1_, bf16[264,512]{1,0:T(8,128)(2,1)S(1)} %collective-permute-done.5.refs_2_), custom_call_target="tpu_custom_call" | custom-call | flops 1342177280 | bytes 524288 | tf_op jit(solution)/shard_map/pallas_call | solution.py:290
  36.1 1.3 %shard_map.41 = (f32[4,256,128]{2,1,0:T(8,128)S(1)}, f32[4,256,128]{2,1,0:T(8,128)S(1)}) custom-call(bf16[3072,1024]{1,0:T(8,128)(2,1)S(1)} %toeplitz.1.refs_0_, bf16[264,512]{1,0:T(8,128)(2,1)S(1)} %collective-permute-done.6.refs_3_.refs_1_, f32[4,256,128]{2,1,0:T(8,128)S(1)} %get-tuple-element.31.refs_2_, f32[4,256,128]{2,1,0:T(8,128)S(1)} %get-tuple-element.32.refs_3_), custom_call_target="tpu_custom_call" | custom-call | flops 536870912 | bytes 524288 | tf_op jit(solution)/shard_map/pallas_call | solution.py:334
  37.4 0.0 collective-permute-done.7.refs_1_
  37.4 0.8 %shard_map.42 = (bf16[256,128]{1,0:T(8,128)(2,1)S(1)}, bf16[256,128]{1,0:T(8,128)(2,1)S(1)}, bf16[256,128]{1,0:T(8,128)(2,1)S(1)}, bf16[256,128]{1,0:T(8,128)(2,1)S(1)}) custom-call(bf16[3072,1024]{1,0:T(8,128)(2,1)S(1)} %toeplitz.1.refs_0_, bf16[256,512]{1,0:T(8,128)(2,1)S(1)} %collective-permute-done.7.refs_1_, f32[4,256,128]{2,1,0:T(8,128)S(1)} %get-tuple-element.33.refs_2_), custom_call_target="tpu_custom_call" | custom-call | flops 268435456 | bytes 524288 | tf_op jit(solution)/shard_map/pallas_call | solution.py:334
  38.2 1.5 %collective-permute-start.8 = (bf16[256,128]{1,0:T(8,128)(2,1)S(1)}, bf16[256,128]{1,0:T(8,128)(2,1)S(1)}, u32[]{:S(2)}, u32[]{:S(2)}) collective-permute-start(bf16[256,128]{1,0:T(8,128)(2,1)S(1)} %get-tuple-element.35), channel_id=1, source_target_pairs={{0,4},{4,0},{8,12},{12,8},{16,20},{20,16},{24,28},{28,24},{1,5},{5... | collective-permute-start | bytes 196616 | tf_op jit(solution)/shard_map/ppermute | solution.py:15
  39.7 1.6 %collective-permute-start.9 = (bf16[256,128]{1,0:T(8,128)(2,1)S(1)}, bf16[256,128]{1,0:T(8,128)(2,1)S(1)}, u32[]{:S(2)}, u32[]{:S(2)}) collective-permute-start(bf16[256,128]{1,0:T(8,128)(2,1)S(1)} %get-tuple-element.36), channel_id=1, source_target_pairs={{0,8},{4,12},{8,0},{12,4},{16,24},{20,28},{24,16},{28,20},{1,9},{5... | collective-permute-start | bytes 196616 | tf_op jit(solution)/shard_map/ppermute | solution.py:15
  41.3 0.4 collective-permute-start.10
  41.8 0.8 %shard_map.43 = (bf16[256,128]{1,0:T(8,128)(2,1)S(1)}, bf16[256,128]{1,0:T(8,128)(2,1)S(1)}, bf16[256,128]{1,0:T(8,128)(2,1)S(1)}, bf16[256,128]{1,0:T(8,128)(2,1)S(1)}) custom-call(bf16[3072,1024]{1,0:T(8,128)(2,1)S(1)} %toeplitz.1.refs_0_, bf16[256,512]{1,0:T(8,128)(2,1)S(1)} %collective-permute-done.7.refs_1_, f32[4,256,128]{2,1,0:T(8,128)S(1)} %get-tuple-element.38.refs_2_), custom_call_target="tpu_custom_call" | custom-call | flops 268435456 | bytes 524288 | tf_op jit(solution)/shard_map/pallas_call | solution.py:334
  42.5 0.3 collective-permute-start.11
  42.9 3.6 %collective-permute-start.12 = (bf16[256,128]{1,0:T(8,128)(2,1)S(1)}, bf16[256,128]{1,0:T(8,128)(2,1)S(1)}, u32[]{:S(2)}, u32[]{:S(2)}) collective-permute-start(bf16[256,128]{1,0:T(8,128)(2,1)S(1)} %get-tuple-element.40), channel_id=1, source_target_pairs={{0,20},{4,16},{8,28},{12,24},{16,4},{20,0},{24,12},{28,8},{1,21},{... | collective-permute-start | bytes 196616 | tf_op jit(solution)/shard_map/ppermute | solution.py:15
  46.4 0.0 collective-permute-done.8.refs_1_
  46.4 1.4 %collective-permute-start.13 = (bf16[256,128]{1,0:T(8,128)(2,1)S(1)}, bf16[256,128]{1,0:T(8,128)(2,1)S(1)}, u32[]{:S(2)}, u32[]{:S(2)}) collective-permute-start(bf16[256,128]{1,0:T(8,128)(2,1)S(1)} %get-tuple-element.41), channel_id=1, source_target_pairs={{0,24},{4,28},{8,16},{12,20},{16,8},{20,12},{24,0},{28,4},{1,25},{... | collective-permute-start | bytes 196616 | tf_op jit(solution)/shard_map/ppermute | solution.py:15
  47.8 0.0 collective-permute-done.9.refs_2_
  47.8 2.4 %collective-permute-start.14 = (bf16[256,128]{1,0:T(8,128)(2,1)S(1)}, bf16[256,128]{1,0:T(8,128)(2,1)S(1)}, u32[]{:S(2)}, u32[]{:S(2)}) collective-permute-start(bf16[256,128]{1,0:T(8,128)(2,1)S(1)} %get-tuple-element.42), channel_id=1, source_target_pairs={{0,28},{4,24},{8,20},{12,16},{16,12},{20,8},{24,4},{28,0},{1,29},{... | collective-permute-start | bytes 196616 | tf_op jit(solution)/shard_map/ppermute | solution.py:15
  50.3 0.0 collective-permute-done.10.refs_3_
  50.3 1.0 %collective-permute-done.11.refs_4_ = bf16[256,128]{1,0:T(8,128)(2,1)S(1)} collective-permute-done((bf16[256,128]{1,0:T(8,128)(2,1)S(1)}, bf16[256,128]{1,0:T(8,128)(2,1)S(1)}, u32[]{:S(2)}, u32[]{:S(2)}) %collective-permute-start.11) | collective-permute-done | bytes 65568 | tf_op jit(solution)/shard_map/ppermute | solution.py:15
  51.3 3.7 %collective-permute-done.12.refs_5_ = bf16[256,128]{1,0:T(8,128)(2,1)S(1)} collective-permute-done((bf16[256,128]{1,0:T(8,128)(2,1)S(1)}, bf16[256,128]{1,0:T(8,128)(2,1)S(1)}, u32[]{:S(2)}, u32[]{:S(2)}) %collective-permute-start.12) | collective-permute-done | bytes 65568 | tf_op jit(solution)/shard_map/ppermute | solution.py:15
  55.0 0.0 collective-permute-done.13.refs_6_
  55.0 0.0 collective-permute-done.14.refs_7_
  55.0 0.8 %finish.1 = bf16[256,512]{1,0:T(8,128)(2,1)} custom-call(bf16[256,128]{1,0:T(8,128)(2,1)S(1)} %get-tuple-element.34.refs_0_, bf16[256,128]{1,0:T(8,128)(2,1)S(1)} %collective-permute-done.8.refs_1_, bf16[256,128]{1,0:T(8,128)(2,1)S(1)} %collective-permute-done.9.refs_2_, bf16[256,128]{1,0:T(8,128)(2,1)S(1)} %collective-permute-done.10.refs_3_, ...), custom_call_target="tpu_custom_call" | custom-call | tf_op jit(solution)/shard_map/finish/pallas_call | solution.py:423
  (1 shorter events, 0.0 us)
Async XLA Ops:
  0.0 16.5 %copy-start = (f32[4,256]{1,0:T(4,128)S(1)}, f32[4,256]{1,0:T(4,128)}, u32[]{:S(2)}) copy-start(f32[4,256]{1,0:T(4,128)} %param.5) | copy-start | bytes 12292
  0.0 9.5 %collective-permute-start.2 = (bf16[256,512]{1,0:T(8,128)(2,1)}, bf16[256,512]{1,0:T(8,128)(2,1)S(1)}, u32[]{:S(2)}, u32[]{:S(2)}) collective-permute-start(bf16[256,512]{1,0:T(8,128)(2,1)} %refs_0_.1), channel_id=1, source_target_pairs={{0,2},{1,3},{2,0},{3,1},{4,6},{5,7},{6,4},{7,5},{8,10},{9,11},{10,... | collective-permute-start | bytes 786440 | tf_op jit(solution)/shard_map/ppermute | solution.py:15
  3.0 13.5 %collective-permute-start.4 = (bf16[256,512]{1,0:T(8,128)(2,1)}, bf16[256,512]{1,0:T(8,128)(2,1)S(1)}, u32[]{:S(2)}, u32[]{:S(2)}) collective-permute-start(bf16[256,512]{1,0:T(8,128)(2,1)} %refs_0_.1), channel_id=1, source_target_pairs={{0,1},{1,0},{2,3},{3,2},{4,5},{5,4},{6,7},{7,6},{8,9},{9,8},{10,11... | collective-permute-start | bytes 786440 | tf_op jit(solution)/shard_map/ppermute | solution.py:15
  9.5 7.8 %collective-permute-start.3 = (bf16[256,512]{1,0:T(8,128)(2,1)S(1)}, bf16[256,512]{1,0:T(8,128)(2,1)S(1)}, u32[]{:S(2)}, u32[]{:S(2)}) collective-permute-start(bf16[256,512]{1,0:T(8,128)(2,1)S(1)} %collective-permute-done.2.refs_1_), channel_id=1, source_target_pairs={{0,1},{1,0},{2,3},{3,2},{4,5},{5,4},{6,7},{7,6},{8,9},{9,8},{10,11... | collective-permute-start | bytes 786440 | tf_op jit(solution)/shard_map/ppermute | solution.py:15
  9.5 7.0 %collective-permute-start = (f32[1,4,256]{2,1,0:T(4,128)}, f32[1,4,256]{2,1,0:T(4,128)S(1)}, u32[]{:S(2)}, u32[]{:S(2)}) collective-permute-start(f32[1,4,256]{2,1,0:T(4,128)} %bitcast.1), channel_id=1, source_target_pairs={{0,16},{4,20},{8,24},{12,28},{16,0},{20,4},{24,8},{28,12},{1,17},{... | collective-permute-start | bytes 12296 | tf_op jit(solution)/shard_map/ppermute | solution.py:15
  17.8 15.7 %collective-permute-start.5 = (bf16[264,512]{1,0:T(8,128)(2,1)S(1)}, bf16[264,512]{1,0:T(8,128)(2,1)S(1)}, u32[]{:S(2)}, u32[]{:S(2)}) collective-permute-start(bf16[264,512]{1,0:T(8,128)(2,1)S(1)} %get-tuple-element.26), channel_id=1, source_target_pairs={{0,4},{4,0},{8,12},{12,8},{16,20},{20,16},{24,28},{28,24},{1,5},{5... | collective-permute-start | bytes 811016 | tf_op jit(solution)/shard_map/ppermute | solution.py:15
  19.3 14.1 %collective-permute-start.6 = (bf16[264,512]{1,0:T(8,128)(2,1)S(1)}, bf16[264,512]{1,0:T(8,128)(2,1)S(1)}, u32[]{:S(2)}, u32[]{:S(2)}) collective-permute-start(bf16[264,512]{1,0:T(8,128)(2,1)S(1)} %get-tuple-element.27), channel_id=1, source_target_pairs={{0,8},{4,12},{8,0},{12,4},{16,24},{20,28},{24,16},{28,20},{1,9},{5... | collective-permute-start | bytes 811016 | tf_op jit(solution)/shard_map/ppermute | solution.py:15
  21.9 15.5 %collective-permute-start.7 = (bf16[256,512]{1,0:T(8,128)(2,1)S(1)}, bf16[256,512]{1,0:T(8,128)(2,1)S(1)}, u32[]{:S(2)}, u32[]{:S(2)}) collective-permute-start(bf16[256,512]{1,0:T(8,128)(2,1)S(1)} %get-tuple-element.29), channel_id=1, source_target_pairs={{0,12},{4,8},{8,4},{12,0},{16,28},{20,24},{24,20},{28,16},{1,13},{... | collective-permute-start | bytes 786440 | tf_op jit(solution)/shard_map/ppermute | solution.py:15
  22.4 11.0 %collective-permute-start.1 = (f32[2,4,256]{2,1,0:T(4,128)S(1)}, f32[2,4,256]{2,1,0:T(4,128)S(1)}, u32[]{:S(2)}, u32[]{:S(2)}) collective-permute-start(f32[2,4,256]{2,1,0:T(4,128)S(1)} %pad_maximum_fusion.refs_3_.refs_0_), channel_id=1, source_target_pairs={{0,12},{4,8},{8,4},{12,0},{16,28},{20,24},{24,20},{28,16},{1,13},{... | collective-permute-start | bytes 24584 | tf_op jit(solution)/shard_map/ppermute | solution.py:15
  38.2 8.2 %collective-permute-start.8 = (bf16[256,128]{1,0:T(8,128)(2,1)S(1)}, bf16[256,128]{1,0:T(8,128)(2,1)S(1)}, u32[]{:S(2)}, u32[]{:S(2)}) collective-permute-start(bf16[256,128]{1,0:T(8,128)(2,1)S(1)} %get-tuple-element.35), channel_id=1, source_target_pairs={{0,4},{4,0},{8,12},{12,8},{16,20},{20,16},{24,28},{28,24},{1,5},{5... | collective-permute-start | bytes 196616 | tf_op jit(solution)/shard_map/ppermute | solution.py:15
  39.7 8.1 %collective-permute-start.9 = (bf16[256,128]{1,0:T(8,128)(2,1)S(1)}, bf16[256,128]{1,0:T(8,128)(2,1)S(1)}, u32[]{:S(2)}, u32[]{:S(2)}) collective-permute-start(bf16[256,128]{1,0:T(8,128)(2,1)S(1)} %get-tuple-element.36), channel_id=1, source_target_pairs={{0,8},{4,12},{8,0},{12,4},{16,24},{20,28},{24,16},{28,20},{1,9},{5... | collective-permute-start | bytes 196616 | tf_op jit(solution)/shard_map/ppermute | solution.py:15
  41.3 8.9 %collective-permute-start.10 = (bf16[256,128]{1,0:T(8,128)(2,1)S(1)}, bf16[256,128]{1,0:T(8,128)(2,1)S(1)}, u32[]{:S(2)}, u32[]{:S(2)}) collective-permute-start(bf16[256,128]{1,0:T(8,128)(2,1)S(1)} %get-tuple-element.37), channel_id=1, source_target_pairs={{0,12},{4,8},{8,4},{12,0},{16,28},{20,24},{24,20},{28,16},{1,13},{... | collective-permute-start | bytes 196616 | tf_op jit(solution)/shard_map/ppermute | solution.py:15
  42.5 8.7 %collective-permute-start.11 = (bf16[256,128]{1,0:T(8,128)(2,1)S(1)}, bf16[256,128]{1,0:T(8,128)(2,1)S(1)}, u32[]{:S(2)}, u32[]{:S(2)}) collective-permute-start(bf16[256,128]{1,0:T(8,128)(2,1)S(1)} %get-tuple-element.39), channel_id=1, source_target_pairs={{0,16},{4,20},{8,24},{12,28},{16,0},{20,4},{24,8},{28,12},{1,17},{... | collective-permute-start | bytes 196616 | tf_op jit(solution)/shard_map/ppermute | solution.py:15
  42.9 12.1 %collective-permute-start.12 = (bf16[256,128]{1,0:T(8,128)(2,1)S(1)}, bf16[256,128]{1,0:T(8,128)(2,1)S(1)}, u32[]{:S(2)}, u32[]{:S(2)}) collective-permute-start(bf16[256,128]{1,0:T(8,128)(2,1)S(1)} %get-tuple-element.40), channel_id=1, source_target_pairs={{0,20},{4,16},{8,28},{12,24},{16,4},{20,0},{24,12},{28,8},{1,21},{... | collective-permute-start | bytes 196616 | tf_op jit(solution)/shard_map/ppermute | solution.py:15
  46.4 8.6 %collective-permute-start.13 = (bf16[256,128]{1,0:T(8,128)(2,1)S(1)}, bf16[256,128]{1,0:T(8,128)(2,1)S(1)}, u32[]{:S(2)}, u32[]{:S(2)}) collective-permute-start(bf16[256,128]{1,0:T(8,128)(2,1)S(1)} %get-tuple-element.41), channel_id=1, source_target_pairs={{0,24},{4,28},{8,16},{12,20},{16,8},{20,12},{24,0},{28,4},{1,25},{... | collective-permute-start | bytes 196616 | tf_op jit(solution)/shard_map/ppermute | solution.py:15
  47.8 7.2 %collective-permute-start.14 = (bf16[256,128]{1,0:T(8,128)(2,1)S(1)}, bf16[256,128]{1,0:T(8,128)(2,1)S(1)}, u32[]{:S(2)}, u32[]{:S(2)}) collective-permute-start(bf16[256,128]{1,0:T(8,128)(2,1)S(1)} %get-tuple-element.42), channel_id=1, source_target_pairs={{0,28},{4,24},{8,20},{12,16},{16,12},{20,8},{24,4},{28,0},{1,29},{... | collective-permute-start | bytes 196616 | tf_op jit(solution)/shard_map/ppermute | solution.py:15

commit v6 on v5

--- a/solution.py
+++ b/solution.py
@@ -405,7 +405,8 @@
 
 
 def finish_body(meta, *refs, group):
-    parts, out_ref = refs[:-1], refs[-1]
+    parts, (out_ref, held, sems) = refs[:-3], refs[-3:]
+    copies = []
     sub = out_ref.shape[1] // group
     place, own = meta[1], meta[2]
     for m in range(group):
@@ -414,7 +415,13 @@
             other = parts[far * group + m][...].astype(f32)
             value = value + jnp.where((own ^ far) < own, other, 0.0)
         at = pl.multiple_of((place ^ m) * sub, sub)
-        out_ref[:, pl.ds(at, sub)] = value.astype(bf16)
+        held[m] = value.astype(bf16)
+        copies.append(
+            pltpu.make_async_copy(held.at[m], out_ref.at[:, pl.ds(at, sub)], sems.at[m])
+        )
+        copies[m].start()
+    for copy in copies:
+        copy.wait()
 
 
 def finish(parts, group):
@@ -423,7 +430,11 @@
     return pl.pallas_call(
         on_device(finish_body, group=group),
         in_specs=[pl.BlockSpec(memory_space=pltpu.VMEM)] * len(parts),
-        out_specs=pl.BlockSpec(memory_space=pltpu.VMEM),
+        out_specs=pl.BlockSpec(memory_space=pltpu.HBM),
+        scratch_shapes=[
+            pltpu.VMEM((group, width, sub), bf16),
+            pltpu.SemaphoreType.DMA((group,)),
+        ],
         out_shape=jax.ShapeDtypeStruct(shape, bf16),
         compiler_params=params(24, 0),
         name="finish",

time: 55.9 us -> 55.9 us (level)
  no operation moved by 1% of the time
where the time goes in v6:
time: 55.9 us; the launch traced here: 55.8 us
  starting transfers between devices  23.2 us (42%)
  waiting for transfers between devices  19.8 us (35%)
  Pallas kernels  12.6 us (23%)
    ppermute x15, starting transfers between devices, swap(): lax.ppermute(value, axis, [(i, i ^ mask) for i in range(lax.axis_size(axi...  23.2 us
    ppermute x15, waiting for transfers between devices, swap(): lax.ppermute(value, axis, [(i, i ^ mask) for i in range(lax.axis_size(axi...  19.8 us
    pallas_call x1, Pallas kernels, project_first(): pl.pallas_call(on_device(project_first_body, group=group, targets=targets...  4.13 us
    pallas_call x3, Pallas kernels, convolve_one(): pl.pallas_call(on_device(convolve_one_body, m=m, ahead=ahead, group=group...  2.82 us
    pallas_call x3, Pallas kernels, project(): pl.pallas_call(on_device(project_body, blocks=blocks, group=group, places...  2.25 us
    pallas_call x1, Pallas kernels, convolve_pair(): pl.pallas_call(on_device(convolve_pair_body, at=at, ahead=ahead, group=gr...  1.61 us
  transfers between devices with their start and end apart: 15, of which 4 were waited for; matrix products, arithmetic and copies ran while one was open for 0% of the time, Pallas kernels for 19%

profile of v6, /device:TPU:0, one launch (start us, length us, event | category | flops | bytes accessed | tf_op | source)
XLA Modules:
  0.0 55.8 jit_solution(14498217158029833976)
XLA Ops:
  0.0 0.0 copy-start
  0.0 3.0 %collective-permute-start.2 = (bf16[256,512]{1,0:T(8,128)(2,1)}, bf16[256,512]{1,0:T(8,128)(2,1)S(1)}, u32[]{:S(2)}, u32[]{:S(2)}) collective-permute-start(bf16[256,512]{1,0:T(8,128)(2,1)} %refs_0_.1), channel_id=1, source_target_pairs={{0,2},{1,3},{2,0},{3,1},{4,6},{5,7},{6,4},{7,5},{8,10},{9,11},{10,... | collective-permute-start | bytes 786440 | tf_op jit(solution)/shard_map/ppermute | solution.py:15
  3.0 0.0 collective-permute-start.4
  3.0 6.5 %collective-permute-done.2.refs_1_ = bf16[256,512]{1,0:T(8,128)(2,1)S(1)} collective-permute-done((bf16[256,512]{1,0:T(8,128)(2,1)}, bf16[256,512]{1,0:T(8,128)(2,1)S(1)}, u32[]{:S(2)}, u32[]{:S(2)}) %collective-permute-start.2) | collective-permute-done | bytes 262176 | tf_op jit(solution)/shard_map/ppermute | solution.py:15
  9.5 0.0 collective-permute-start.3
  9.5 2.8 %collective-permute-start = (f32[1,4,256]{2,1,0:T(4,128)}, f32[1,4,256]{2,1,0:T(4,128)S(1)}, u32[]{:S(2)}, u32[]{:S(2)}) collective-permute-start(f32[1,4,256]{2,1,0:T(4,128)} %bitcast.1), channel_id=1, source_target_pairs={{0,16},{4,20},{8,24},{12,28},{16,0},{20,4},{24,8},{28,12},{1,17},{... | collective-permute-start | bytes 12296 | tf_op jit(solution)/shard_map/ppermute | solution.py:15
  12.3 4.1 %project_first.1 = (f32[4,256,256]{2,1,0:T(8,128)S(1)}, f32[4,256,256]{2,1,0:T(8,128)S(1)}, bf16[3,4,512,512]{3,2,1,0:T(8,128)(2,1)S(1)}) custom-call(bf16[256,512]{1,0:T(8,128)(2,1)} %refs_0_.1, bf16[4,2048,512]{2,1,0:T(8,128)(2,1)} %refs_1_.1), custom_call_target="tpu_custom_call" | custom-call | flops 536870912 | bytes 8388608 | tf_op jit(solution)/shard_map/project_first/pallas_call | solution.py:77
  16.5 0.0 collective-permute-done
  16.5 0.0 copy-done
  16.5 0.0 collective-permute-done.4.refs_0_
  16.5 0.8 %shard_map.37.refs_2_ = f32[4,256,256]{2,1,0:T(8,128)S(1)} custom-call(bf16[256,512]{1,0:T(8,128)(2,1)S(1)} %collective-permute-done.4.refs_0_, bf16[256,512]{1,0:T(8,128)(2,1)S(1)} %collective-permute-done.2.refs_1_, bf16[3,4,512,512]{3,2,1,0:T(8,128)(2,1)S(1)} %get-tuple-element.24.refs_2_.refs_1_.refs_3_, f32[4,256,256]{2,1,0:T(8,128)S(1)} %get-tuple-element.25.refs_3_), custom_call_target="tpu_custom_call" | custom-call | flops 536870912 | bytes 2097152 | tf_op jit(solution)/shard_map/pallas_call | solution.py:140
  17.3 0.0 collective-permute-done.3.refs_0_.refs_2_
  17.3 0.5 shard_map.38
  17.8 1.5 %collective-permute-start.5 = (bf16[264,512]{1,0:T(8,128)(2,1)S(1)}, bf16[264,512]{1,0:T(8,128)(2,1)S(1)}, u32[]{:S(2)}, u32[]{:S(2)}) collective-permute-start(bf16[264,512]{1,0:T(8,128)(2,1)S(1)} %get-tuple-element.26), channel_id=1, source_target_pairs={{0,4},{4,0},{8,12},{12,8},{16,20},{20,16},{24,28},{28,24},{1,5},{5... | collective-permute-start | bytes 811016 | tf_op jit(solution)/shard_map/ppermute | solution.py:15
  19.3 1.6 %collective-permute-start.6 = (bf16[264,512]{1,0:T(8,128)(2,1)S(1)}, bf16[264,512]{1,0:T(8,128)(2,1)S(1)}, u32[]{:S(2)}, u32[]{:S(2)}) collective-permute-start(bf16[264,512]{1,0:T(8,128)(2,1)S(1)} %get-tuple-element.27), channel_id=1, source_target_pairs={{0,8},{4,12},{8,0},{12,4},{16,24},{20,28},{24,16},{28,20},{1,9},{5... | collective-permute-start | bytes 811016 | tf_op jit(solution)/shard_map/ppermute | solution.py:15
  20.9 1.0 %shard_map.39 = (bf16[256,512]{1,0:T(8,128)(2,1)S(1)}, bf16[256,512]{1,0:T(8,128)(2,1)S(1)}) custom-call(bf16[256,512]{1,0:T(8,128)(2,1)S(1)} %collective-permute-done.4.refs_0_, bf16[256,512]{1,0:T(8,128)(2,1)S(1)} %collective-permute-done.2.refs_1_, bf16[256,512]{1,0:T(8,128)(2,1)S(1)} %collective-permute-done.3.refs_0_.refs_2_, ...), custom_call_target="tpu_custom_call" | custom-call | flops 805306368 | bytes 3145728 | tf_op jit(solution)/shard_map/pallas_call | solution.py:140
  21.9 0.5 collective-permute-start.7
  22.4 2.5 %collective-permute-start.1 = (f32[2,4,256]{2,1,0:T(4,128)S(1)}, f32[2,4,256]{2,1,0:T(4,128)S(1)}, u32[]{:S(2)}, u32[]{:S(2)}) collective-permute-start(f32[2,4,256]{2,1,0:T(4,128)S(1)} %pad_maximum_fusion.refs_3_.refs_0_), channel_id=1, source_target_pairs={{0,12},{4,8},{8,4},{12,0},{16,28},{20,24},{24,20},{28,16},{1,13},{... | collective-permute-start | bytes 24584 | tf_op jit(solution)/shard_map/ppermute | solution.py:15
  24.9 8.5 %collective-permute-done.1.refs_1_ = f32[2,4,256]{2,1,0:T(4,128)S(1)} collective-permute-done((f32[2,4,256]{2,1,0:T(4,128)S(1)}, f32[2,4,256]{2,1,0:T(4,128)S(1)}, u32[]{:S(2)}, u32[]{:S(2)}) %collective-permute-start.1) | collective-permute-done | bytes 8224 | tf_op jit(solution)/shard_map/ppermute | solution.py:15
  33.4 0.0 collective-permute-done.5.refs_2_
  33.4 0.0 collective-permute-done.6.refs_3_.refs_1_
  33.4 1.1 %toeplitz.1.refs_0_ = bf16[3072,1024]{1,0:T(8,128)(2,1)S(1)} custom-call(f32[2,4,256]{2,1,0:T(4,128)S(1)} %pad_maximum_fusion.refs_3_.refs_0_, f32[2,4,256]{2,1,0:T(4,128)S(1)} %collective-permute-done.1.refs_1_, bf16[264,512]{1,0:T(8,128)(2,1)S(1)} %collective-permute-done.5.refs_2_, bf16[264,512]{1,0:T(8,128)(2,1)S(1)} %collective-permute-done.6.refs_3_.refs_1_), custom_call_target="tpu_custom_call" | custom-call | flops 16777216 | bytes 4194304 | tf_op jit(solution)/shard_map/toeplitz/pallas_call | solution.py:213
  34.5 1.6 %shard_map.40 = (f32[4,256,128]{2,1,0:T(8,128)S(1)}, f32[4,256,128]{2,1,0:T(8,128)S(1)}) custom-call(bf16[3072,1024]{1,0:T(8,128)(2,1)S(1)} %toeplitz.1.refs_0_, bf16[256,512]{1,0:T(8,128)(2,1)S(1)} %get-tuple-element.30.refs_1_, bf16[264,512]{1,0:T(8,128)(2,1)S(1)} %collective-permute-done.5.refs_2_), custom_call_target="tpu_custom_call" | custom-call | flops 1342177280 | bytes 524288 | tf_op jit(solution)/shard_map/pallas_call | solution.py:290
  36.1 1.3 %shard_map.41 = (f32[4,256,128]{2,1,0:T(8,128)S(1)}, f32[4,256,128]{2,1,0:T(8,128)S(1)}) custom-call(bf16[3072,1024]{1,0:T(8,128)(2,1)S(1)} %toeplitz.1.refs_0_, bf16[264,512]{1,0:T(8,128)(2,1)S(1)} %collective-permute-done.6.refs_3_.refs_1_, f32[4,256,128]{2,1,0:T(8,128)S(1)} %get-tuple-element.31.refs_2_, f32[4,256,128]{2,1,0:T(8,128)S(1)} %get-tuple-element.32.refs_3_), custom_call_target="tpu_custom_call" | custom-call | flops 536870912 | bytes 524288 | tf_op jit(solution)/shard_map/pallas_call | solution.py:334
  37.4 0.0 collective-permute-done.7.refs_1_
  37.4 0.8 %shard_map.42 = (bf16[256,128]{1,0:T(8,128)(2,1)S(1)}, bf16[256,128]{1,0:T(8,128)(2,1)S(1)}, bf16[256,128]{1,0:T(8,128)(2,1)S(1)}, bf16[256,128]{1,0:T(8,128)(2,1)S(1)}) custom-call(bf16[3072,1024]{1,0:T(8,128)(2,1)S(1)} %toeplitz.1.refs_0_, bf16[256,512]{1,0:T(8,128)(2,1)S(1)} %collective-permute-done.7.refs_1_, f32[4,256,128]{2,1,0:T(8,128)S(1)} %get-tuple-element.33.refs_2_), custom_call_target="tpu_custom_call" | custom-call | flops 268435456 | bytes 524288 | tf_op jit(solution)/shard_map/pallas_call | solution.py:334
  38.2 1.5 %collective-permute-start.8 = (bf16[256,128]{1,0:T(8,128)(2,1)S(1)}, bf16[256,128]{1,0:T(8,128)(2,1)S(1)}, u32[]{:S(2)}, u32[]{:S(2)}) collective-permute-start(bf16[256,128]{1,0:T(8,128)(2,1)S(1)} %get-tuple-element.35), channel_id=1, source_target_pairs={{0,4},{4,0},{8,12},{12,8},{16,20},{20,16},{24,28},{28,24},{1,5},{5... | collective-permute-start | bytes 196616 | tf_op jit(solution)/shard_map/ppermute | solution.py:15
  39.7 1.6 %collective-permute-start.9 = (bf16[256,128]{1,0:T(8,128)(2,1)S(1)}, bf16[256,128]{1,0:T(8,128)(2,1)S(1)}, u32[]{:S(2)}, u32[]{:S(2)}) collective-permute-start(bf16[256,128]{1,0:T(8,128)(2,1)S(1)} %get-tuple-element.36), channel_id=1, source_target_pairs={{0,8},{4,12},{8,0},{12,4},{16,24},{20,28},{24,16},{28,20},{1,9},{5... | collective-permute-start | bytes 196616 | tf_op jit(solution)/shard_map/ppermute | solution.py:15
  41.3 0.4 collective-permute-start.10
  41.8 0.8 %shard_map.43 = (bf16[256,128]{1,0:T(8,128)(2,1)S(1)}, bf16[256,128]{1,0:T(8,128)(2,1)S(1)}, bf16[256,128]{1,0:T(8,128)(2,1)S(1)}, bf16[256,128]{1,0:T(8,128)(2,1)S(1)}) custom-call(bf16[3072,1024]{1,0:T(8,128)(2,1)S(1)} %toeplitz.1.refs_0_, bf16[256,512]{1,0:T(8,128)(2,1)S(1)} %collective-permute-done.7.refs_1_, f32[4,256,128]{2,1,0:T(8,128)S(1)} %get-tuple-element.38.refs_2_), custom_call_target="tpu_custom_call" | custom-call | flops 268435456 | bytes 524288 | tf_op jit(solution)/shard_map/pallas_call | solution.py:334
  42.5 0.3 collective-permute-start.11
  42.9 3.6 %collective-permute-start.12 = (bf16[256,128]{1,0:T(8,128)(2,1)S(1)}, bf16[256,128]{1,0:T(8,128)(2,1)S(1)}, u32[]{:S(2)}, u32[]{:S(2)}) collective-permute-start(bf16[256,128]{1,0:T(8,128)(2,1)S(1)} %get-tuple-element.40), channel_id=1, source_target_pairs={{0,20},{4,16},{8,28},{12,24},{16,4},{20,0},{24,12},{28,8},{1,21},{... | collective-permute-start | bytes 196616 | tf_op jit(solution)/shard_map/ppermute | solution.py:15
  46.4 0.0 collective-permute-done.8.refs_1_
  46.4 1.4 %collective-permute-start.13 = (bf16[256,128]{1,0:T(8,128)(2,1)S(1)}, bf16[256,128]{1,0:T(8,128)(2,1)S(1)}, u32[]{:S(2)}, u32[]{:S(2)}) collective-permute-start(bf16[256,128]{1,0:T(8,128)(2,1)S(1)} %get-tuple-element.41), channel_id=1, source_target_pairs={{0,24},{4,28},{8,16},{12,20},{16,8},{20,12},{24,0},{28,4},{1,25},{... | collective-permute-start | bytes 196616 | tf_op jit(solution)/shard_map/ppermute | solution.py:15
  47.8 0.0 collective-permute-done.9.refs_2_
  47.8 2.4 %collective-permute-start.14 = (bf16[256,128]{1,0:T(8,128)(2,1)S(1)}, bf16[256,128]{1,0:T(8,128)(2,1)S(1)}, u32[]{:S(2)}, u32[]{:S(2)}) collective-permute-start(bf16[256,128]{1,0:T(8,128)(2,1)S(1)} %get-tuple-element.42), channel_id=1, source_target_pairs={{0,28},{4,24},{8,20},{12,16},{16,12},{20,8},{24,4},{28,0},{1,29},{... | collective-permute-start | bytes 196616 | tf_op jit(solution)/shard_map/ppermute | solution.py:15
  50.3 0.0 collective-permute-done.10.refs_3_
  50.3 1.0 %collective-permute-done.11.refs_4_ = bf16[256,128]{1,0:T(8,128)(2,1)S(1)} collective-permute-done((bf16[256,128]{1,0:T(8,128)(2,1)S(1)}, bf16[256,128]{1,0:T(8,128)(2,1)S(1)}, u32[]{:S(2)}, u32[]{:S(2)}) %collective-permute-start.11) | collective-permute-done | bytes 65568 | tf_op jit(solution)/shard_map/ppermute | solution.py:15
  51.3 3.7 %collective-permute-done.12.refs_5_ = bf16[256,128]{1,0:T(8,128)(2,1)S(1)} collective-permute-done((bf16[256,128]{1,0:T(8,128)(2,1)S(1)}, bf16[256,128]{1,0:T(8,128)(2,1)S(1)}, u32[]{:S(2)}, u32[]{:S(2)}) %collective-permute-start.12) | collective-permute-done | bytes 65568 | tf_op jit(solution)/shard_map/ppermute | solution.py:15
  55.0 0.0 collective-permute-done.13.refs_6_
  55.0 0.0 collective-permute-done.14.refs_7_
  55.0 0.8 %finish.1 = bf16[256,512]{1,0:T(8,128)(2,1)} custom-call(bf16[256,128]{1,0:T(8,128)(2,1)S(1)} %get-tuple-element.34.refs_0_, bf16[256,128]{1,0:T(8,128)(2,1)S(1)} %collective-permute-done.8.refs_1_, bf16[256,128]{1,0:T(8,128)(2,1)S(1)} %collective-permute-done.9.refs_2_, bf16[256,128]{1,0:T(8,128)(2,1)S(1)} %collective-permute-done.10.refs_3_, ...), custom_call_target="tpu_custom_call" | custom-call | tf_op jit(solution)/shard_map/finish/pallas_call | solution.py:430
  (1 shorter events, 0.0 us)
Async XLA Ops:
  0.0 16.5 %copy-start = (f32[4,256]{1,0:T(4,128)S(1)}, f32[4,256]{1,0:T(4,128)}, u32[]{:S(2)}) copy-start(f32[4,256]{1,0:T(4,128)} %param.5) | copy-start | bytes 12292
  0.0 9.5 %collective-permute-start.2 = (bf16[256,512]{1,0:T(8,128)(2,1)}, bf16[256,512]{1,0:T(8,128)(2,1)S(1)}, u32[]{:S(2)}, u32[]{:S(2)}) collective-permute-start(bf16[256,512]{1,0:T(8,128)(2,1)} %refs_0_.1), channel_id=1, source_target_pairs={{0,2},{1,3},{2,0},{3,1},{4,6},{5,7},{6,4},{7,5},{8,10},{9,11},{10,... | collective-permute-start | bytes 786440 | tf_op jit(solution)/shard_map/ppermute | solution.py:15
  3.0 13.5 %collective-permute-start.4 = (bf16[256,512]{1,0:T(8,128)(2,1)}, bf16[256,512]{1,0:T(8,128)(2,1)S(1)}, u32[]{:S(2)}, u32[]{:S(2)}) collective-permute-start(bf16[256,512]{1,0:T(8,128)(2,1)} %refs_0_.1), channel_id=1, source_target_pairs={{0,1},{1,0},{2,3},{3,2},{4,5},{5,4},{6,7},{7,6},{8,9},{9,8},{10,11... | collective-permute-start | bytes 786440 | tf_op jit(solution)/shard_map/ppermute | solution.py:15
  9.5 7.8 %collective-permute-start.3 = (bf16[256,512]{1,0:T(8,128)(2,1)S(1)}, bf16[256,512]{1,0:T(8,128)(2,1)S(1)}, u32[]{:S(2)}, u32[]{:S(2)}) collective-permute-start(bf16[256,512]{1,0:T(8,128)(2,1)S(1)} %collective-permute-done.2.refs_1_), channel_id=1, source_target_pairs={{0,1},{1,0},{2,3},{3,2},{4,5},{5,4},{6,7},{7,6},{8,9},{9,8},{10,11... | collective-permute-start | bytes 786440 | tf_op jit(solution)/shard_map/ppermute | solution.py:15
  9.5 7.0 %collective-permute-start = (f32[1,4,256]{2,1,0:T(4,128)}, f32[1,4,256]{2,1,0:T(4,128)S(1)}, u32[]{:S(2)}, u32[]{:S(2)}) collective-permute-start(f32[1,4,256]{2,1,0:T(4,128)} %bitcast.1), channel_id=1, source_target_pairs={{0,16},{4,20},{8,24},{12,28},{16,0},{20,4},{24,8},{28,12},{1,17},{... | collective-permute-start | bytes 12296 | tf_op jit(solution)/shard_map/ppermute | solution.py:15
  17.8 15.7 %collective-permute-start.5 = (bf16[264,512]{1,0:T(8,128)(2,1)S(1)}, bf16[264,512]{1,0:T(8,128)(2,1)S(1)}, u32[]{:S(2)}, u32[]{:S(2)}) collective-permute-start(bf16[264,512]{1,0:T(8,128)(2,1)S(1)} %get-tuple-element.26), channel_id=1, source_target_pairs={{0,4},{4,0},{8,12},{12,8},{16,20},{20,16},{24,28},{28,24},{1,5},{5... | collective-permute-start | bytes 811016 | tf_op jit(solution)/shard_map/ppermute | solution.py:15
  19.3 14.1 %collective-permute-start.6 = (bf16[264,512]{1,0:T(8,128)(2,1)S(1)}, bf16[264,512]{1,0:T(8,128)(2,1)S(1)}, u32[]{:S(2)}, u32[]{:S(2)}) collective-permute-start(bf16[264,512]{1,0:T(8,128)(2,1)S(1)} %get-tuple-element.27), channel_id=1, source_target_pairs={{0,8},{4,12},{8,0},{12,4},{16,24},{20,28},{24,16},{28,20},{1,9},{5... | collective-permute-start | bytes 811016 | tf_op jit(solution)/shard_map/ppermute | solution.py:15
  21.9 15.5 %collective-permute-start.7 = (bf16[256,512]{1,0:T(8,128)(2,1)S(1)}, bf16[256,512]{1,0:T(8,128)(2,1)S(1)}, u32[]{:S(2)}, u32[]{:S(2)}) collective-permute-start(bf16[256,512]{1,0:T(8,128)(2,1)S(1)} %get-tuple-element.29), channel_id=1, source_target_pairs={{0,12},{4,8},{8,4},{12,0},{16,28},{20,24},{24,20},{28,16},{1,13},{... | collective-permute-start | bytes 786440 | tf_op jit(solution)/shard_map/ppermute | solution.py:15
  22.4 11.0 %collective-permute-start.1 = (f32[2,4,256]{2,1,0:T(4,128)S(1)}, f32[2,4,256]{2,1,0:T(4,128)S(1)}, u32[]{:S(2)}, u32[]{:S(2)}) collective-permute-start(f32[2,4,256]{2,1,0:T(4,128)S(1)} %pad_maximum_fusion.refs_3_.refs_0_), channel_id=1, source_target_pairs={{0,12},{4,8},{8,4},{12,0},{16,28},{20,24},{24,20},{28,16},{1,13},{... | collective-permute-start | bytes 24584 | tf_op jit(solution)/shard_map/ppermute | solution.py:15
  38.2 8.2 %collective-permute-start.8 = (bf16[256,128]{1,0:T(8,128)(2,1)S(1)}, bf16[256,128]{1,0:T(8,128)(2,1)S(1)}, u32[]{:S(2)}, u32[]{:S(2)}) collective-permute-start(bf16[256,128]{1,0:T(8,128)(2,1)S(1)} %get-tuple-element.35), channel_id=1, source_target_pairs={{0,4},{4,0},{8,12},{12,8},{16,20},{20,16},{24,28},{28,24},{1,5},{5... | collective-permute-start | bytes 196616 | tf_op jit(solution)/shard_map/ppermute | solution.py:15
  39.7 8.1 %collective-permute-start.9 = (bf16[256,128]{1,0:T(8,128)(2,1)S(1)}, bf16[256,128]{1,0:T(8,128)(2,1)S(1)}, u32[]{:S(2)}, u32[]{:S(2)}) collective-permute-start(bf16[256,128]{1,0:T(8,128)(2,1)S(1)} %get-tuple-element.36), channel_id=1, source_target_pairs={{0,8},{4,12},{8,0},{12,4},{16,24},{20,28},{24,16},{28,20},{1,9},{5... | collective-permute-start | bytes 196616 | tf_op jit(solution)/shard_map/ppermute | solution.py:15
  41.3 8.9 %collective-permute-start.10 = (bf16[256,128]{1,0:T(8,128)(2,1)S(1)}, bf16[256,128]{1,0:T(8,128)(2,1)S(1)}, u32[]{:S(2)}, u32[]{:S(2)}) collective-permute-start(bf16[256,128]{1,0:T(8,128)(2,1)S(1)} %get-tuple-element.37), channel_id=1, source_target_pairs={{0,12},{4,8},{8,4},{12,0},{16,28},{20,24},{24,20},{28,16},{1,13},{... | collective-permute-start | bytes 196616 | tf_op jit(solution)/shard_map/ppermute | solution.py:15
  42.5 8.7 %collective-permute-start.11 = (bf16[256,128]{1,0:T(8,128)(2,1)S(1)}, bf16[256,128]{1,0:T(8,128)(2,1)S(1)}, u32[]{:S(2)}, u32[]{:S(2)}) collective-permute-start(bf16[256,128]{1,0:T(8,128)(2,1)S(1)} %get-tuple-element.39), channel_id=1, source_target_pairs={{0,16},{4,20},{8,24},{12,28},{16,0},{20,4},{24,8},{28,12},{1,17},{... | collective-permute-start | bytes 196616 | tf_op jit(solution)/shard_map/ppermute | solution.py:15
  42.9 12.1 %collective-permute-start.12 = (bf16[256,128]{1,0:T(8,128)(2,1)S(1)}, bf16[256,128]{1,0:T(8,128)(2,1)S(1)}, u32[]{:S(2)}, u32[]{:S(2)}) collective-permute-start(bf16[256,128]{1,0:T(8,128)(2,1)S(1)} %get-tuple-element.40), channel_id=1, source_target_pairs={{0,20},{4,16},{8,28},{12,24},{16,4},{20,0},{24,12},{28,8},{1,21},{... | collective-permute-start | bytes 196616 | tf_op jit(solution)/shard_map/ppermute | solution.py:15
  46.4 8.6 %collective-permute-start.13 = (bf16[256,128]{1,0:T(8,128)(2,1)S(1)}, bf16[256,128]{1,0:T(8,128)(2,1)S(1)}, u32[]{:S(2)}, u32[]{:S(2)}) collective-permute-start(bf16[256,128]{1,0:T(8,128)(2,1)S(1)} %get-tuple-element.41), channel_id=1, source_target_pairs={{0,24},{4,28},{8,16},{12,20},{16,8},{20,12},{24,0},{28,4},{1,25},{... | collective-permute-start | bytes 196616 | tf_op jit(solution)/shard_map/ppermute | solution.py:15
  47.8 7.2 %collective-permute-start.14 = (bf16[256,128]{1,0:T(8,128)(2,1)S(1)}, bf16[256,128]{1,0:T(8,128)(2,1)S(1)}, u32[]{:S(2)}, u32[]{:S(2)}) collective-permute-start(bf16[256,128]{1,0:T(8,128)(2,1)S(1)} %get-tuple-element.42), channel_id=1, source_target_pairs={{0,28},{4,24},{8,20},{12,16},{16,12},{20,8},{24,4},{28,0},{1,29},{... | collective-permute-start | bytes 196616 | tf_op jit(solution)/shard_map/ppermute | solution.py:15
